TPU v7x, 32 devices: a whole 2x2x4 slice. The times are simulated.
32 devices in a mesh: member: 4 (over y, x), lon: 8 (over z, core).
Axes of the slice: x: 2, y: 2, z: 4, core: 2. Of those that a mesh axis runs over, the one named last changes fastest.
Arguments:
- fields: bfloat16 [4, 641, 20, 360], P('member', None, None, 'lon'), may hold values from -6 to 6
- weight: bfloat16 [5, 5, 73, 641], replicated, may hold values from -0.046875 to 0.046875
- out_bias: float32 [73], replicated, may hold values from -3 to 3
- observed: float32 [73, 16, 360], P(None, None, 'lon'), may hold values from -6 to 6
- widths: float32 [73], replicated, may hold values from 0.5 to 2
- owner_start: int32 [8, 5], P('lon'), may hold values from 0 to 16, as said below
Outputs:
- out_grad: bfloat16 [4, 73, 16, 360], P('member', None, None, 'lon')
- owned_score: float32 [8, 4, 540], P('lon', 'member')
- weight_grad: float32 [5, 5, 73, 641], replicated
- bias_grad: float32 [73], replicated
Inputs may be any that keep to these rules, and one draw needn't show every extreme that they name: Each row owner_start[l] starts at 0, never falls and ends at 16; owner r of longitude group l holds blocks owner_start[l, r] to owner_start[l, r + 1] - 1, at most 12 of them, and in every group some owner holds exactly 12.
All inputs are finite; a program needn't handle non-finite values.
Results may differ from a plain program's by a relative error of at most 0.0063.
Values may be sent and summed in bfloat16 or wider, within the bound.
No kernel may reach another device: no remote copies, remote signals or barrier semaphores. Data moves between devices by JAX's collectives and lax.ppermute only.
A program may use at most 128 MiB of HBM per device.

v0:
```python
import functools
import math
import types

import jax
import jax.numpy as jnp
from jax import lax
from jax.experimental import pallas as pl
from jax.experimental.pallas import tpu as pltpu
from jax.sharding import PartitionSpec as P


BLOCK = 45
LANES = 128
ROWS = 8
SPECIAL = 16


NT = (((1,), (1,)), ((), ()))
NN = (((1,), (0,)), ((), ()))


def round_up(value, unit):
    return -(-value // unit) * unit


def vmem():
    return pl.BlockSpec(memory_space=pltpu.VMEM)


def smem():
    return pl.BlockSpec(memory_space=pltpu.SMEM)


def limit(mib):
    return pltpu.CompilerParams(vmem_limit_bytes=mib << 20)


def here():
    lon = lax.axis_index("lon")
    return lax.axis_index("member"), lax.div(lon, 2), lax.rem(lon, 2)


def cost(flops, moved, special=0):
    return pl.CostEstimate(flops=flops, bytes_accessed=moved, transcendentals=special)


def column_of(row_ref, fill):
    count = row_ref.shape[1]
    row = jnp.concatenate(
        [row_ref[...], jnp.full((1, LANES - count), fill, jnp.float32)], axis=1
    )
    return jnp.transpose(jnp.broadcast_to(row, (LANES, LANES)))[:, :1]


def pack_kernel(plan, f_ref, near_ref, far_ref, *out_refs):
    members, main, rest = plan.members, plan.main, plan.rest
    pack, valid, sub = plan.pack, plan.valid, plan.sub
    rows_in, lon_dev, in_chan = f_ref.shape
    place_ref = here()
    halo = 2 * plan.half
    even = place_ref[2] == 0
    start_edge = f_ref[:, :halo, :].astype(jnp.float32)
    final = (lon_dev - halo) // ROWS * ROWS
    end_edge = f_ref[:, final:, :].astype(jnp.float32)[:, lon_dev - halo - final :]
    far_ref[...] = jnp.where(even, start_edge, end_edge).astype(far_ref.dtype)
    near_ref[...] = jnp.where(even, end_edge, start_edge).astype(near_ref.dtype)
    group = rows_in // pack
    base = main * members
    lane = lax.broadcasted_iota(jnp.int32, (1, 1, LANES), 2)
    full = (base + rest) * LANES
    slab = jnp.zeros((1, lon_dev, LANES), jnp.float32)
    for e in range(in_chan - full):
        for r in range(rows_in):
            value = f_ref[r : r + 1, :, full + e : full + e + 1].astype(jnp.float32)
            slab = jnp.where(lane == e * rows_in + r, value, slab)
    for d in range(members):
        owner = place_ref[0] ^ d
        out = out_refs[d]
        for k in range(main):
            spot = pl.ds(pl.multiple_of((k * members + owner) * LANES, LANES), LANES)
            out[k * rows_in : (k + 1) * rows_in] = f_ref[:, :, spot]
        for i in range(group):
            row = None
            for g in range(pack):
                for k in range(rest):
                    tile = f_ref[
                        g * group + i, :, (base + k) * LANES : (base + k + 1) * LANES
                    ].astype(jnp.float32)
                    start = g * valid + k * sub
                    moved = pltpu.roll(tile, lax.rem(start - owner * sub + LANES, LANES), 1)
                    row = moved if row is None else jnp.where(lane[0] >= start, moved, row)
            out[main * rows_in + i] = row.astype(out.dtype)
        out[main * rows_in + group] = slab[0].astype(out.dtype)


def forward_kernel(
    plan, field_ref, near_ref, far_ref, weight_ref, b_ref, o_ref,
    f_s, raw_s, x_s, w_s, acc_s, sems,
):
    taps, half, offset = plan.taps, plan.half, plan.offset
    lon_dev, halo = plan.lon_dev, 2 * plan.half
    rows_in, slots, wide = x_s.shape
    out_chan, in_chan = plan.out_chan, near_ref.shape[2]
    padded_out = w_s.shape[1]
    rows_out = rows_in - taps + 1
    points = rows_out * slots
    bulk = lon_dev // ROWS * ROWS
    full = in_chan // LANES * LANES
    field_copies = []
    for part in range(2):
        span = pl.ds(part * (rows_in // 2), rows_in // 2)
        copy = pltpu.make_async_copy(field_ref.at[span], f_s.at[span], sems.at[taps + part])
        copy.start()
        field_copies.append(copy)
    weight_copies = []
    for a in range(taps):
        span = pl.ds(a * taps, taps)
        copy = pltpu.make_async_copy(weight_ref.at[span], raw_s.at[span], sems.at[a])
        weight_copies.append(copy)
    weight_copies[0].start()
    x_s[:, :, full:] = jnp.zeros((rows_in, slots, wide - full), x_s.dtype)
    w_s[:, :, full:] = jnp.zeros((taps * taps, padded_out, wide - full), w_s.dtype)
    for copy in field_copies:
        copy.wait()
    for copy in weight_copies[1:]:
        copy.start()
    x_s[:, offset : offset + bulk, :in_chan] = f_s[:, :bulk, :]
    near = near_ref[...].astype(jnp.float32)
    far = far_ref[...].astype(jnp.float32)
    even = here()[2] == 0
    first = jnp.concatenate(
        [
            jnp.zeros((rows_in, offset - halo, in_chan), jnp.float32),
            jnp.where(even, far, near),
        ],
        axis=1,
    )
    x_s[:, :offset, :in_chan] = first.astype(x_s.dtype)
    tail = slots - offset - bulk
    final = jnp.concatenate(
        [
            f_s[:, bulk:, :].astype(jnp.float32),
            jnp.where(even, near, far),
            jnp.zeros((rows_in, tail - (lon_dev - bulk) - halo, in_chan), jnp.float32),
        ],
        axis=1,
    )
    x_s[:, offset + bulk :, :in_chan] = final.astype(x_s.dtype)
    for a in range(taps):
        weight_copies[a].wait()
        mine = slice(a * taps, (a + 1) * taps)
        w_s[mine, :out_chan, :in_chan] = raw_s[mine]
        part = lax.dot_general(
            w_s[a * taps : (a + 1) * taps].reshape(taps * padded_out, wide),
            x_s[a : a + rows_out].reshape(points, wide),
            NT,
            preferred_element_type=jnp.float32,
        )
        if a == 0:
            acc_s[...] = part
        else:
            acc_s[...] += part
    slot = lax.broadcasted_iota(jnp.int32, (1, points), 1) % slots
    inside = (slot >= offset - half) & (slot < offset + lon_dev + half)
    bias = column_of(b_ref, 0.0)
    for lo in range(0, padded_out, 2 * ROWS):
        rows = slice(lo, lo + 2 * ROWS)
        total = jnp.zeros((2 * ROWS, points), jnp.float32) + bias[rows]
        for b in range(taps):
            piece = acc_s[b * padded_out + lo : b * padded_out + lo + 2 * ROWS, :]
            shift = (half - b) % points
            total = total + (pltpu.roll(piece, shift, 1) if shift else piece)
        row = lo + lax.broadcasted_iota(jnp.int32, (2 * ROWS, 1), 0)
        keep = inside & (row < out_chan)
        o_ref[rows, :] = jnp.where(keep, total, 0.0).astype(o_ref.dtype)


def prep_kernel(plan, obs_ref, near_ref, far_ref, *refs):
    truth_ref, row_s = refs[-2:]
    refs = refs[:-2]
    half, offset, padded_out = plan.half, plan.offset, plan.padded_out
    even = here()[2] == 0
    near, far = near_ref[...], far_ref[...]
    out_chan = obs_ref.shape[2]
    total_rows = obs_ref.shape[1]
    width = plan.points // total_rows
    per = LANES // width
    row_s[...] = jnp.zeros(row_s.shape, jnp.float32)
    for x in range(half):
        row_s[:, offset - half + x, :out_chan] = jnp.where(even, far[x], near[x])
        row_s[:, offset + plan.lon_dev + x, :out_chan] = jnp.where(even, near[x], far[x])
    for x in range(plan.lon_dev):
        row_s[:, offset + x, :out_chan] = obs_ref[x]
    for j in range(total_rows // per):
        tile = row_s[j * per : (j + 1) * per].reshape(LANES, LANES)
        truth_ref[:, j * LANES : (j + 1) * LANES] = jnp.transpose(tile)[:padded_out]
    members, main = plan.members, plan.main
    pack, valid, extras = plan.pack, plan.valid, plan.extras
    out_ref = refs[-1]
    _, rows_in, slots, _ = out_ref.shape
    lon_dev = plan.lon_dev
    bulk = lon_dev // ROWS * ROWS
    group = rows_in // pack
    lane = lax.broadcasted_iota(jnp.int32, (1, LANES), 1)
    out_ref[:, :, bulk:, :] = jnp.zeros(
        (members, rows_in, slots - bulk, out_ref.shape[3]), out_ref.dtype
    )
    for d in range(members):
        ref = refs[d]
        for k in range(main):
            out_ref[d, :, :lon_dev, k * LANES : (k + 1) * LANES] = ref[
                k * rows_in : (k + 1) * rows_in
            ]
        slab = ref[main * rows_in + group].astype(jnp.float32)
        for g in range(pack):
            for i in range(group):
                value = ref[main * rows_in + i].astype(jnp.float32)
                if g:
                    value = pltpu.roll(value, LANES - g * valid, 1)
                r = g * group + i
                for e in range(extras):
                    shift = (valid + e - (e * rows_in + r)) % LANES
                    moved = pltpu.roll(slab, shift, 1) if shift else slab
                    value = jnp.where(lane == valid + e, moved, value)
                value = jnp.where(lane == valid + extras, 1.0, value)
                out_ref[d, r, :lon_dev, main * LANES :] = value.astype(out_ref.dtype)


def split_bias(tile, row_high):
    row = lax.broadcasted_iota(jnp.int32, tile.shape, 0)
    size = tile.shape[0]
    total = jnp.where(row == row_high, tile + pltpu.roll(tile, size - 1, 0), tile)
    left = total - total.astype(jnp.bfloat16).astype(jnp.float32)
    return jnp.where(row == row_high + 1, pltpu.roll(left, 1, 0), total)


def fix_rows(plan, ref, index, piece, value_of):
    @pl.when(piece == 2 * plan.pairs - 1)
    def _():
        lo = plan.special_row
        tile = value_of(lo, lo + SPECIAL)
        ref[index, lo : lo + SPECIAL, :] = split_bias(tile, plan.bias_row).astype(ref.dtype)


def gradient_kernel(plan, *refs):
    members, taps, half = plan.members, plan.taps, plan.half
    out_chan, padded_out, points = plan.out_chan, plan.padded_out, plan.points
    main, pairs, pack, valid = plan.main, plan.pairs, plan.pack, plan.valid
    rows_out, size, extras = plan.rows_out, plan.half_rows, plan.extras
    per_half, special = plan.per_half, plan.special
    place_ref = here()
    y_refs = refs[:members]
    x_ref, obs_ref, wid_ref = refs[members : 3 + members]
    g_ref, score_ref, send_ref, keep_ref = refs[3 + members : 7 + members]
    g_s, gs_s, wide_s, packed_s = refs[7 + members :]
    step = 2 * LANES
    width_all = column_of(wid_ref, 1.0)
    for left in range(0, points, step):
        tally = jnp.zeros((ROWS, step), jnp.float32)
        for lo in range(0, padded_out, 2 * ROWS):
            rows = slice(lo, lo + 2 * ROWS)
            cols = slice(left, left + step)
            shape = (2 * ROWS, step)
            width = width_all[rows]
            inverse = 1.0 / (width * width)
            values = [y[rows, cols].astype(jnp.float32) for y in y_refs]
            target = obs_ref[rows, cols]
            pair_sum = jnp.full(shape, float(members), jnp.float32)
            pull = [jnp.zeros(shape, jnp.float32) for _ in values]
            for x in range(members):
                for y in range(x + 1, members):
                    spread = values[x] - values[y]
                    kernel_pair = jnp.exp(-0.5 * spread * spread * inverse)
                    pair_sum = pair_sum + 2.0 * kernel_pair
                    weighted = kernel_pair * spread
                    pull[x] = pull[x] + weighted
                    pull[y] = pull[y] - weighted
            obs_sum = jnp.zeros(shape, jnp.float32)
            for x in range(members):
                misfit = values[x] - target
                kernel_obs = jnp.exp(-0.5 * misfit * misfit * inverse)
                obs_sum = obs_sum + kernel_obs
                grad = inverse * (misfit * kernel_obs - pull[x] / members)
                g_s[x, rows, cols] = grad.astype(jnp.bfloat16)
            terms = pair_sum / (2.0 * members * members) - obs_sum / members
            row = lo + lax.broadcasted_iota(jnp.int32, (2 * ROWS, 1), 0)
            terms = jnp.where(row < out_chan, terms, 0.0)
            tally = tally + terms[:ROWS] + terms[ROWS:]
        score_ref[:, left : left + step] = jnp.sum(tally, axis=0, keepdims=True) / out_chan
    g_ref[...] = g_s[0]
    for x in range(members):
        for lo in range(0, padded_out, 2 * ROWS):
            grad = g_s[x, lo : lo + 2 * ROWS, :].astype(jnp.float32)
            for b in range(taps):
                shift = (b - half - plan.offset) % points
                moved = pltpu.roll(grad, shift, 1) if shift else grad
                start = b * padded_out + lo
                gs_s[x, start : start + 2 * ROWS, :] = moved.astype(jnp.bfloat16)
    tiles = main + 1
    split = size - special - SPECIAL
    for h in range(2):
        wide_s[:, h * size + special : (h + 1) * size, :] = jnp.zeros(
            (tiles, size - special, LANES), jnp.float32
        )
    for a in range(taps):
        total = None
        for x in range(members):
            part = lax.dot_general(
                gs_s[x],
                x_ref[x, a : a + rows_out].reshape(points, tiles * LANES),
                NN,
                preferred_element_type=jnp.float32,
            )
            total = part if total is None else total + part
        for b in range(taps):
            tap = a * taps + b
            block = total[b * padded_out : (b + 1) * padded_out]
            across = jnp.transpose(block[:, main * LANES :])
            if tap < 2 * per_half:
                h, i = tap // per_half, tap % per_half
                spans = [(0, padded_out, h * size + i * padded_out)]
                line = h * size + special + i * extras
            else:
                first = size - split
                spans = [(0, split, first), (split, padded_out, size + first)]
                line = size + special + per_half * extras
            for k in range(tiles):
                for lo, hi, at in spans:
                    wide_s[k, at : at + hi - lo, :] = block[lo:hi, k * LANES : (k + 1) * LANES]
            for e in range(extras):
                wide_s[0, line + e : line + e + 1, :padded_out] = across[valid + e : valid + e + 1]
            if a == 0 and b == half:
                line = size + special + plan.bias_row
                ones = valid + extras
                wide_s[0, line : line + 1, :padded_out] = across[ones : ones + 1]
    short = size // pack
    lane = lax.broadcasted_iota(jnp.int32, (1, LANES), 1)
    for h in range(2):
        packed = wide_s[main, h * size : h * size + short, :]
        for g in range(1, pack):
            at = h * size + g * short
            moved = pltpu.roll(wide_s[main, at : at + short, :], g * valid, 1)
            packed = jnp.where(lane >= g * valid, moved, packed)
        packed_s[h * short : (h + 1) * short, :] = packed
    pair, core = place_ref[1], place_ref[2]
    main_rows = size // pairs
    rest_rows = main_rows // pack
    for s in range(pairs):
        for out, side in ((keep_ref, core), (send_ref, 1 - core)):
            piece = 2 * (pair ^ s) + side
            at = 0
            for k in range(main):
                source = pl.ds(pl.multiple_of(piece * main_rows, main_rows), main_rows)
                out[s, at : at + main_rows, :] = wide_s[k, source, :].astype(out.dtype)
                at += main_rows
            source = pl.ds(pl.multiple_of(piece * rest_rows, rest_rows), rest_rows)
            out[s, at : at + rest_rows, :] = packed_s[source, :].astype(out.dtype)
        spot = 2 * size - main_rows
        fix_rows(
            plan, send_ref, s, 2 * (pair ^ s) + 1 - core,
            lambda lo, hi: wide_s[0, spot + lo : spot + hi, :]
            if main
            else packed_s[spot + lo : spot + hi, :],
        )


def core_add_kernel(plan, keep_ref, got_ref, mine_ref, *out_refs):
    place_ref = here()
    mine_ref[...] = keep_ref[0] + got_ref[0].astype(jnp.float32)
    pair, core = place_ref[1], place_ref[2]
    for s in range(1, plan.pairs):
        out = out_refs[s - 1]
        out[0] = (keep_ref[s] + got_ref[s].astype(jnp.float32)).astype(out.dtype)
        fix_rows(
            plan, out, 0, 2 * (pair ^ s) + core,
            lambda lo, hi: keep_ref[s, lo:hi, :] + got_ref[s, lo:hi, :].astype(jnp.float32),
        )


def pair_add_kernel(plan, factor, mine_ref, *refs):
    place_ref = here()
    out = refs[-1]

    def value(lo, hi):
        total = mine_ref[lo:hi, :]
        for ref in refs[:-1]:
            total = total + ref[0, lo:hi, :].astype(jnp.float32)
        return total * factor

    out[0] = value(0, mine_ref.shape[0]).astype(out.dtype)
    fix_rows(plan, out, 0, 2 * place_ref[1] + place_ref[2], value)


def out_grad_kernel(plan, g_ref, out_ref, row_s):
    lon_dev, offset = plan.lon_dev, plan.offset
    rows_out, out_chan = out_ref.shape[1:]
    width = plan.points // rows_out
    per = LANES // width
    padded_out = g_ref.shape[0]
    for j in range(rows_out // per):
        tile = g_ref[:, j * LANES : (j + 1) * LANES].astype(jnp.float32)
        tile = jnp.concatenate(
            [tile, jnp.zeros((LANES - padded_out, LANES), jnp.float32)], axis=0
        )
        row_s[j * per : (j + 1) * per] = jnp.transpose(tile).reshape(per, width, LANES)
    for x in range(lon_dev):
        out_ref[x] = row_s[:, offset + x, :out_chan].astype(out_ref.dtype)


def owned_kernel(plan, start_ref, score_ref, out_ref, row_s):
    lon_dev, offset, points = plan.lon_dev, plan.offset, plan.points
    rows_out = plan.rows_out
    width = points // rows_out
    capacity = out_ref.shape[1] // lon_dev
    member = here()[0]
    first = start_ref[0, member]
    count = start_ref[0, member + 1] - first
    lane = lax.broadcasted_iota(jnp.int32, (1, points), 1)
    row_s[...] = jnp.zeros(row_s.shape, jnp.float32)
    score = score_ref[...]
    for i in range(rows_out):
        moved = pltpu.roll(score, (points - i * width - offset) % points, 1)
        row_s[i : i + 1, :] = jnp.where(lane < lon_dev, moved, 0.0)[:, :LANES]
    reach = round_up(capacity * lon_dev, LANES)
    total = jnp.zeros((1, reach), jnp.float32)
    blank = jnp.zeros((1, reach - LANES), jnp.float32)
    for t in range(capacity):
        row = jnp.where(t < count, row_s[pl.ds(first + t, 1), :], 0.0)
        row = jnp.concatenate([row, blank], axis=1)
        total = total + (pltpu.roll(row, t * lon_dev, 1) if t else row)
    out_ref[...] = total[:, : capacity * lon_dev]


def assemble_kernel(plan, second, layout, final, *refs):
    members, main, rest = plan.members, plan.main, plan.rest
    out_chan, padded_out, pairs = plan.out_chan, plan.padded_out, plan.pairs
    pack, valid, sub = plan.pack, plan.valid, plan.sub
    size, extras, per_half = plan.half_rows, plan.extras, plan.per_half
    special = plan.special
    member, pair, core = here()
    piece_refs = refs[: len(layout)]
    refs = refs[len(layout) :]
    own_half = lax.div(pair, pairs // 2)
    this_half = 1 - own_half if second else own_half
    low = this_half == 0
    main_rows = size // pairs
    rest_rows = main_rows // pack
    split = size - special - SPECIAL
    begin = special + SPECIAL
    known_ref = carry_ref = None
    if second:
        carry_ref, _, *refs = refs
        if final == "late":
            known_ref, *refs = refs
    out_ref, other_ref, main_s, packed_s, main_stage, rest_stage, sems = refs
    if known_ref is not None:
        packed_s[...] = known_ref[:members]
    shown = []
    for d, _, _ in layout:
        if d not in shown:
            shown.append(d)
    for ref, (d, s, other) in zip(piece_refs, layout):
        side = 1 - core if other else core
        piece = lax.rem(2 * (pair ^ s) + side, pairs)
        row = 0
        for k in range(main):
            spot = pl.ds(pl.multiple_of(piece * main_rows, ROWS), main_rows)
            main_s[shown.index(d) * main + k, spot, :] = ref[0, row : row + main_rows, :].astype(
                jnp.float32
            )
            row += main_rows
        spot = pl.ds(pl.multiple_of(piece * rest_rows, ROWS), rest_rows)
        packed_s[member ^ d, spot, :] = ref[0, row : row + rest_rows, :].astype(jnp.float32)
    lines = packed_s[0, special:begin, :] if not main else None
    for at, d in enumerate(shown if main else ()):
        found = main_s[at * main, special:begin, :]
        if lines is None:
            lines = found if known_ref is None else known_ref[members, :SPECIAL, :]
        lines = jnp.where(member == d, found, lines)
    copies = []

    def emit(source, stage, lanes):
        spans = [(pl.ds(0, per_half), pl.ds(this_half * per_half, per_half))]
        if second:
            spans.append((pl.ds(per_half, 1), pl.ds(2 * per_half, 1)))
        for from_span, to_span in spans:
            copy = pltpu.make_async_copy(
                source.at[stage, from_span],
                out_ref.at[to_span, :, lanes],
                sems.at[len(copies)],
            )
            copy.start()
            copies.append(copy)

    def fill(stage_ref, stage, lanes, tile, block):
        for i in range(per_half):
            stage_ref[stage, i, :, lanes] = tile[i * padded_out : i * padded_out + out_chan]
        mine = tile[begin:size]
        if second:
            theirs = carry_ref[block, SPECIAL:, :]
            stage_ref[stage, per_half, :split, lanes] = jnp.where(low, mine, theirs)
            stage_ref[stage, per_half, split:, lanes] = jnp.where(low, theirs, mine)[
                : out_chan - split
            ]
        else:
            other_ref[block, SPECIAL:, :] = mine

    if not second:
        other_ref[:, :SPECIAL, :] = jnp.zeros(
            (other_ref.shape[0], SPECIAL, LANES), jnp.float32
        )
        other_ref[0, :SPECIAL, :] = lines
    for at, d in enumerate(shown if main else ()):
        for k in range(main):
            block = k * members + (member ^ d)
            fill(main_stage, at * main + k, slice(None), main_s[at * main + k], block)
            emit(
                main_stage,
                at * main + k,
                pl.ds(pl.multiple_of(block * LANES, LANES), LANES),
            )
    if final == "early":
        other_ref[:members] = packed_s[...]
        other_ref[members] = jnp.zeros(other_ref.shape[1:], jnp.float32)
        other_ref[members, :SPECIAL, :] = lines
    else:
        lane = lax.broadcasted_iota(jnp.int32, (1, LANES), 1)
        base = main * members
        for k in range(rest):
            tiles = []
            for g in range(pack):
                tile = None
                for owner in range(members):
                    shift = (owner * sub - g * valid - k * sub) % LANES
                    value = packed_s[owner]
                    if shift:
                        value = pltpu.roll(value, shift, 1)
                    tile = (
                        value if tile is None else jnp.where(lane >= owner * sub, value, tile)
                    )
                tiles.append(tile)
            tile = tiles[0] if pack == 1 else jnp.concatenate(tiles, axis=0)
            fill(rest_stage, 0, slice(k * LANES, (k + 1) * LANES), tile, base + k)
        blank = jnp.zeros((LANES - SPECIAL, LANES), jnp.float32)

        def put_columns(rows, first, count, tap):
            columns = jnp.transpose(jnp.concatenate([rows, blank], axis=0))
            for i in range(count):
                for e in range(extras):
                    at = first + i * extras + e
                    lanes = slice(rest * LANES + e, rest * LANES + e + 1)
                    rest_stage[0, tap + i, :, lanes] = columns[:out_chan, at : at + 1]

        put_columns(lines, 0, per_half, 0)
        if second:
            top = jnp.where(low, carry_ref[0, :SPECIAL, :], lines)
            put_columns(top, per_half * extras, 1, per_half)
            line = plan.bias_row
            other_ref[...] = (top[line : line + 1] + top[line + 1 : line + 2])[:, :out_chan]
        emit(rest_stage, 0, pl.ds(base * LANES, rest * LANES + extras))
    for copy in copies:
        copy.wait()


def body(fields, weight, out_bias, observed, widths, owner_start):
    _, in_chan, rows_in, lon_dev = fields.shape
    taps, _, out_chan, _ = weight.shape
    half = taps // 2
    halo = 2 * half
    members = lax.axis_size("member")
    lon_count = lax.axis_size("lon")
    pairs = lon_count // 2
    rows_out = rows_in - taps + 1
    offset = round_up(halo, ROWS)
    slots = round_up(offset + lon_dev + halo, 2 * ROWS)
    points = rows_out * slots
    padded_out = round_up(out_chan, 2 * ROWS)
    full_blocks = in_chan // LANES
    main, rest = full_blocks // members, full_blocks % members
    sub = LANES // members
    valid = rest * sub
    pack = LANES // valid if rows_in % (LANES // valid) == 0 else 1
    extras = in_chan - full_blocks * LANES
    stack = taps * padded_out
    total_taps = taps * taps
    per_half = total_taps // 2
    special = per_half * padded_out
    half_rows = round_up(
        special + SPECIAL + round_up(-(-out_chan // 2), ROWS), ROWS * pack * pairs
    )
    bias_row = (per_half + 1) * extras
    assert rest and total_taps % 2 and bias_row + 2 <= SPECIAL
    wide = round_up(in_chan, LANES)
    plan = types.SimpleNamespace(
        members=members, taps=taps, half=half, offset=offset, lon_dev=lon_dev, out_chan=out_chan,
        padded_out=padded_out, rows_out=rows_out, points=points, main=main, rest=rest, pairs=pairs,
        pack=pack, valid=valid, sub=sub, extras=extras, half_rows=half_rows, per_half=per_half,
        special=special, bias_row=bias_row,
        special_row=special - (pairs - 1) * (half_rows // pairs),
    )
    own_lon = lax.axis_index("lon")
    factor = 1.0 / math.sqrt(members * rows_out * lon_dev * lon_count)
    even = own_lon % 2 == 0

    def swap_lon(value, d):
        return lax.ppermute(value, "lon", [(i, i ^ d) for i in range(lon_count)])

    def swap_far(value):
        step = [(i, (i + 1 if i % 2 else i - 1) % lon_count) for i in range(lon_count)]
        return lax.ppermute(value, "lon", step)

    def swap_member(value, d):
        return lax.ppermute(value, "member", [(i, i ^ d) for i in range(members)])

    any_space = pl.BlockSpec(memory_space=pl.ANY)
    field = jnp.transpose(fields[0], (1, 2, 0))
    packed_rows = main * rows_in + rows_in // pack + 1
    edge = jax.ShapeDtypeStruct((rows_in, halo, in_chan), jnp.bfloat16)
    near, far, *packed = pl.pallas_call(
        functools.partial(pack_kernel, plan),
        out_shape=[edge, edge]
        + [jax.ShapeDtypeStruct((packed_rows, lon_dev, LANES), jnp.bfloat16)] * members,
        in_specs=[vmem()],
        out_specs=[vmem()] * (members + 2),
        cost_estimate=cost(0, 4_000_000),
        compiler_params=limit(16),
        name="pack",
    )(field)
    far = swap_far(far)
    near = swap_lon(near, 1)
    traded = [packed[0]]
    for d in range(1, members):
        traded.append(swap_member(packed[d], d))

    own_outputs = pl.pallas_call(
        functools.partial(forward_kernel, plan),
        out_shape=jax.ShapeDtypeStruct((padded_out, points), jnp.bfloat16),
        in_specs=[any_space, vmem(), vmem(), any_space, vmem()],
        out_specs=vmem(),
        scratch_shapes=[
            pltpu.VMEM((rows_in, lon_dev, in_chan), jnp.bfloat16),
            pltpu.VMEM((total_taps, out_chan, in_chan), jnp.bfloat16),
            pltpu.VMEM((rows_in, slots, wide), jnp.bfloat16),
            pltpu.VMEM((total_taps, padded_out, wide), jnp.bfloat16),
            pltpu.VMEM((stack, points), jnp.float32),
            pltpu.SemaphoreType.DMA((taps + 2,)),
        ],
        cost_estimate=cost(2 * taps * stack * points * wide, 6_000_000),
        compiler_params=limit(56),
        name="forward",
    )(field, near, far, weight.reshape(total_taps, out_chan, in_chan), out_bias[None, :])
    outputs = [own_outputs]
    for d in range(1, members):
        outputs.append(swap_member(own_outputs, d))

    seen = jnp.transpose(observed, (2, 1, 0))
    start_edge = seen[:half]
    end_edge = seen[lon_dev - half :]
    strips = (jnp.where(even, start_edge, end_edge), jnp.where(even, end_edge, start_edge))
    strips, _ = lax.optimization_barrier((strips, own_outputs))
    far = swap_far(strips[0])
    near = swap_lon(strips[1], 1)
    tiles = main + 1
    x_all, truth = pl.pallas_call(
        functools.partial(prep_kernel, plan),
        out_shape=(
            jax.ShapeDtypeStruct((members, rows_in, slots, tiles * LANES), jnp.bfloat16),
            jax.ShapeDtypeStruct((padded_out, points), jnp.float32),
        ),
        in_specs=[vmem()] * (members + 3),
        out_specs=[vmem()] * 2,
        scratch_shapes=[pltpu.VMEM((rows_out, slots, LANES), jnp.float32)],
        cost_estimate=cost(0, 4_000_000),
        compiler_params=limit(20),
        name="prep",
    )(seen, near, far, *traded)

    main_rows = half_rows // pairs
    piece_rows = main * main_rows + main_rows // pack
    piece = jax.ShapeDtypeStruct((1, piece_rows, LANES), jnp.bfloat16)
    grad_own, score, send, keep = pl.pallas_call(
        functools.partial(gradient_kernel, plan),
        out_shape=(
            jax.ShapeDtypeStruct((padded_out, points), jnp.bfloat16),
            jax.ShapeDtypeStruct((1, points), jnp.float32),
            jax.ShapeDtypeStruct((pairs, piece_rows, LANES), jnp.bfloat16),
            jax.ShapeDtypeStruct((pairs, piece_rows, LANES), jnp.float32),
        ),
        in_specs=[vmem()] * (members + 3),
        out_specs=[vmem()] * 4,
        scratch_shapes=[
            pltpu.VMEM((members, padded_out, points), jnp.bfloat16),
            pltpu.VMEM((members, stack, points), jnp.bfloat16),
            pltpu.VMEM((tiles, 2 * half_rows, LANES), jnp.float32),
            pltpu.VMEM((2 * half_rows // pack, LANES), jnp.float32),
        ],
        cost_estimate=cost(
            2 * taps * stack * points * members * tiles * LANES, 6_000_000, 1_000_000
        ),
        compiler_params=limit(32),
        name="gradient",
    )(*outputs, x_all, truth, widths[None, :])

    mine, *out_pieces = pl.pallas_call(
        functools.partial(core_add_kernel, plan),
        out_shape=[jax.ShapeDtypeStruct((piece_rows, LANES), jnp.float32)] + [piece] * (pairs - 1),
        in_specs=[vmem(), vmem()],
        out_specs=[vmem()] * pairs,
        cost_estimate=cost(0, 1_500_000),
        compiler_params=limit(16),
        name="core_add",
    )(keep, swap_lon(send, 1))
    got = []
    for at, value in enumerate(out_pieces, 1):
        got.append(swap_lon(value, 2 * at))
    final = pl.pallas_call(
        functools.partial(pair_add_kernel, plan, factor),
        out_shape=piece,
        in_specs=[vmem()] * pairs,
        out_specs=vmem(),
        cost_estimate=cost(0, 600_000),
        compiler_params=limit(16),
        name="pair_add",
    )(mine, *got)

    gathered = [final]
    for at in range(1, pairs):
        gathered.append(swap_lon(final, 2 * at))
    grad_shape = jax.ShapeDtypeStruct((total_taps, out_chan, in_chan), jnp.float32)
    blocks = full_blocks
    tail_rows = half_rows - special
    halves = []
    for second in range(2):
        group = range(second * pairs // 2, (second + 1) * pairs // 2)
        column = jnp.concatenate([gathered[s] for s in group])
        held = []
        for d in range(members):
            value = column
            if d:
                value = swap_member(column, d)
            held.append((d, (value, swap_lon(value, 1))))
        halves.append((group, held))
    rest_lanes = rest * LANES + extras
    short = half_rows // pack

    def assemble(second, final, held, extra_inputs, other_shape):
        group = halves[second][0]
        arrays, layout = [], []
        for d, both in held:
            for other, value in enumerate(both):
                arrays.append(value)
                layout += [(d, s, bool(other)) for s in group]
        count, each = len(arrays), len(group)
        stages = max(len(held) * main, 1)
        taps_held = per_half + second

        def kernel(*refs):
            pieces = [ref.at[pl.ds(at, 1)] for ref in refs[:count] for at in range(each)]
            assemble_kernel(plan, second, tuple(layout), final, *pieces, *refs[count:])

        specs = [vmem()] * count
        if second:
            specs += [vmem(), any_space] + [vmem()] * (len(extra_inputs) - 2)
        return pl.pallas_call(
            kernel,
            out_shape=[grad_shape, jax.ShapeDtypeStruct(other_shape, jnp.float32)],
            in_specs=specs,
            out_specs=[any_space, vmem()],
            scratch_shapes=[
                pltpu.VMEM((stages, half_rows, LANES), jnp.float32),
                pltpu.VMEM((members, short, LANES), jnp.float32),
                pltpu.VMEM((stages, taps_held, out_chan, LANES), jnp.float32),
                pltpu.VMEM((1, taps_held, out_chan, rest_lanes), jnp.float32),
                pltpu.SemaphoreType.DMA((2 * stages + 2,)),
            ],
            input_output_aliases={count + 1: 0} if second else {},
            cost_estimate=cost(0, 5_000_000),
            compiler_params=limit(24),
            name="assemble",
        )(*arrays, *extra_inputs)

    weight_grad, carry = assemble(0, "all", halves[0][1], (), (blocks, tail_rows, LANES))
    held = halves[1][1]
    if main:
        weight_grad, known = assemble(
            1, "early", held[:-1], (carry, weight_grad), (members + 1, short, LANES)
        )
        weight_grad, bias_out = assemble(
            1, "late", held[-1:], (carry, weight_grad, known), (1, out_chan)
        )
    else:
        weight_grad, bias_out = assemble(1, "all", held, (carry, weight_grad), (1, out_chan))
    bias_grad = bias_out[0]
    weight_grad = weight_grad.reshape(taps, taps, out_chan, in_chan)

    assert BLOCK == lon_dev
    out_grad = pl.pallas_call(
        functools.partial(out_grad_kernel, plan),
        out_shape=jax.ShapeDtypeStruct((lon_dev, rows_out, out_chan), jnp.bfloat16),
        in_specs=[vmem()],
        out_specs=vmem(),
        scratch_shapes=[pltpu.VMEM((rows_out, slots, LANES), jnp.float32)],
        cost_estimate=cost(0, 400_000),
        compiler_params=limit(8),
        name="out_grad",
    )(grad_own)
    out_grad = jnp.transpose(out_grad, (2, 1, 0))[None]
    capacity = max(2, 3 * rows_out // members)
    owned_score = pl.pallas_call(
        functools.partial(owned_kernel, plan),
        out_shape=jax.ShapeDtypeStruct((1, capacity * lon_dev), jnp.float32),
        in_specs=[smem(), vmem()],
        out_specs=vmem(),
        scratch_shapes=[pltpu.VMEM((round_up(rows_out + capacity, ROWS), LANES), jnp.float32)],
        cost_estimate=cost(0, 100_000),
        compiler_params=limit(8),
        name="owned",
    )(owner_start, score)
    owned_score = owned_score[None]
    return (out_grad, owned_score, weight_grad, bias_grad)


def solution(mesh):
    in_specs = (P("member", None, None, "lon"), P(), P(), P(None, None, "lon"), P(), P("lon", None))
    out_specs = (P("member", None, None, "lon"), P("lon", "member", None), P(), P())
    return jax.shard_map(body, mesh=mesh, in_specs=in_specs, out_specs=out_specs, check_vma=False)
```

profile of v0, /device:TPU:0, one launch (start us, length us, event | category | flops | bytes accessed | tf_op | source)
XLA Modules:
  0.0 84.4 jit_solution(13953398591902461325)
XLA Ops:
  3.3 4.7 %collective-permute-start.1 = (bf16[20,4,641]{2,1,0:T(4,128)(2,1)S(1)}, bf16[20,4,641]{2,1,0:T(4,128)(2,1)S(1)}, u32[]{:S(2)}, u32[]{:S(2)}) collective-permute-start(bf16[20,4,641]{2,1,0:T(4,128)(2,1)S(1)} %get-tuple-element.29), channel_id=1, source_target_pairs={{0,7},{1,2},{2,1},{3,4},{4,3},{5,6},{6,5},{7,0},{8,15},{9,10},{10,... | collective-permute-start | bytes 307688 | tf_op jit(solution)/shard_map/ppermute | solution.py:611
  8.0 1.5 %collective-permute-start.7 = (bf16[26,45,128]{2,1,0:T(8,128)(2,1)S(1)}, bf16[26,45,128]{2,1,0:T(8,128)(2,1)S(1)}, u32[]{:S(2)}, u32[]{:S(2)}) collective-permute-start(bf16[26,45,128]{2,1,0:T(8,128)(2,1)S(1)} %get-tuple-element.33), channel_id=1, source_target_pairs={{0,8},{8,0},{16,24},{24,16},{1,9},{9,1},{17,25},{25,17},{2,10},{10... | collective-permute-start | bytes 898568 | tf_op jit(solution)/shard_map/ppermute | solution.py:614
  9.5 1.5 %collective-permute-start.8 = (bf16[26,45,128]{2,1,0:T(8,128)(2,1)S(1)}, bf16[26,45,128]{2,1,0:T(8,128)(2,1)S(1)}, u32[]{:S(2)}, u32[]{:S(2)}) collective-permute-start(bf16[26,45,128]{2,1,0:T(8,128)(2,1)S(1)} %get-tuple-element.34), channel_id=1, source_target_pairs={{0,16},{8,24},{16,0},{24,8},{1,17},{9,25},{17,1},{25,9},{2,18},{10... | collective-permute-start | bytes 898568 | tf_op jit(solution)/shard_map/ppermute | solution.py:614
  12.9 7.3 %forward.1.refs_0_ = bf16[80,1024]{1,0:T(8,128)(2,1)} custom-call(bf16[20,45,641]{2,1,0:T(8,128)(2,1)} %bitcast.13, bf16[20,4,641]{2,1,0:T(4,128)(2,1)} %copy-done.5, bf16[20,4,641]{2,1,0:T(4,128)(2,1)} %copy-done.6, bf16[25,73,641]{2,1,0:T(8,128)(2,1)} %bitcast.21, f32[1,73]{1,0:T(1,128)} %bitcast.22), custom_call_target="tpu_custom_call" | custom-call | flops 3145728000 | bytes 6000000 | tf_op jit(solution)/shard_map/forward/pallas_call | solution.py:636
  20.3 1.9 %collective-permute-start.6 = (f32[2,16,73]{2,1,0:T(8,128)S(1)}, f32[2,16,73]{2,1,0:T(8,128)S(1)}, u32[]{:S(2)}, u32[]{:S(2)}) collective-permute-start(f32[2,16,73]{2,1,0:T(8,128)S(1)} %get-tuple-element.31), channel_id=1, source_target_pairs={{0,7},{1,2},{2,1},{3,4},{4,3},{5,6},{6,5},{7,0},{8,15},{9,10},{10,... | collective-permute-start | bytes 28040 | tf_op jit(solution)/shard_map/ppermute | solution.py:611
  22.2 1.5 %collective-permute-start.2 = (bf16[80,1024]{1,0:T(8,128)(2,1)}, bf16[80,1024]{1,0:T(8,128)(2,1)S(1)}, u32[]{:S(2)}, u32[]{:S(2)}) collective-permute-start(bf16[80,1024]{1,0:T(8,128)(2,1)} %forward.1.refs_0_), channel_id=1, source_target_pairs={{0,8},{8,0},{16,24},{24,16},{1,9},{9,1},{17,25},{25,17},{2,10},{10... | collective-permute-start | bytes 491528 | tf_op jit(solution)/shard_map/ppermute | solution.py:614
  23.7 1.6 %collective-permute-done.6.far_ref = f32[2,16,73]{2,1,0:T(8,128)S(1)} collective-permute-done((f32[2,16,73]{2,1,0:T(8,128)S(1)}, f32[2,16,73]{2,1,0:T(8,128)S(1)}, u32[]{:S(2)}, u32[]{:S(2)}) %collective-permute-start.6) | collective-permute-done | bytes 9376 | tf_op jit(solution)/shard_map/ppermute | solution.py:611
  25.3 1.5 %collective-permute-start.3 = (bf16[80,1024]{1,0:T(8,128)(2,1)}, bf16[80,1024]{1,0:T(8,128)(2,1)S(1)}, u32[]{:S(2)}, u32[]{:S(2)}) collective-permute-start(bf16[80,1024]{1,0:T(8,128)(2,1)} %forward.1.refs_0_), channel_id=1, source_target_pairs={{0,16},{8,24},{16,0},{24,8},{1,17},{9,25},{17,1},{25,9},{2,18},{10... | collective-permute-start | bytes 491528 | tf_op jit(solution)/shard_map/ppermute | solution.py:614
  26.9 1.4 %collective-permute-start.4 = (bf16[80,1024]{1,0:T(8,128)(2,1)}, bf16[80,1024]{1,0:T(8,128)(2,1)S(1)}, u32[]{:S(2)}, u32[]{:S(2)}) collective-permute-start(bf16[80,1024]{1,0:T(8,128)(2,1)} %forward.1.refs_0_), channel_id=1, source_target_pairs={{0,24},{8,16},{16,8},{24,0},{1,25},{9,17},{17,9},{25,1},{2,26},{10... | collective-permute-start | bytes 491528 | tf_op jit(solution)/shard_map/ppermute | solution.py:614
  29.4 4.8 %collective-permute-done.3.refs_2_ = bf16[80,1024]{1,0:T(8,128)(2,1)S(1)} collective-permute-done((bf16[80,1024]{1,0:T(8,128)(2,1)}, bf16[80,1024]{1,0:T(8,128)(2,1)S(1)}, u32[]{:S(2)}, u32[]{:S(2)}) %collective-permute-start.3) | collective-permute-done | bytes 163872 | tf_op jit(solution)/shard_map/ppermute | solution.py:614
  35.1 6.3 %gradient.1 = (bf16[80,1024]{1,0:T(8,128)(2,1)S(1)}, f32[1,1024]{1,0:T(1,128)S(1)}, bf16[4,320,128]{2,1,0:T(8,128)(2,1)S(1)}, f32[4,320,128]{2,1,0:T(8,128)S(1)}) custom-call(bf16[80,1024]{1,0:T(8,128)(2,1)S(1)} %copy-done.3, bf16[80,1024]{1,0:T(8,128)(2,1)S(1)} %collective-permute-done.2.refs_1_, bf16[80,1024]{1,0:T(8,128)(2,1)S(1)} %collective-permute-done.3.refs_2_, ...), custom_call_target="tpu_custom_call" | custom-call | flops 4194304000 | bytes 6000000 | tf_op jit(solution)/shard_map/gradient/pallas_call | solution.py:682
  41.5 1.6 %collective-permute-done.10.got_ref = bf16[4,320,128]{2,1,0:T(8,128)(2,1)S(1)} collective-permute-done((bf16[4,320,128]{2,1,0:T(8,128)(2,1)S(1)}, bf16[4,320,128]{2,1,0:T(8,128)(2,1)S(1)}, u32[]{:S(2)}, u32[]{:S(2)}) %collective-permute-start.10) | collective-permute-done | bytes 327712 | tf_op jit(solution)/shard_map/ppermute | solution.py:607
  43.3 2.3 %collective-permute-start.12 = (bf16[1,320,128]{2,1,0:T(8,128)(2,1)S(1)}, bf16[1,320,128]{2,1,0:T(8,128)(2,1)S(1)}, u32[]{:S(2)}, u32[]{:S(2)}) collective-permute-start(bf16[1,320,128]{2,1,0:T(8,128)(2,1)S(1)} %get-tuple-element.44), channel_id=1, source_target_pairs={{0,4},{1,5},{2,6},{3,7},{4,0},{5,1},{6,2},{7,3},{8,12},{9,13},{10,... | collective-permute-start | bytes 245768 | tf_op jit(solution)/shard_map/ppermute | solution.py:607
  45.6 2.1 %collective-permute-start.13 = (bf16[1,320,128]{2,1,0:T(8,128)(2,1)S(1)}, bf16[1,320,128]{2,1,0:T(8,128)(2,1)S(1)}, u32[]{:S(2)}, u32[]{:S(2)}) collective-permute-start(bf16[1,320,128]{2,1,0:T(8,128)(2,1)S(1)} %get-tuple-element.45), channel_id=1, source_target_pairs={{0,6},{1,7},{2,4},{3,5},{4,2},{5,3},{6,0},{7,1},{8,14},{9,15},{10,... | collective-permute-start | bytes 245768 | tf_op jit(solution)/shard_map/ppermute | solution.py:607
  48.8 4.3 %collective-permute-done.12.refs_1_ = bf16[1,320,128]{2,1,0:T(8,128)(2,1)S(1)} collective-permute-done((bf16[1,320,128]{2,1,0:T(8,128)(2,1)S(1)}, bf16[1,320,128]{2,1,0:T(8,128)(2,1)S(1)}, u32[]{:S(2)}, u32[]{:S(2)}) %collective-permute-start.12) | collective-permute-done | bytes 81952 | tf_op jit(solution)/shard_map/ppermute | solution.py:607
  53.3 1.6 %collective-permute-start.18 = (bf16[1,320,128]{2,1,0:T(8,128)(2,1)S(1)}, bf16[1,320,128]{2,1,0:T(8,128)(2,1)S(1)}, u32[]{:S(2)}, u32[]{:S(2)}) collective-permute-start(bf16[1,320,128]{2,1,0:T(8,128)(2,1)S(1)} %pair_add.1), channel_id=1, source_target_pairs={{0,2},{1,3},{2,0},{3,1},{4,6},{5,7},{6,4},{7,5},{8,10},{9,11},{10,... | collective-permute-start | bytes 245768 | tf_op jit(solution)/shard_map/ppermute | solution.py:607
  55.7 2.0 %collective-permute-start.15 = (bf16[1,320,128]{2,1,0:T(8,128)(2,1)S(1)}, bf16[1,320,128]{2,1,0:T(8,128)(2,1)S(1)}, u32[]{:S(2)}, u32[]{:S(2)}) collective-permute-start(bf16[1,320,128]{2,1,0:T(8,128)(2,1)S(1)} %pair_add.1), channel_id=1, source_target_pairs={{0,6},{1,7},{2,4},{3,5},{4,2},{5,3},{6,0},{7,1},{8,14},{9,15},{10,... | collective-permute-start | bytes 245768 | tf_op jit(solution)/shard_map/ppermute | solution.py:607
  58.4 1.6 %collective-permute-start.20 = (bf16[2,320,128]{2,1,0:T(8,128)(2,1)S(1)}, bf16[2,320,128]{2,1,0:T(8,128)(2,1)S(1)}, u32[]{:S(2)}, u32[]{:S(2)}) collective-permute-start(bf16[2,320,128]{2,1,0:T(8,128)(2,1)S(1)} %pad_maximum_fusion.refs_0_), channel_id=1, source_target_pairs={{0,8},{8,0},{16,24},{24,16},{1,9},{9,1},{17,25},{25,17},{2,10},{10... | collective-permute-start | bytes 491528 | tf_op jit(solution)/shard_map/ppermute | solution.py:614
  62.0 1.5 %collective-permute-done.14 = bf16[1,320,128]{2,1,0:T(8,128)(2,1)S(1)} collective-permute-done((bf16[1,320,128]{2,1,0:T(8,128)(2,1)S(1)}, bf16[1,320,128]{2,1,0:T(8,128)(2,1)S(1)}, u32[]{:S(2)}, u32[]{:S(2)}) %collective-permute-start.14) | collective-permute-done | bytes 81952 | tf_op jit(solution)/shard_map/ppermute | solution.py:607
  63.6 1.6 %collective-permute-start.27 = (bf16[2,320,128]{2,1,0:T(8,128)(2,1)S(1)}, bf16[2,320,128]{2,1,0:T(8,128)(2,1)S(1)}, u32[]{:S(2)}, u32[]{:S(2)}) collective-permute-start(bf16[2,320,128]{2,1,0:T(8,128)(2,1)S(1)} %constant_dynamic-update-slice_fusion.refs_0_), channel_id=1, source_target_pairs={{0,8},{8,0},{16,24},{24,16},{1,9},{9,1},{17,25},{25,17},{2,10},{10... | collective-permute-start | bytes 491528 | tf_op jit(solution)/shard_map/ppermute | solution.py:614
  68.4 2.3 %collective-permute-done.27.refs_2_ = bf16[2,320,128]{2,1,0:T(8,128)(2,1)S(1)} collective-permute-done((bf16[2,320,128]{2,1,0:T(8,128)(2,1)S(1)}, bf16[2,320,128]{2,1,0:T(8,128)(2,1)S(1)}, u32[]{:S(2)}, u32[]{:S(2)}) %collective-permute-start.27) | collective-permute-done | bytes 163872 | tf_op jit(solution)/shard_map/ppermute | solution.py:614
  70.7 4.3 %collective-permute-done.29.refs_4_ = bf16[2,320,128]{2,1,0:T(8,128)(2,1)S(1)} collective-permute-done((bf16[2,320,128]{2,1,0:T(8,128)(2,1)S(1)}, bf16[2,320,128]{2,1,0:T(8,128)(2,1)S(1)}, u32[]{:S(2)}, u32[]{:S(2)}) %collective-permute-start.29) | collective-permute-done | bytes 163872 | tf_op jit(solution)/shard_map/ppermute | solution.py:614
  78.5 2.0 %assemble.3 = (f32[25,73,641]{2,1,0:T(8,128)}, f32[5,64,128]{2,1,0:T(8,128)S(1)}) custom-call(bf16[2,320,128]{2,1,0:T(8,128)(2,1)S(1)} %pad_maximum_fusion.refs_0_, bf16[2,320,128]{2,1,0:T(8,128)(2,1)S(1)} %collective-permute-done.19.refs_1_, bf16[2,320,128]{2,1,0:T(8,128)(2,1)S(1)} %collective-permute-done.20.refs_2_, ...), custom_call_target="tpu_custom_call" | custom-call | bytes 5000000 | tf_op jit(solution)/shard_map/assemble/pallas_call | solution.py:765
  81.9 2.3 %assemble.5 = (f32[25,73,641]{2,1,0:T(8,128)}, f32[1,73]{1,0:T(1,128)}) custom-call(bf16[2,320,128]{2,1,0:T(8,128)(2,1)S(1)} %collective-permute-done.16.refs_0_, bf16[2,320,128]{2,1,0:T(8,128)(2,1)S(1)} %collective-permute-done.17.refs_1_, f32[5,64,128]{2,1,0:T(8,128)S(1)} %get-tuple-element.46.refs_6_.refs_2_, ...), custom_call_target="tpu_custom_call", output_to_operand_aliasing={{0}: (3, {})} | custom-call | bytes 5000000 | tf_op jit(solution)/shard_map/assemble/pallas_call | solution.py:765
  (67 shorter events, 19.9 us)
Async XLA Ops:
  2.8 9.5 %collective-permute-start = (bf16[20,4,641]{2,1,0:T(4,128)(2,1)S(1)}, bf16[20,4,641]{2,1,0:T(4,128)(2,1)S(1)}, u32[]{:S(2)}, u32[]{:S(2)}) collective-permute-start(bf16[20,4,641]{2,1,0:T(4,128)(2,1)S(1)} %get-tuple-element.28), channel_id=1, source_target_pairs={{0,1},{1,0},{2,3},{3,2},{4,5},{5,4},{6,7},{7,6},{8,9},{9,8},{10,11... | collective-permute-start | bytes 307688 | tf_op jit(solution)/shard_map/ppermute | solution.py:607
  3.3 8.9 %collective-permute-start.1 = (bf16[20,4,641]{2,1,0:T(4,128)(2,1)S(1)}, bf16[20,4,641]{2,1,0:T(4,128)(2,1)S(1)}, u32[]{:S(2)}, u32[]{:S(2)}) collective-permute-start(bf16[20,4,641]{2,1,0:T(4,128)(2,1)S(1)} %get-tuple-element.29), channel_id=1, source_target_pairs={{0,7},{1,2},{2,1},{3,4},{4,3},{5,6},{6,5},{7,0},{8,15},{9,10},{10,... | collective-permute-start | bytes 307688 | tf_op jit(solution)/shard_map/ppermute | solution.py:611
  8.0 18.8 %collective-permute-start.7 = (bf16[26,45,128]{2,1,0:T(8,128)(2,1)S(1)}, bf16[26,45,128]{2,1,0:T(8,128)(2,1)S(1)}, u32[]{:S(2)}, u32[]{:S(2)}) collective-permute-start(bf16[26,45,128]{2,1,0:T(8,128)(2,1)S(1)} %get-tuple-element.33), channel_id=1, source_target_pairs={{0,8},{8,0},{16,24},{24,16},{1,9},{9,1},{17,25},{25,17},{2,10},{10... | collective-permute-start | bytes 898568 | tf_op jit(solution)/shard_map/ppermute | solution.py:614
  9.5 18.8 %collective-permute-start.8 = (bf16[26,45,128]{2,1,0:T(8,128)(2,1)S(1)}, bf16[26,45,128]{2,1,0:T(8,128)(2,1)S(1)}, u32[]{:S(2)}, u32[]{:S(2)}) collective-permute-start(bf16[26,45,128]{2,1,0:T(8,128)(2,1)S(1)} %get-tuple-element.34), channel_id=1, source_target_pairs={{0,16},{8,24},{16,0},{24,8},{1,17},{9,25},{17,1},{25,9},{2,18},{10... | collective-permute-start | bytes 898568 | tf_op jit(solution)/shard_map/ppermute | solution.py:614
  11.0 17.3 %collective-permute-start.9 = (bf16[26,45,128]{2,1,0:T(8,128)(2,1)S(1)}, bf16[26,45,128]{2,1,0:T(8,128)(2,1)S(1)}, u32[]{:S(2)}, u32[]{:S(2)}) collective-permute-start(bf16[26,45,128]{2,1,0:T(8,128)(2,1)S(1)} %get-tuple-element.35), channel_id=1, source_target_pairs={{0,24},{8,16},{16,8},{24,0},{1,25},{9,17},{17,9},{25,1},{2,26},{10... | collective-permute-start | bytes 898568 | tf_op jit(solution)/shard_map/ppermute | solution.py:614
  22.2 7.1 %collective-permute-start.2 = (bf16[80,1024]{1,0:T(8,128)(2,1)}, bf16[80,1024]{1,0:T(8,128)(2,1)S(1)}, u32[]{:S(2)}, u32[]{:S(2)}) collective-permute-start(bf16[80,1024]{1,0:T(8,128)(2,1)} %forward.1.refs_0_), channel_id=1, source_target_pairs={{0,8},{8,0},{16,24},{24,16},{1,9},{9,1},{17,25},{25,17},{2,10},{10... | collective-permute-start | bytes 491528 | tf_op jit(solution)/shard_map/ppermute | solution.py:614
  25.3 8.8 %collective-permute-start.3 = (bf16[80,1024]{1,0:T(8,128)(2,1)}, bf16[80,1024]{1,0:T(8,128)(2,1)S(1)}, u32[]{:S(2)}, u32[]{:S(2)}) collective-permute-start(bf16[80,1024]{1,0:T(8,128)(2,1)} %forward.1.refs_0_), channel_id=1, source_target_pairs={{0,16},{8,24},{16,0},{24,8},{1,17},{9,25},{17,1},{25,9},{2,18},{10... | collective-permute-start | bytes 491528 | tf_op jit(solution)/shard_map/ppermute | solution.py:614
  26.9 7.3 %collective-permute-start.4 = (bf16[80,1024]{1,0:T(8,128)(2,1)}, bf16[80,1024]{1,0:T(8,128)(2,1)S(1)}, u32[]{:S(2)}, u32[]{:S(2)}) collective-permute-start(bf16[80,1024]{1,0:T(8,128)(2,1)} %forward.1.refs_0_), channel_id=1, source_target_pairs={{0,24},{8,16},{16,8},{24,0},{1,25},{9,17},{17,9},{25,1},{2,26},{10... | collective-permute-start | bytes 491528 | tf_op jit(solution)/shard_map/ppermute | solution.py:614
  43.2 5.6 %collective-permute-start.11 = (bf16[1,320,128]{2,1,0:T(8,128)(2,1)S(1)}, bf16[1,320,128]{2,1,0:T(8,128)(2,1)S(1)}, u32[]{:S(2)}, u32[]{:S(2)}) collective-permute-start(bf16[1,320,128]{2,1,0:T(8,128)(2,1)S(1)} %get-tuple-element.43), channel_id=1, source_target_pairs={{0,2},{1,3},{2,0},{3,1},{4,6},{5,7},{6,4},{7,5},{8,10},{9,11},{10,... | collective-permute-start | bytes 245768 | tf_op jit(solution)/shard_map/ppermute | solution.py:607
  43.3 9.8 %collective-permute-start.12 = (bf16[1,320,128]{2,1,0:T(8,128)(2,1)S(1)}, bf16[1,320,128]{2,1,0:T(8,128)(2,1)S(1)}, u32[]{:S(2)}, u32[]{:S(2)}) collective-permute-start(bf16[1,320,128]{2,1,0:T(8,128)(2,1)S(1)} %get-tuple-element.44), channel_id=1, source_target_pairs={{0,4},{1,5},{2,6},{3,7},{4,0},{5,1},{6,2},{7,3},{8,12},{9,13},{10,... | collective-permute-start | bytes 245768 | tf_op jit(solution)/shard_map/ppermute | solution.py:607
  45.6 7.5 %collective-permute-start.13 = (bf16[1,320,128]{2,1,0:T(8,128)(2,1)S(1)}, bf16[1,320,128]{2,1,0:T(8,128)(2,1)S(1)}, u32[]{:S(2)}, u32[]{:S(2)}) collective-permute-start(bf16[1,320,128]{2,1,0:T(8,128)(2,1)S(1)} %get-tuple-element.45), channel_id=1, source_target_pairs={{0,6},{1,7},{2,4},{3,5},{4,2},{5,3},{6,0},{7,1},{8,14},{9,15},{10,... | collective-permute-start | bytes 245768 | tf_op jit(solution)/shard_map/ppermute | solution.py:607
  54.9 8.6 %collective-permute-start.14 = (bf16[1,320,128]{2,1,0:T(8,128)(2,1)S(1)}, bf16[1,320,128]{2,1,0:T(8,128)(2,1)S(1)}, u32[]{:S(2)}, u32[]{:S(2)}) collective-permute-start(bf16[1,320,128]{2,1,0:T(8,128)(2,1)S(1)} %pair_add.1), channel_id=1, source_target_pairs={{0,4},{1,5},{2,6},{3,7},{4,0},{5,1},{6,2},{7,3},{8,12},{9,13},{10,... | collective-permute-start | bytes 245768 | tf_op jit(solution)/shard_map/ppermute | solution.py:607
  55.7 7.8 %collective-permute-start.15 = (bf16[1,320,128]{2,1,0:T(8,128)(2,1)S(1)}, bf16[1,320,128]{2,1,0:T(8,128)(2,1)S(1)}, u32[]{:S(2)}, u32[]{:S(2)}) collective-permute-start(bf16[1,320,128]{2,1,0:T(8,128)(2,1)S(1)} %pair_add.1), channel_id=1, source_target_pairs={{0,6},{1,7},{2,4},{3,5},{4,2},{5,3},{6,0},{7,1},{8,14},{9,15},{10,... | collective-permute-start | bytes 245768 | tf_op jit(solution)/shard_map/ppermute | solution.py:607
  58.4 6.7 %collective-permute-start.20 = (bf16[2,320,128]{2,1,0:T(8,128)(2,1)S(1)}, bf16[2,320,128]{2,1,0:T(8,128)(2,1)S(1)}, u32[]{:S(2)}, u32[]{:S(2)}) collective-permute-start(bf16[2,320,128]{2,1,0:T(8,128)(2,1)S(1)} %pad_maximum_fusion.refs_0_), channel_id=1, source_target_pairs={{0,8},{8,0},{16,24},{24,16},{1,9},{9,1},{17,25},{25,17},{2,10},{10... | collective-permute-start | bytes 491528 | tf_op jit(solution)/shard_map/ppermute | solution.py:614
  60.0 7.9 %collective-permute-start.22 = (bf16[2,320,128]{2,1,0:T(8,128)(2,1)S(1)}, bf16[2,320,128]{2,1,0:T(8,128)(2,1)S(1)}, u32[]{:S(2)}, u32[]{:S(2)}) collective-permute-start(bf16[2,320,128]{2,1,0:T(8,128)(2,1)S(1)} %pad_maximum_fusion.refs_0_), channel_id=1, source_target_pairs={{0,16},{8,24},{16,0},{24,8},{1,17},{9,25},{17,1},{25,9},{2,18},{10... | collective-permute-start | bytes 491528 | tf_op jit(solution)/shard_map/ppermute | solution.py:614
  61.2 6.7 %collective-permute-start.24 = (bf16[2,320,128]{2,1,0:T(8,128)(2,1)S(1)}, bf16[2,320,128]{2,1,0:T(8,128)(2,1)S(1)}, u32[]{:S(2)}, u32[]{:S(2)}) collective-permute-start(bf16[2,320,128]{2,1,0:T(8,128)(2,1)S(1)} %pad_maximum_fusion.refs_0_), channel_id=1, source_target_pairs={{0,24},{8,16},{16,8},{24,0},{1,25},{9,17},{17,9},{25,1},{2,26},{10... | collective-permute-start | bytes 491528 | tf_op jit(solution)/shard_map/ppermute | solution.py:614
  63.6 7.1 %collective-permute-start.27 = (bf16[2,320,128]{2,1,0:T(8,128)(2,1)S(1)}, bf16[2,320,128]{2,1,0:T(8,128)(2,1)S(1)}, u32[]{:S(2)}, u32[]{:S(2)}) collective-permute-start(bf16[2,320,128]{2,1,0:T(8,128)(2,1)S(1)} %constant_dynamic-update-slice_fusion.refs_0_), channel_id=1, source_target_pairs={{0,8},{8,0},{16,24},{24,16},{1,9},{9,1},{17,25},{25,17},{2,10},{10... | collective-permute-start | bytes 491528 | tf_op jit(solution)/shard_map/ppermute | solution.py:614
  65.1 9.8 %collective-permute-start.29 = (bf16[2,320,128]{2,1,0:T(8,128)(2,1)S(1)}, bf16[2,320,128]{2,1,0:T(8,128)(2,1)S(1)}, u32[]{:S(2)}, u32[]{:S(2)}) collective-permute-start(bf16[2,320,128]{2,1,0:T(8,128)(2,1)S(1)} %constant_dynamic-update-slice_fusion.refs_0_), channel_id=1, source_target_pairs={{0,16},{8,24},{16,0},{24,8},{1,17},{9,25},{17,1},{25,9},{2,18},{10... | collective-permute-start | bytes 491528 | tf_op jit(solution)/shard_map/ppermute | solution.py:614
  67.9 7.1 %collective-permute-start.16 = (bf16[2,320,128]{2,1,0:T(8,128)(2,1)S(1)}, bf16[2,320,128]{2,1,0:T(8,128)(2,1)S(1)}, u32[]{:S(2)}, u32[]{:S(2)}) collective-permute-start(bf16[2,320,128]{2,1,0:T(8,128)(2,1)S(1)} %constant_dynamic-update-slice_fusion.refs_0_), channel_id=1, source_target_pairs={{0,24},{8,16},{16,8},{24,0},{1,25},{9,17},{17,9},{25,1},{2,26},{10... | collective-permute-start | bytes 491528 | tf_op jit(solution)/shard_map/ppermute | solution.py:614
  67.9 7.6 %collective-permute-start.21 = (bf16[2,320,128]{2,1,0:T(8,128)(2,1)S(1)}, bf16[2,320,128]{2,1,0:T(8,128)(2,1)S(1)}, u32[]{:S(2)}, u32[]{:S(2)}) collective-permute-start(bf16[2,320,128]{2,1,0:T(8,128)(2,1)S(1)} %collective-permute-done.20.refs_2_), channel_id=1, source_target_pairs={{0,1},{1,0},{2,3},{3,2},{4,5},{5,4},{6,7},{7,6},{8,9},{9,8},{10,11... | collective-permute-start | bytes 491528 | tf_op jit(solution)/shard_map/ppermute | solution.py:607
  67.9 7.7 %collective-permute-start.23 = (bf16[2,320,128]{2,1,0:T(8,128)(2,1)S(1)}, bf16[2,320,128]{2,1,0:T(8,128)(2,1)S(1)}, u32[]{:S(2)}, u32[]{:S(2)}) collective-permute-start(bf16[2,320,128]{2,1,0:T(8,128)(2,1)S(1)} %collective-permute-done.22.refs_4_), channel_id=1, source_target_pairs={{0,1},{1,0},{2,3},{3,2},{4,5},{5,4},{6,7},{7,6},{8,9},{9,8},{10,11... | collective-permute-start | bytes 491528 | tf_op jit(solution)/shard_map/ppermute | solution.py:607
  70.7 9.8 %collective-permute-start.26 = (bf16[2,320,128]{2,1,0:T(8,128)(2,1)S(1)}, bf16[2,320,128]{2,1,0:T(8,128)(2,1)S(1)}, u32[]{:S(2)}, u32[]{:S(2)}) collective-permute-start(bf16[2,320,128]{2,1,0:T(8,128)(2,1)S(1)} %constant_dynamic-update-slice_fusion.refs_0_), channel_id=1, source_target_pairs={{0,1},{1,0},{2,3},{3,2},{4,5},{5,4},{6,7},{7,6},{8,9},{9,8},{10,11... | collective-permute-start | bytes 491528 | tf_op jit(solution)/shard_map/ppermute | solution.py:607
  75.0 5.5 %collective-permute-start.28 = (bf16[2,320,128]{2,1,0:T(8,128)(2,1)S(1)}, bf16[2,320,128]{2,1,0:T(8,128)(2,1)S(1)}, u32[]{:S(2)}, u32[]{:S(2)}) collective-permute-start(bf16[2,320,128]{2,1,0:T(8,128)(2,1)S(1)} %collective-permute-done.27.refs_2_), channel_id=1, source_target_pairs={{0,1},{1,0},{2,3},{3,2},{4,5},{5,4},{6,7},{7,6},{8,9},{9,8},{10,11... | collective-permute-start | bytes 491528 | tf_op jit(solution)/shard_map/ppermute | solution.py:607
  75.6 6.3 %collective-permute-start.17 = (bf16[2,320,128]{2,1,0:T(8,128)(2,1)S(1)}, bf16[2,320,128]{2,1,0:T(8,128)(2,1)S(1)}, u32[]{:S(2)}, u32[]{:S(2)}) collective-permute-start(bf16[2,320,128]{2,1,0:T(8,128)(2,1)S(1)} %collective-permute-done.16.refs_0_), channel_id=1, source_target_pairs={{0,1},{1,0},{2,3},{3,2},{4,5},{5,4},{6,7},{7,6},{8,9},{9,8},{10,11... | collective-permute-start | bytes 491528 | tf_op jit(solution)/shard_map/ppermute | solution.py:607
  (14 other events, 119.2 us)
where the time goes:
time: 84.6 us; the launch traced here: 84.4 us
  starting transfers between devices  32.1 us (38%)
  Pallas kernels  23.8 us (28%)
  waiting for transfers between devices  23.7 us (28%)
  local copies, waits for them, and re-layouts  2.98 us (4%)
  between operations  1.01 us (1%)
    ppermute x12, starting transfers between devices, swap_member(): return lax.ppermute(value, 'member', [(i, i ^ d) for i in range(members)])  14.4 us
    ppermute x12, waiting for transfers between devices, swap_member(): return lax.ppermute(value, 'member', [(i, i ^ d) for i in range(members)])  12.8 us
    ppermute x17, starting transfers between devices, swap_lon(): return lax.ppermute(value, 'lon', [(i, i ^ d) for i in range(lon_count)])  11.1 us
    ppermute x17, waiting for transfers between devices, swap_lon(): return lax.ppermute(value, 'lon', [(i, i ^ d) for i in range(lon_count)])  9.24 us
    pallas_call x1, Pallas kernels, body(): pl.pallas_call(functools.partial(forward_kernel, plan), out_shape=jax.Sha...  7.28 us
    ppermute x2, starting transfers between devices, swap_far(): return lax.ppermute(value, 'lon', step)  6.6 us
    pallas_call x1, Pallas kernels, body(): pl.pallas_call(functools.partial(gradient_kernel, plan), out_shape=(jax.S...  6.28 us
    pallas_call x3, Pallas kernels, assemble(): pl.pallas_call(kernel, out_shape=[grad_shape, jax.ShapeDtypeStruct(other_...  5.66 us
  transfers between devices with their start and end apart: 31, of which 10 were waited for; matrix products, arithmetic and copies ran while one was open for 1% of the time, Pallas kernels for 17%

commit v1 on v0

--- a/solution.py
+++ b/solution.py
@@ -176,9 +176,10 @@
         o_ref[rows, :] = jnp.where(keep, total, 0.0).astype(o_ref.dtype)
 
 
-def prep_kernel(plan, obs_ref, near_ref, far_ref, *refs):
-    truth_ref, row_s = refs[-2:]
-    refs = refs[:-2]
+def prep_kernel(plan, obs_ref, near_ref, far_ref, own_ref, *refs):
+    truth_ref, own_out_ref, row_s = refs[-3:]
+    refs = refs[:-3]
+    own_out_ref[...] = own_ref[...]
     half, offset, padded_out = plan.half, plan.offset, plan.padded_out
     even = here()[2] == 0
     near, far = near_ref[...], far_ref[...]
@@ -662,19 +663,21 @@
     far = swap_far(strips[0])
     near = swap_lon(strips[1], 1)
     tiles = main + 1
-    x_all, truth = pl.pallas_call(
+    x_all, truth, own_copy = pl.pallas_call(
         functools.partial(prep_kernel, plan),
         out_shape=(
             jax.ShapeDtypeStruct((members, rows_in, slots, tiles * LANES), jnp.bfloat16),
             jax.ShapeDtypeStruct((padded_out, points), jnp.float32),
+            jax.ShapeDtypeStruct((padded_out, points), jnp.bfloat16),
         ),
-        in_specs=[vmem()] * (members + 3),
-        out_specs=[vmem()] * 2,
+        in_specs=[vmem()] * (members + 4),
+        out_specs=[vmem()] * 3,
         scratch_shapes=[pltpu.VMEM((rows_out, slots, LANES), jnp.float32)],
         cost_estimate=cost(0, 4_000_000),
         compiler_params=limit(20),
         name="prep",
-    )(seen, near, far, *traded)
+    )(seen, near, far, own_outputs, *traded)
+    outputs[0] = own_copy
 
     main_rows = half_rows // pairs
     piece_rows = main * main_rows + main_rows // pack

time: 84.6 us -> 83.7 us (0.989)
  waiting for transfers between devices: 23.7 us -> 22.1 us
    ppermute x12, waiting for transfers between devices: 12.8 us -> 11.2 us  [swap_member(): return lax.ppermute(value, 'member', [(i, i ^ d) for i in range(members)])]
where the time goes in v1:
time: 83.7 us; the launch traced here: 83.4 us
  starting transfers between devices  32.9 us (39%)
  Pallas kernels  23.8 us (28%)
  waiting for transfers between devices  22.1 us (26%)
  local copies, waits for them, and re-layouts  2.99 us (4%)
  between operations  1.01 us (1%)
    ppermute x12, starting transfers between devices, swap_member(): return lax.ppermute(value, 'member', [(i, i ^ d) for i in range(members)])  15.1 us
    ppermute x12, waiting for transfers between devices, swap_member(): return lax.ppermute(value, 'member', [(i, i ^ d) for i in range(members)])  11.2 us
    ppermute x17, starting transfers between devices, swap_lon(): return lax.ppermute(value, 'lon', [(i, i ^ d) for i in range(lon_count)])  11.1 us
    ppermute x17, waiting for transfers between devices, swap_lon(): return lax.ppermute(value, 'lon', [(i, i ^ d) for i in range(lon_count)])  9.24 us
    pallas_call x1, Pallas kernels, body(): pl.pallas_call(functools.partial(forward_kernel, plan), out_shape=jax.Sha...  7.28 us
    ppermute x2, starting transfers between devices, swap_far(): return lax.ppermute(value, 'lon', step)  6.6 us
    pallas_call x1, Pallas kernels, body(): pl.pallas_call(functools.partial(gradient_kernel, plan), out_shape=(jax.S...  6.29 us
    pallas_call x3, Pallas kernels, assemble(): pl.pallas_call(kernel, out_shape=[grad_shape, jax.ShapeDtypeStruct(other_...  5.66 us
  transfers between devices with their start and end apart: 31, of which 10 were waited for; matrix products, arithmetic and copies ran while one was open for 1% of the time, Pallas kernels for 17%

profile of v1, /device:TPU:0, one launch (start us, length us, event | category | flops | bytes accessed | tf_op | source)
XLA Modules:
  0.0 83.4 jit_solution(10723398439607235620)
XLA Ops:
  3.3 4.7 %collective-permute-start.1 = (bf16[20,4,641]{2,1,0:T(4,128)(2,1)S(1)}, bf16[20,4,641]{2,1,0:T(4,128)(2,1)S(1)}, u32[]{:S(2)}, u32[]{:S(2)}) collective-permute-start(bf16[20,4,641]{2,1,0:T(4,128)(2,1)S(1)} %get-tuple-element.30), channel_id=1, source_target_pairs={{0,7},{1,2},{2,1},{3,4},{4,3},{5,6},{6,5},{7,0},{8,15},{9,10},{10,... | collective-permute-start | bytes 307688 | tf_op jit(solution)/shard_map/ppermute | solution.py:612
  8.0 1.5 %collective-permute-start.4 = (bf16[26,45,128]{2,1,0:T(8,128)(2,1)S(1)}, bf16[26,45,128]{2,1,0:T(8,128)(2,1)S(1)}, u32[]{:S(2)}, u32[]{:S(2)}) collective-permute-start(bf16[26,45,128]{2,1,0:T(8,128)(2,1)S(1)} %get-tuple-element.34), channel_id=1, source_target_pairs={{0,8},{8,0},{16,24},{24,16},{1,9},{9,1},{17,25},{25,17},{2,10},{10... | collective-permute-start | bytes 898568 | tf_op jit(solution)/shard_map/ppermute | solution.py:615
  9.5 1.5 %collective-permute-start.5 = (bf16[26,45,128]{2,1,0:T(8,128)(2,1)S(1)}, bf16[26,45,128]{2,1,0:T(8,128)(2,1)S(1)}, u32[]{:S(2)}, u32[]{:S(2)}) collective-permute-start(bf16[26,45,128]{2,1,0:T(8,128)(2,1)S(1)} %get-tuple-element.35), channel_id=1, source_target_pairs={{0,16},{8,24},{16,0},{24,8},{1,17},{9,25},{17,1},{25,9},{2,18},{10... | collective-permute-start | bytes 898568 | tf_op jit(solution)/shard_map/ppermute | solution.py:615
  12.9 7.3 %forward.1.own_ref = bf16[80,1024]{1,0:T(8,128)(2,1)} custom-call(bf16[20,45,641]{2,1,0:T(8,128)(2,1)} %bitcast.13, bf16[20,4,641]{2,1,0:T(4,128)(2,1)} %copy-done.5, bf16[20,4,641]{2,1,0:T(4,128)(2,1)} %copy-done.6, bf16[25,73,641]{2,1,0:T(8,128)(2,1)} %bitcast.21, f32[1,73]{1,0:T(1,128)} %bitcast.22), custom_call_target="tpu_custom_call" | custom-call | flops 3145728000 | bytes 6000000 | tf_op jit(solution)/shard_map/forward/pallas_call | solution.py:637
  20.3 1.9 %collective-permute-start.3 = (f32[2,16,73]{2,1,0:T(8,128)S(1)}, f32[2,16,73]{2,1,0:T(8,128)S(1)}, u32[]{:S(2)}, u32[]{:S(2)}) collective-permute-start(f32[2,16,73]{2,1,0:T(8,128)S(1)} %get-tuple-element.32), channel_id=1, source_target_pairs={{0,7},{1,2},{2,1},{3,4},{4,3},{5,6},{6,5},{7,0},{8,15},{9,10},{10,... | collective-permute-start | bytes 28040 | tf_op jit(solution)/shard_map/ppermute | solution.py:612
  22.2 1.5 %collective-permute-start.7 = (bf16[80,1024]{1,0:T(8,128)(2,1)}, bf16[80,1024]{1,0:T(8,128)(2,1)S(1)}, u32[]{:S(2)}, u32[]{:S(2)}) collective-permute-start(bf16[80,1024]{1,0:T(8,128)(2,1)} %forward.1.own_ref), channel_id=1, source_target_pairs={{0,8},{8,0},{16,24},{24,16},{1,9},{9,1},{17,25},{25,17},{2,10},{10... | collective-permute-start | bytes 491528 | tf_op jit(solution)/shard_map/ppermute | solution.py:615
  23.7 1.6 %collective-permute-done.3.far_ref = f32[2,16,73]{2,1,0:T(8,128)S(1)} collective-permute-done((f32[2,16,73]{2,1,0:T(8,128)S(1)}, f32[2,16,73]{2,1,0:T(8,128)S(1)}, u32[]{:S(2)}, u32[]{:S(2)}) %collective-permute-start.3) | collective-permute-done | bytes 9376 | tf_op jit(solution)/shard_map/ppermute | solution.py:612
  25.3 1.5 %collective-permute-start.8 = (bf16[80,1024]{1,0:T(8,128)(2,1)}, bf16[80,1024]{1,0:T(8,128)(2,1)S(1)}, u32[]{:S(2)}, u32[]{:S(2)}) collective-permute-start(bf16[80,1024]{1,0:T(8,128)(2,1)} %forward.1.own_ref), channel_id=1, source_target_pairs={{0,16},{8,24},{16,0},{24,8},{1,17},{9,25},{17,1},{25,9},{2,18},{10... | collective-permute-start | bytes 491528 | tf_op jit(solution)/shard_map/ppermute | solution.py:615
  26.9 1.4 %collective-permute-start.9 = (bf16[80,1024]{1,0:T(8,128)(2,1)}, bf16[80,1024]{1,0:T(8,128)(2,1)S(1)}, u32[]{:S(2)}, u32[]{:S(2)}) collective-permute-start(bf16[80,1024]{1,0:T(8,128)(2,1)} %forward.1.own_ref), channel_id=1, source_target_pairs={{0,24},{8,16},{16,8},{24,0},{1,25},{9,17},{17,9},{25,1},{2,26},{10... | collective-permute-start | bytes 491528 | tf_op jit(solution)/shard_map/ppermute | solution.py:615
  30.3 3.9 %collective-permute-done.8.refs_2_ = bf16[80,1024]{1,0:T(8,128)(2,1)S(1)} collective-permute-done((bf16[80,1024]{1,0:T(8,128)(2,1)}, bf16[80,1024]{1,0:T(8,128)(2,1)S(1)}, u32[]{:S(2)}, u32[]{:S(2)}) %collective-permute-start.8) | collective-permute-done | bytes 163872 | tf_op jit(solution)/shard_map/ppermute | solution.py:615
  34.2 6.3 %gradient.1 = (bf16[80,1024]{1,0:T(8,128)(2,1)S(1)}, f32[1,1024]{1,0:T(1,128)S(1)}, bf16[4,320,128]{2,1,0:T(8,128)(2,1)S(1)}, f32[4,320,128]{2,1,0:T(8,128)S(1)}) custom-call(bf16[80,1024]{1,0:T(8,128)(2,1)S(1)} %get-tuple-element.37.refs_0_, bf16[80,1024]{1,0:T(8,128)(2,1)S(1)} %collective-permute-done.7.refs_1_, ...), custom_call_target="tpu_custom_call" | custom-call | flops 4194304000 | bytes 6000000 | tf_op jit(solution)/shard_map/gradient/pallas_call | solution.py:685
  40.6 1.6 %collective-permute-done.10.got_ref = bf16[4,320,128]{2,1,0:T(8,128)(2,1)S(1)} collective-permute-done((bf16[4,320,128]{2,1,0:T(8,128)(2,1)S(1)}, bf16[4,320,128]{2,1,0:T(8,128)(2,1)S(1)}, u32[]{:S(2)}, u32[]{:S(2)}) %collective-permute-start.10) | collective-permute-done | bytes 327712 | tf_op jit(solution)/shard_map/ppermute | solution.py:608
  42.4 2.3 %collective-permute-start.12 = (bf16[1,320,128]{2,1,0:T(8,128)(2,1)S(1)}, bf16[1,320,128]{2,1,0:T(8,128)(2,1)S(1)}, u32[]{:S(2)}, u32[]{:S(2)}) collective-permute-start(bf16[1,320,128]{2,1,0:T(8,128)(2,1)S(1)} %get-tuple-element.46), channel_id=1, source_target_pairs={{0,4},{1,5},{2,6},{3,7},{4,0},{5,1},{6,2},{7,3},{8,12},{9,13},{10,... | collective-permute-start | bytes 245768 | tf_op jit(solution)/shard_map/ppermute | solution.py:608
  44.7 2.1 %collective-permute-start.13 = (bf16[1,320,128]{2,1,0:T(8,128)(2,1)S(1)}, bf16[1,320,128]{2,1,0:T(8,128)(2,1)S(1)}, u32[]{:S(2)}, u32[]{:S(2)}) collective-permute-start(bf16[1,320,128]{2,1,0:T(8,128)(2,1)S(1)} %get-tuple-element.47), channel_id=1, source_target_pairs={{0,6},{1,7},{2,4},{3,5},{4,2},{5,3},{6,0},{7,1},{8,14},{9,15},{10,... | collective-permute-start | bytes 245768 | tf_op jit(solution)/shard_map/ppermute | solution.py:608
  47.9 4.3 %collective-permute-done.12.refs_1_ = bf16[1,320,128]{2,1,0:T(8,128)(2,1)S(1)} collective-permute-done((bf16[1,320,128]{2,1,0:T(8,128)(2,1)S(1)}, bf16[1,320,128]{2,1,0:T(8,128)(2,1)S(1)}, u32[]{:S(2)}, u32[]{:S(2)}) %collective-permute-start.12) | collective-permute-done | bytes 81952 | tf_op jit(solution)/shard_map/ppermute | solution.py:608
  52.4 1.6 %collective-permute-start.18 = (bf16[1,320,128]{2,1,0:T(8,128)(2,1)S(1)}, bf16[1,320,128]{2,1,0:T(8,128)(2,1)S(1)}, u32[]{:S(2)}, u32[]{:S(2)}) collective-permute-start(bf16[1,320,128]{2,1,0:T(8,128)(2,1)S(1)} %pair_add.1), channel_id=1, source_target_pairs={{0,2},{1,3},{2,0},{3,1},{4,6},{5,7},{6,4},{7,5},{8,10},{9,11},{10,... | collective-permute-start | bytes 245768 | tf_op jit(solution)/shard_map/ppermute | solution.py:608
  54.8 2.0 %collective-permute-start.15 = (bf16[1,320,128]{2,1,0:T(8,128)(2,1)S(1)}, bf16[1,320,128]{2,1,0:T(8,128)(2,1)S(1)}, u32[]{:S(2)}, u32[]{:S(2)}) collective-permute-start(bf16[1,320,128]{2,1,0:T(8,128)(2,1)S(1)} %pair_add.1), channel_id=1, source_target_pairs={{0,6},{1,7},{2,4},{3,5},{4,2},{5,3},{6,0},{7,1},{8,14},{9,15},{10,... | collective-permute-start | bytes 245768 | tf_op jit(solution)/shard_map/ppermute | solution.py:608
  57.5 1.6 %collective-permute-start.20 = (bf16[2,320,128]{2,1,0:T(8,128)(2,1)S(1)}, bf16[2,320,128]{2,1,0:T(8,128)(2,1)S(1)}, u32[]{:S(2)}, u32[]{:S(2)}) collective-permute-start(bf16[2,320,128]{2,1,0:T(8,128)(2,1)S(1)} %pad_maximum_fusion.refs_0_), channel_id=1, source_target_pairs={{0,8},{8,0},{16,24},{24,16},{1,9},{9,1},{17,25},{25,17},{2,10},{10... | collective-permute-start | bytes 491528 | tf_op jit(solution)/shard_map/ppermute | solution.py:615
  61.1 1.5 %collective-permute-done.14 = bf16[1,320,128]{2,1,0:T(8,128)(2,1)S(1)} collective-permute-done((bf16[1,320,128]{2,1,0:T(8,128)(2,1)S(1)}, bf16[1,320,128]{2,1,0:T(8,128)(2,1)S(1)}, u32[]{:S(2)}, u32[]{:S(2)}) %collective-permute-start.14) | collective-permute-done | bytes 81952 | tf_op jit(solution)/shard_map/ppermute | solution.py:608
  62.7 1.6 %collective-permute-start.27 = (bf16[2,320,128]{2,1,0:T(8,128)(2,1)S(1)}, bf16[2,320,128]{2,1,0:T(8,128)(2,1)S(1)}, u32[]{:S(2)}, u32[]{:S(2)}) collective-permute-start(bf16[2,320,128]{2,1,0:T(8,128)(2,1)S(1)} %constant_dynamic-update-slice_fusion.refs_0_), channel_id=1, source_target_pairs={{0,8},{8,0},{16,24},{24,16},{1,9},{9,1},{17,25},{25,17},{2,10},{10... | collective-permute-start | bytes 491528 | tf_op jit(solution)/shard_map/ppermute | solution.py:615
  67.9 1.9 %collective-permute-done.27.refs_2_ = bf16[2,320,128]{2,1,0:T(8,128)(2,1)S(1)} collective-permute-done((bf16[2,320,128]{2,1,0:T(8,128)(2,1)S(1)}, bf16[2,320,128]{2,1,0:T(8,128)(2,1)S(1)}, u32[]{:S(2)}, u32[]{:S(2)}) %collective-permute-start.27) | collective-permute-done | bytes 163872 | tf_op jit(solution)/shard_map/ppermute | solution.py:615
  69.8 4.3 %collective-permute-done.29.refs_4_ = bf16[2,320,128]{2,1,0:T(8,128)(2,1)S(1)} collective-permute-done((bf16[2,320,128]{2,1,0:T(8,128)(2,1)S(1)}, bf16[2,320,128]{2,1,0:T(8,128)(2,1)S(1)}, u32[]{:S(2)}, u32[]{:S(2)}) %collective-permute-start.29) | collective-permute-done | bytes 163872 | tf_op jit(solution)/shard_map/ppermute | solution.py:615
  77.6 2.0 %assemble.3 = (f32[25,73,641]{2,1,0:T(8,128)}, f32[5,64,128]{2,1,0:T(8,128)S(1)}) custom-call(bf16[2,320,128]{2,1,0:T(8,128)(2,1)S(1)} %pad_maximum_fusion.refs_0_, bf16[2,320,128]{2,1,0:T(8,128)(2,1)S(1)} %collective-permute-done.19.refs_1_, bf16[2,320,128]{2,1,0:T(8,128)(2,1)S(1)} %collective-permute-done.20.refs_2_, ...), custom_call_target="tpu_custom_call" | custom-call | bytes 5000000 | tf_op jit(solution)/shard_map/assemble/pallas_call | solution.py:768
  81.0 2.3 %assemble.5 = (f32[25,73,641]{2,1,0:T(8,128)}, f32[1,73]{1,0:T(1,128)}) custom-call(bf16[2,320,128]{2,1,0:T(8,128)(2,1)S(1)} %collective-permute-done.16.refs_0_, bf16[2,320,128]{2,1,0:T(8,128)(2,1)S(1)} %collective-permute-done.17.refs_1_, f32[5,64,128]{2,1,0:T(8,128)S(1)} %get-tuple-element.48.refs_6_.refs_2_, ...), custom_call_target="tpu_custom_call", output_to_operand_aliasing={{0}: (3, {})} | custom-call | bytes 5000000 | tf_op jit(solution)/shard_map/assemble/pallas_call | solution.py:768
  (67 shorter events, 20.3 us)
Async XLA Ops:
  2.8 9.5 %collective-permute-start = (bf16[20,4,641]{2,1,0:T(4,128)(2,1)S(1)}, bf16[20,4,641]{2,1,0:T(4,128)(2,1)S(1)}, u32[]{:S(2)}, u32[]{:S(2)}) collective-permute-start(bf16[20,4,641]{2,1,0:T(4,128)(2,1)S(1)} %get-tuple-element.29), channel_id=1, source_target_pairs={{0,1},{1,0},{2,3},{3,2},{4,5},{5,4},{6,7},{7,6},{8,9},{9,8},{10,11... | collective-permute-start | bytes 307688 | tf_op jit(solution)/shard_map/ppermute | solution.py:608
  3.3 8.9 %collective-permute-start.1 = (bf16[20,4,641]{2,1,0:T(4,128)(2,1)S(1)}, bf16[20,4,641]{2,1,0:T(4,128)(2,1)S(1)}, u32[]{:S(2)}, u32[]{:S(2)}) collective-permute-start(bf16[20,4,641]{2,1,0:T(4,128)(2,1)S(1)} %get-tuple-element.30), channel_id=1, source_target_pairs={{0,7},{1,2},{2,1},{3,4},{4,3},{5,6},{6,5},{7,0},{8,15},{9,10},{10,... | collective-permute-start | bytes 307688 | tf_op jit(solution)/shard_map/ppermute | solution.py:612
  8.0 18.8 %collective-permute-start.4 = (bf16[26,45,128]{2,1,0:T(8,128)(2,1)S(1)}, bf16[26,45,128]{2,1,0:T(8,128)(2,1)S(1)}, u32[]{:S(2)}, u32[]{:S(2)}) collective-permute-start(bf16[26,45,128]{2,1,0:T(8,128)(2,1)S(1)} %get-tuple-element.34), channel_id=1, source_target_pairs={{0,8},{8,0},{16,24},{24,16},{1,9},{9,1},{17,25},{25,17},{2,10},{10... | collective-permute-start | bytes 898568 | tf_op jit(solution)/shard_map/ppermute | solution.py:615
  9.5 18.8 %collective-permute-start.5 = (bf16[26,45,128]{2,1,0:T(8,128)(2,1)S(1)}, bf16[26,45,128]{2,1,0:T(8,128)(2,1)S(1)}, u32[]{:S(2)}, u32[]{:S(2)}) collective-permute-start(bf16[26,45,128]{2,1,0:T(8,128)(2,1)S(1)} %get-tuple-element.35), channel_id=1, source_target_pairs={{0,16},{8,24},{16,0},{24,8},{1,17},{9,25},{17,1},{25,9},{2,18},{10... | collective-permute-start | bytes 898568 | tf_op jit(solution)/shard_map/ppermute | solution.py:615
  11.0 17.3 %collective-permute-start.6 = (bf16[26,45,128]{2,1,0:T(8,128)(2,1)S(1)}, bf16[26,45,128]{2,1,0:T(8,128)(2,1)S(1)}, u32[]{:S(2)}, u32[]{:S(2)}) collective-permute-start(bf16[26,45,128]{2,1,0:T(8,128)(2,1)S(1)} %get-tuple-element.36), channel_id=1, source_target_pairs={{0,24},{8,16},{16,8},{24,0},{1,25},{9,17},{17,9},{25,1},{2,26},{10... | collective-permute-start | bytes 898568 | tf_op jit(solution)/shard_map/ppermute | solution.py:615
  22.2 8.1 %collective-permute-start.7 = (bf16[80,1024]{1,0:T(8,128)(2,1)}, bf16[80,1024]{1,0:T(8,128)(2,1)S(1)}, u32[]{:S(2)}, u32[]{:S(2)}) collective-permute-start(bf16[80,1024]{1,0:T(8,128)(2,1)} %forward.1.own_ref), channel_id=1, source_target_pairs={{0,8},{8,0},{16,24},{24,16},{1,9},{9,1},{17,25},{25,17},{2,10},{10... | collective-permute-start | bytes 491528 | tf_op jit(solution)/shard_map/ppermute | solution.py:615
  25.3 8.8 %collective-permute-start.8 = (bf16[80,1024]{1,0:T(8,128)(2,1)}, bf16[80,1024]{1,0:T(8,128)(2,1)S(1)}, u32[]{:S(2)}, u32[]{:S(2)}) collective-permute-start(bf16[80,1024]{1,0:T(8,128)(2,1)} %forward.1.own_ref), channel_id=1, source_target_pairs={{0,16},{8,24},{16,0},{24,8},{1,17},{9,25},{17,1},{25,9},{2,18},{10... | collective-permute-start | bytes 491528 | tf_op jit(solution)/shard_map/ppermute | solution.py:615
  26.9 7.3 %collective-permute-start.9 = (bf16[80,1024]{1,0:T(8,128)(2,1)}, bf16[80,1024]{1,0:T(8,128)(2,1)S(1)}, u32[]{:S(2)}, u32[]{:S(2)}) collective-permute-start(bf16[80,1024]{1,0:T(8,128)(2,1)} %forward.1.own_ref), channel_id=1, source_target_pairs={{0,24},{8,16},{16,8},{24,0},{1,25},{9,17},{17,9},{25,1},{2,26},{10... | collective-permute-start | bytes 491528 | tf_op jit(solution)/shard_map/ppermute | solution.py:615
  42.3 5.6 %collective-permute-start.11 = (bf16[1,320,128]{2,1,0:T(8,128)(2,1)S(1)}, bf16[1,320,128]{2,1,0:T(8,128)(2,1)S(1)}, u32[]{:S(2)}, u32[]{:S(2)}) collective-permute-start(bf16[1,320,128]{2,1,0:T(8,128)(2,1)S(1)} %get-tuple-element.45), channel_id=1, source_target_pairs={{0,2},{1,3},{2,0},{3,1},{4,6},{5,7},{6,4},{7,5},{8,10},{9,11},{10,... | collective-permute-start | bytes 245768 | tf_op jit(solution)/shard_map/ppermute | solution.py:608
  42.4 9.8 %collective-permute-start.12 = (bf16[1,320,128]{2,1,0:T(8,128)(2,1)S(1)}, bf16[1,320,128]{2,1,0:T(8,128)(2,1)S(1)}, u32[]{:S(2)}, u32[]{:S(2)}) collective-permute-start(bf16[1,320,128]{2,1,0:T(8,128)(2,1)S(1)} %get-tuple-element.46), channel_id=1, source_target_pairs={{0,4},{1,5},{2,6},{3,7},{4,0},{5,1},{6,2},{7,3},{8,12},{9,13},{10,... | collective-permute-start | bytes 245768 | tf_op jit(solution)/shard_map/ppermute | solution.py:608
  44.7 7.5 %collective-permute-start.13 = (bf16[1,320,128]{2,1,0:T(8,128)(2,1)S(1)}, bf16[1,320,128]{2,1,0:T(8,128)(2,1)S(1)}, u32[]{:S(2)}, u32[]{:S(2)}) collective-permute-start(bf16[1,320,128]{2,1,0:T(8,128)(2,1)S(1)} %get-tuple-element.47), channel_id=1, source_target_pairs={{0,6},{1,7},{2,4},{3,5},{4,2},{5,3},{6,0},{7,1},{8,14},{9,15},{10,... | collective-permute-start | bytes 245768 | tf_op jit(solution)/shard_map/ppermute | solution.py:608
  54.0 8.6 %collective-permute-start.14 = (bf16[1,320,128]{2,1,0:T(8,128)(2,1)S(1)}, bf16[1,320,128]{2,1,0:T(8,128)(2,1)S(1)}, u32[]{:S(2)}, u32[]{:S(2)}) collective-permute-start(bf16[1,320,128]{2,1,0:T(8,128)(2,1)S(1)} %pair_add.1), channel_id=1, source_target_pairs={{0,4},{1,5},{2,6},{3,7},{4,0},{5,1},{6,2},{7,3},{8,12},{9,13},{10,... | collective-permute-start | bytes 245768 | tf_op jit(solution)/shard_map/ppermute | solution.py:608
  54.8 7.8 %collective-permute-start.15 = (bf16[1,320,128]{2,1,0:T(8,128)(2,1)S(1)}, bf16[1,320,128]{2,1,0:T(8,128)(2,1)S(1)}, u32[]{:S(2)}, u32[]{:S(2)}) collective-permute-start(bf16[1,320,128]{2,1,0:T(8,128)(2,1)S(1)} %pair_add.1), channel_id=1, source_target_pairs={{0,6},{1,7},{2,4},{3,5},{4,2},{5,3},{6,0},{7,1},{8,14},{9,15},{10,... | collective-permute-start | bytes 245768 | tf_op jit(solution)/shard_map/ppermute | solution.py:608
  57.5 6.7 %collective-permute-start.20 = (bf16[2,320,128]{2,1,0:T(8,128)(2,1)S(1)}, bf16[2,320,128]{2,1,0:T(8,128)(2,1)S(1)}, u32[]{:S(2)}, u32[]{:S(2)}) collective-permute-start(bf16[2,320,128]{2,1,0:T(8,128)(2,1)S(1)} %pad_maximum_fusion.refs_0_), channel_id=1, source_target_pairs={{0,8},{8,0},{16,24},{24,16},{1,9},{9,1},{17,25},{25,17},{2,10},{10... | collective-permute-start | bytes 491528 | tf_op jit(solution)/shard_map/ppermute | solution.py:615
  59.1 7.6 %collective-permute-start.22 = (bf16[2,320,128]{2,1,0:T(8,128)(2,1)S(1)}, bf16[2,320,128]{2,1,0:T(8,128)(2,1)S(1)}, u32[]{:S(2)}, u32[]{:S(2)}) collective-permute-start(bf16[2,320,128]{2,1,0:T(8,128)(2,1)S(1)} %pad_maximum_fusion.refs_0_), channel_id=1, source_target_pairs={{0,16},{8,24},{16,0},{24,8},{1,17},{9,25},{17,1},{25,9},{2,18},{10... | collective-permute-start | bytes 491528 | tf_op jit(solution)/shard_map/ppermute | solution.py:615
  60.3 7.1 %collective-permute-start.24 = (bf16[2,320,128]{2,1,0:T(8,128)(2,1)S(1)}, bf16[2,320,128]{2,1,0:T(8,128)(2,1)S(1)}, u32[]{:S(2)}, u32[]{:S(2)}) collective-permute-start(bf16[2,320,128]{2,1,0:T(8,128)(2,1)S(1)} %pad_maximum_fusion.refs_0_), channel_id=1, source_target_pairs={{0,24},{8,16},{16,8},{24,0},{1,25},{9,17},{17,9},{25,1},{2,26},{10... | collective-permute-start | bytes 491528 | tf_op jit(solution)/shard_map/ppermute | solution.py:615
  62.7 7.1 %collective-permute-start.27 = (bf16[2,320,128]{2,1,0:T(8,128)(2,1)S(1)}, bf16[2,320,128]{2,1,0:T(8,128)(2,1)S(1)}, u32[]{:S(2)}, u32[]{:S(2)}) collective-permute-start(bf16[2,320,128]{2,1,0:T(8,128)(2,1)S(1)} %constant_dynamic-update-slice_fusion.refs_0_), channel_id=1, source_target_pairs={{0,8},{8,0},{16,24},{24,16},{1,9},{9,1},{17,25},{25,17},{2,10},{10... | collective-permute-start | bytes 491528 | tf_op jit(solution)/shard_map/ppermute | solution.py:615
  64.2 9.8 %collective-permute-start.29 = (bf16[2,320,128]{2,1,0:T(8,128)(2,1)S(1)}, bf16[2,320,128]{2,1,0:T(8,128)(2,1)S(1)}, u32[]{:S(2)}, u32[]{:S(2)}) collective-permute-start(bf16[2,320,128]{2,1,0:T(8,128)(2,1)S(1)} %constant_dynamic-update-slice_fusion.refs_0_), channel_id=1, source_target_pairs={{0,16},{8,24},{16,0},{24,8},{1,17},{9,25},{17,1},{25,9},{2,18},{10... | collective-permute-start | bytes 491528 | tf_op jit(solution)/shard_map/ppermute | solution.py:615
  66.7 7.4 %collective-permute-start.16 = (bf16[2,320,128]{2,1,0:T(8,128)(2,1)S(1)}, bf16[2,320,128]{2,1,0:T(8,128)(2,1)S(1)}, u32[]{:S(2)}, u32[]{:S(2)}) collective-permute-start(bf16[2,320,128]{2,1,0:T(8,128)(2,1)S(1)} %constant_dynamic-update-slice_fusion.refs_0_), channel_id=1, source_target_pairs={{0,24},{8,16},{16,8},{24,0},{1,25},{9,17},{17,9},{25,1},{2,26},{10... | collective-permute-start | bytes 491528 | tf_op jit(solution)/shard_map/ppermute | solution.py:615
  67.4 7.2 %collective-permute-start.21 = (bf16[2,320,128]{2,1,0:T(8,128)(2,1)S(1)}, bf16[2,320,128]{2,1,0:T(8,128)(2,1)S(1)}, u32[]{:S(2)}, u32[]{:S(2)}) collective-permute-start(bf16[2,320,128]{2,1,0:T(8,128)(2,1)S(1)} %collective-permute-done.20.refs_2_), channel_id=1, source_target_pairs={{0,1},{1,0},{2,3},{3,2},{4,5},{5,4},{6,7},{7,6},{8,9},{9,8},{10,11... | collective-permute-start | bytes 491528 | tf_op jit(solution)/shard_map/ppermute | solution.py:608
  67.4 7.2 %collective-permute-start.23 = (bf16[2,320,128]{2,1,0:T(8,128)(2,1)S(1)}, bf16[2,320,128]{2,1,0:T(8,128)(2,1)S(1)}, u32[]{:S(2)}, u32[]{:S(2)}) collective-permute-start(bf16[2,320,128]{2,1,0:T(8,128)(2,1)S(1)} %collective-permute-done.22.refs_4_), channel_id=1, source_target_pairs={{0,1},{1,0},{2,3},{3,2},{4,5},{5,4},{6,7},{7,6},{8,9},{9,8},{10,11... | collective-permute-start | bytes 491528 | tf_op jit(solution)/shard_map/ppermute | solution.py:608
  69.8 9.8 %collective-permute-start.26 = (bf16[2,320,128]{2,1,0:T(8,128)(2,1)S(1)}, bf16[2,320,128]{2,1,0:T(8,128)(2,1)S(1)}, u32[]{:S(2)}, u32[]{:S(2)}) collective-permute-start(bf16[2,320,128]{2,1,0:T(8,128)(2,1)S(1)} %constant_dynamic-update-slice_fusion.refs_0_), channel_id=1, source_target_pairs={{0,1},{1,0},{2,3},{3,2},{4,5},{5,4},{6,7},{7,6},{8,9},{9,8},{10,11... | collective-permute-start | bytes 491528 | tf_op jit(solution)/shard_map/ppermute | solution.py:608
  74.1 5.5 %collective-permute-start.28 = (bf16[2,320,128]{2,1,0:T(8,128)(2,1)S(1)}, bf16[2,320,128]{2,1,0:T(8,128)(2,1)S(1)}, u32[]{:S(2)}, u32[]{:S(2)}) collective-permute-start(bf16[2,320,128]{2,1,0:T(8,128)(2,1)S(1)} %collective-permute-done.27.refs_2_), channel_id=1, source_target_pairs={{0,1},{1,0},{2,3},{3,2},{4,5},{5,4},{6,7},{7,6},{8,9},{9,8},{10,11... | collective-permute-start | bytes 491528 | tf_op jit(solution)/shard_map/ppermute | solution.py:608
  74.7 6.3 %collective-permute-start.17 = (bf16[2,320,128]{2,1,0:T(8,128)(2,1)S(1)}, bf16[2,320,128]{2,1,0:T(8,128)(2,1)S(1)}, u32[]{:S(2)}, u32[]{:S(2)}) collective-permute-start(bf16[2,320,128]{2,1,0:T(8,128)(2,1)S(1)} %collective-permute-done.16.refs_0_), channel_id=1, source_target_pairs={{0,1},{1,0},{2,3},{3,2},{4,5},{5,4},{6,7},{7,6},{8,9},{9,8},{10,11... | collective-permute-start | bytes 491528 | tf_op jit(solution)/shard_map/ppermute | solution.py:608
  (14 other events, 119.6 us)

commit v2 on v1

--- a/solution.py
+++ b/solution.py
@@ -53,7 +53,7 @@
     return jnp.transpose(jnp.broadcast_to(row, (LANES, LANES)))[:, :1]
 
 
-def pack_kernel(plan, f_ref, near_ref, far_ref, *out_refs):
+def pack_kernel(plan, f_ref, seen_ref, near_ref, far_ref, seen_near_ref, seen_far_ref, *out_refs):
     members, main, rest = plan.members, plan.main, plan.rest
     pack, valid, sub = plan.pack, plan.valid, plan.sub
     rows_in, lon_dev, in_chan = f_ref.shape
@@ -65,6 +65,10 @@
     end_edge = f_ref[:, final:, :].astype(jnp.float32)[:, lon_dev - halo - final :]
     far_ref[...] = jnp.where(even, start_edge, end_edge).astype(far_ref.dtype)
     near_ref[...] = jnp.where(even, end_edge, start_edge).astype(near_ref.dtype)
+    start_seen = seen_ref[: plan.half]
+    end_seen = seen_ref[lon_dev - plan.half :]
+    seen_far_ref[...] = jnp.where(even, start_seen, end_seen)
+    seen_near_ref[...] = jnp.where(even, end_seen, start_seen)
     group = rows_in // pack
     base = main * members
     lane = lax.broadcasted_iota(jnp.int32, (1, 1, LANES), 2)
@@ -94,9 +98,17 @@
         out[main * rows_in + group] = slab[0].astype(out.dtype)
 
 
+def stage_kernel(w_ref, w_out):
+    _, out_chan, in_chan = w_ref.shape
+    full = in_chan // LANES * LANES
+    w_out[:, :, full:] = jnp.zeros(
+        (w_out.shape[0], w_out.shape[1], w_out.shape[2] - full), w_out.dtype
+    )
+    w_out[:, :out_chan, :in_chan] = w_ref[...]
+
+
 def forward_kernel(
-    plan, field_ref, near_ref, far_ref, weight_ref, b_ref, o_ref,
-    f_s, raw_s, x_s, w_s, acc_s, sems,
+    plan, f_s, near_ref, far_ref, w_s, b_ref, o_ref, x_s, acc_s,
 ):
     taps, half, offset = plan.taps, plan.half, plan.offset
     lon_dev, halo = plan.lon_dev, 2 * plan.half
@@ -107,24 +119,7 @@
     points = rows_out * slots
     bulk = lon_dev // ROWS * ROWS
     full = in_chan // LANES * LANES
-    field_copies = []
-    for part in range(2):
-        span = pl.ds(part * (rows_in // 2), rows_in // 2)
-        copy = pltpu.make_async_copy(field_ref.at[span], f_s.at[span], sems.at[taps + part])
-        copy.start()
-        field_copies.append(copy)
-    weight_copies = []
-    for a in range(taps):
-        span = pl.ds(a * taps, taps)
-        copy = pltpu.make_async_copy(weight_ref.at[span], raw_s.at[span], sems.at[a])
-        weight_copies.append(copy)
-    weight_copies[0].start()
     x_s[:, :, full:] = jnp.zeros((rows_in, slots, wide - full), x_s.dtype)
-    w_s[:, :, full:] = jnp.zeros((taps * taps, padded_out, wide - full), w_s.dtype)
-    for copy in field_copies:
-        copy.wait()
-    for copy in weight_copies[1:]:
-        copy.start()
     x_s[:, offset : offset + bulk, :in_chan] = f_s[:, :bulk, :]
     near = near_ref[...].astype(jnp.float32)
     far = far_ref[...].astype(jnp.float32)
@@ -148,9 +143,6 @@
     )
     x_s[:, offset + bulk :, :in_chan] = final.astype(x_s.dtype)
     for a in range(taps):
-        weight_copies[a].wait()
-        mine = slice(a * taps, (a + 1) * taps)
-        w_s[mine, :out_chan, :in_chan] = raw_s[mine]
         part = lax.dot_general(
             w_s[a * taps : (a + 1) * taps].reshape(taps * padded_out, wide),
             x_s[a : a + rows_out].reshape(points, wide),
@@ -600,9 +592,7 @@
         special=special, bias_row=bias_row,
         special_row=special - (pairs - 1) * (half_rows // pairs),
     )
-    own_lon = lax.axis_index("lon")
     factor = 1.0 / math.sqrt(members * rows_out * lon_dev * lon_count)
-    even = own_lon % 2 == 0
 
     def swap_lon(value, d):
         return lax.ppermute(value, "lon", [(i, i ^ d) for i in range(lon_count)])
@@ -618,50 +608,53 @@
     field = jnp.transpose(fields[0], (1, 2, 0))
     packed_rows = main * rows_in + rows_in // pack + 1
     edge = jax.ShapeDtypeStruct((rows_in, halo, in_chan), jnp.bfloat16)
-    near, far, *packed = pl.pallas_call(
+    seen = jnp.transpose(observed, (2, 1, 0))
+    strip = jax.ShapeDtypeStruct((half, rows_out, out_chan), jnp.float32)
+    near, far, seen_near, seen_far, *packed = pl.pallas_call(
         functools.partial(pack_kernel, plan),
-        out_shape=[edge, edge]
+        out_shape=[edge, edge, strip, strip]
         + [jax.ShapeDtypeStruct((packed_rows, lon_dev, LANES), jnp.bfloat16)] * members,
-        in_specs=[vmem()],
-        out_specs=[vmem()] * (members + 2),
+        in_specs=[vmem()] * 2,
+        out_specs=[vmem()] * (members + 4),
         cost_estimate=cost(0, 4_000_000),
         compiler_params=limit(16),
         name="pack",
-    )(field)
+    )(field, seen)
     far = swap_far(far)
     near = swap_lon(near, 1)
     traded = [packed[0]]
     for d in range(1, members):
         traded.append(swap_member(packed[d], d))
 
+    seen_far = swap_far(seen_far)
+    seen_near = swap_lon(seen_near, 1)
+    weight_flat = weight.reshape(total_taps, out_chan, in_chan)
+    w_all = pl.pallas_call(
+        stage_kernel,
+        out_shape=jax.ShapeDtypeStruct((total_taps, padded_out, wide), jnp.bfloat16),
+        in_specs=[vmem()],
+        out_specs=vmem(),
+        cost_estimate=cost(0, 5_000_000),
+        compiler_params=limit(8),
+        name="stage",
+    )(weight_flat)
     own_outputs = pl.pallas_call(
         functools.partial(forward_kernel, plan),
         out_shape=jax.ShapeDtypeStruct((padded_out, points), jnp.bfloat16),
-        in_specs=[any_space, vmem(), vmem(), any_space, vmem()],
+        in_specs=[vmem()] * 5,
         out_specs=vmem(),
         scratch_shapes=[
-            pltpu.VMEM((rows_in, lon_dev, in_chan), jnp.bfloat16),
-            pltpu.VMEM((total_taps, out_chan, in_chan), jnp.bfloat16),
             pltpu.VMEM((rows_in, slots, wide), jnp.bfloat16),
-            pltpu.VMEM((total_taps, padded_out, wide), jnp.bfloat16),
             pltpu.VMEM((stack, points), jnp.float32),
-            pltpu.SemaphoreType.DMA((taps + 2,)),
         ],
         cost_estimate=cost(2 * taps * stack * points * wide, 6_000_000),
-        compiler_params=limit(56),
+        compiler_params=limit(20),
         name="forward",
-    )(field, near, far, weight.reshape(total_taps, out_chan, in_chan), out_bias[None, :])
+    )(field, near, far, w_all, out_bias[None, :])
     outputs = [own_outputs]
     for d in range(1, members):
         outputs.append(swap_member(own_outputs, d))
 
-    seen = jnp.transpose(observed, (2, 1, 0))
-    start_edge = seen[:half]
-    end_edge = seen[lon_dev - half :]
-    strips = (jnp.where(even, start_edge, end_edge), jnp.where(even, end_edge, start_edge))
-    strips, _ = lax.optimization_barrier((strips, own_outputs))
-    far = swap_far(strips[0])
-    near = swap_lon(strips[1], 1)
     tiles = main + 1
     x_all, truth, own_copy = pl.pallas_call(
         functools.partial(prep_kernel, plan),
@@ -676,7 +669,7 @@
         cost_estimate=cost(0, 4_000_000),
         compiler_params=limit(20),
         name="prep",
-    )(seen, near, far, own_outputs, *traded)
+    )(seen, seen_near, seen_far, own_outputs, *traded)
     outputs[0] = own_copy
 
     main_rows = half_rows // pairs

time: 83.7 us -> 81.7 us (0.976)
  Pallas kernels: 23.8 us -> 20.4 us
  local copies, waits for them, and re-layouts: 2.99 us -> 4.66 us
  waiting for transfers between devices: 22.1 us -> 23.6 us
  starting transfers between devices: 32.9 us -> 31.7 us
    pallas_call x1, Pallas kernels: 7.28 us -> 3.59 us  [body(): pl.pallas_call(functools.partial(forward_kernel, plan), out_shape=jax.Sha...]
    ppermute x12, waiting for transfers between devices: 11.2 us -> 13.1 us  [swap_member(): return lax.ppermute(value, 'member', [(i, i ^ d) for i in range(members)])]
    unnamed x15 -> x17, local copies, waits for them, and re-layouts: 2.98 us -> 4.64 us
    ppermute x2, waiting for transfers between devices: 1.63 us -> 0.01 us  [swap_far(): return lax.ppermute(value, 'lon', step)]
    ppermute x2, starting transfers between devices: 6.6 us -> 5.24 us  [swap_far(): return lax.ppermute(value, 'lon', step)]
    ppermute x17, waiting for transfers between devices: 9.24 us -> 10.6 us  [swap_lon(): return lax.ppermute(value, 'lon', [(i, i ^ d) for i in range(lon_count)])]
  transfers between devices with their start and end apart: 31 -> 31, of which waited for: 10 -> 12; matrix products, arithmetic and copies ran while one was open for 1% -> 0% of each run, Pallas kernels for 17% -> 13%
where the time goes in v2:
time: 81.7 us; the launch traced here: 81.4 us
  starting transfers between devices  31.7 us (39%)
  waiting for transfers between devices  23.6 us (29%)
  Pallas kernels  20.4 us (25%)
  local copies, waits for them, and re-layouts  4.66 us (6%)
  between operations  0.98 us (1%)
    ppermute x12, starting transfers between devices, swap_member(): return lax.ppermute(value, 'member', [(i, i ^ d) for i in range(members)])  15.8 us
    ppermute x12, waiting for transfers between devices, swap_member(): return lax.ppermute(value, 'member', [(i, i ^ d) for i in range(members)])  13.1 us
    ppermute x17, starting transfers between devices, swap_lon(): return lax.ppermute(value, 'lon', [(i, i ^ d) for i in range(lon_count)])  10.7 us
    ppermute x17, waiting for transfers between devices, swap_lon(): return lax.ppermute(value, 'lon', [(i, i ^ d) for i in range(lon_count)])  10.6 us
    pallas_call x1, Pallas kernels, body(): pl.pallas_call(functools.partial(gradient_kernel, plan), out_shape=(jax.S...  6.29 us
    pallas_call x3, Pallas kernels, assemble(): pl.pallas_call(kernel, out_shape=[grad_shape, jax.ShapeDtypeStruct(other_...  5.66 us
    ppermute x2, starting transfers between devices, swap_far(): return lax.ppermute(value, 'lon', step)  5.24 us
    unnamed x17, local copies, waits for them, and re-layouts  4.64 us
  transfers between devices with their start and end apart: 31, of which 12 were waited for; matrix products, arithmetic and copies ran while one was open for 0% of the time, Pallas kernels for 13%

profile of v2, /device:TPU:0, one launch (start us, length us, event | category | flops | bytes accessed | tf_op | source)
XLA Modules:
  0.0 81.4 jit_solution(13081304161159124118)
XLA Ops:
  4.3 4.7 %collective-permute-start.3 = (bf16[20,4,641]{2,1,0:T(4,128)(2,1)S(1)}, bf16[20,4,641]{2,1,0:T(4,128)(2,1)S(1)}, u32[]{:S(2)}, u32[]{:S(2)}) collective-permute-start(bf16[20,4,641]{2,1,0:T(4,128)(2,1)S(1)} %get-tuple-element.32), channel_id=1, source_target_pairs={{0,7},{1,2},{2,1},{3,4},{4,3},{5,6},{6,5},{7,0},{8,15},{9,10},{10,... | collective-permute-start | bytes 307688 | tf_op jit(solution)/shard_map/ppermute | solution.py:602
  9.0 1.5 %collective-permute-start.4 = (bf16[26,45,128]{2,1,0:T(8,128)(2,1)S(1)}, bf16[26,45,128]{2,1,0:T(8,128)(2,1)S(1)}, u32[]{:S(2)}, u32[]{:S(2)}) collective-permute-start(bf16[26,45,128]{2,1,0:T(8,128)(2,1)S(1)} %get-tuple-element.34), channel_id=1, source_target_pairs={{0,8},{8,0},{16,24},{24,16},{1,9},{9,1},{17,25},{25,17},{2,10},{10... | collective-permute-start | bytes 898568 | tf_op jit(solution)/shard_map/ppermute | solution.py:605
  10.5 1.5 %collective-permute-start.5 = (bf16[26,45,128]{2,1,0:T(8,128)(2,1)S(1)}, bf16[26,45,128]{2,1,0:T(8,128)(2,1)S(1)}, u32[]{:S(2)}, u32[]{:S(2)}) collective-permute-start(bf16[26,45,128]{2,1,0:T(8,128)(2,1)S(1)} %get-tuple-element.35), channel_id=1, source_target_pairs={{0,16},{8,24},{16,0},{24,8},{1,17},{9,25},{17,1},{25,9},{2,18},{10... | collective-permute-start | bytes 898568 | tf_op jit(solution)/shard_map/ppermute | solution.py:605
  12.5 1.9 %copy-done = bf16[5,5,73,641]{3,2,1,0:T(8,128)(2,1)S(1)} copy-done((bf16[5,5,73,641]{3,2,1,0:T(8,128)(2,1)S(1)}, bf16[5,5,73,641]{3,2,1,0:T(8,128)(2,1)}, u32[]{:S(2)}) %copy-start) | copy-done | bytes 2339674
  15.7 3.6 %forward.1.own_ref = bf16[80,1024]{1,0:T(8,128)(2,1)S(1)} custom-call(bf16[20,45,641]{2,1,0:T(8,128)(2,1)S(1)} %bitcast.17, bf16[20,4,641]{2,1,0:T(4,128)(2,1)S(1)} %collective-permute-done.2.near_ref, bf16[20,4,641]{2,1,0:T(4,128)(2,1)S(1)} %collective-permute-done.3.far_ref, bf16[25,80,768]{2,1,0:T(8,128)(2,1)S(1)} %stage.1.w_s, f32[1,73]{1,0:T(1,128)S(1)} %bitcast.18), custom_call_target="tpu_custom_call" | custom-call | flops 3145728000 | bytes 6000000 | tf_op jit(solution)/shard_map/forward/pallas_call | solution.py:641
  19.4 1.6 %collective-permute-start.7 = (bf16[80,1024]{1,0:T(8,128)(2,1)S(1)}, bf16[80,1024]{1,0:T(8,128)(2,1)S(1)}, u32[]{:S(2)}, u32[]{:S(2)}) collective-permute-start(bf16[80,1024]{1,0:T(8,128)(2,1)S(1)} %forward.1.own_ref), channel_id=1, source_target_pairs={{0,8},{8,0},{16,24},{24,16},{1,9},{9,1},{17,25},{25,17},{2,10},{10... | collective-permute-start | bytes 491528 | tf_op jit(solution)/shard_map/ppermute | solution.py:605
  20.9 1.5 %collective-permute-start.8 = (bf16[80,1024]{1,0:T(8,128)(2,1)S(1)}, bf16[80,1024]{1,0:T(8,128)(2,1)S(1)}, u32[]{:S(2)}, u32[]{:S(2)}) collective-permute-start(bf16[80,1024]{1,0:T(8,128)(2,1)S(1)} %forward.1.own_ref), channel_id=1, source_target_pairs={{0,16},{8,24},{16,0},{24,8},{1,17},{9,25},{17,1},{25,9},{2,18},{10... | collective-permute-start | bytes 491528 | tf_op jit(solution)/shard_map/ppermute | solution.py:605
  23.7 2.4 %collective-permute-done.6.refs_3_ = bf16[26,45,128]{2,1,0:T(8,128)(2,1)S(1)} collective-permute-done((bf16[26,45,128]{2,1,0:T(8,128)(2,1)S(1)}, bf16[26,45,128]{2,1,0:T(8,128)(2,1)S(1)}, u32[]{:S(2)}, u32[]{:S(2)}) %collective-permute-start.6) | collective-permute-done | bytes 299552 | tf_op jit(solution)/shard_map/ppermute | solution.py:605
  27.2 1.5 %collective-permute-done.7.refs_1_ = bf16[80,1024]{1,0:T(8,128)(2,1)S(1)} collective-permute-done((bf16[80,1024]{1,0:T(8,128)(2,1)S(1)}, bf16[80,1024]{1,0:T(8,128)(2,1)S(1)}, u32[]{:S(2)}, u32[]{:S(2)}) %collective-permute-start.7) | collective-permute-done | bytes 163872 | tf_op jit(solution)/shard_map/ppermute | solution.py:605
  28.7 2.9 %collective-permute-done.8.refs_2_ = bf16[80,1024]{1,0:T(8,128)(2,1)S(1)} collective-permute-done((bf16[80,1024]{1,0:T(8,128)(2,1)S(1)}, bf16[80,1024]{1,0:T(8,128)(2,1)S(1)}, u32[]{:S(2)}, u32[]{:S(2)}) %collective-permute-start.8) | collective-permute-done | bytes 163872 | tf_op jit(solution)/shard_map/ppermute | solution.py:605
  31.6 6.3 %gradient.1 = (bf16[80,1024]{1,0:T(8,128)(2,1)S(1)}, f32[1,1024]{1,0:T(1,128)S(1)}, bf16[4,320,128]{2,1,0:T(8,128)(2,1)S(1)}, f32[4,320,128]{2,1,0:T(8,128)S(1)}) custom-call(bf16[80,1024]{1,0:T(8,128)(2,1)S(1)} %get-tuple-element.37.refs_0_, bf16[80,1024]{1,0:T(8,128)(2,1)S(1)} %collective-permute-done.7.refs_1_, ...), custom_call_target="tpu_custom_call" | custom-call | flops 4194304000 | bytes 6000000 | tf_op jit(solution)/shard_map/gradient/pallas_call | solution.py:678
  38.0 1.6 %collective-permute-done.10.got_ref = bf16[4,320,128]{2,1,0:T(8,128)(2,1)S(1)} collective-permute-done((bf16[4,320,128]{2,1,0:T(8,128)(2,1)S(1)}, bf16[4,320,128]{2,1,0:T(8,128)(2,1)S(1)}, u32[]{:S(2)}, u32[]{:S(2)}) %collective-permute-start.10) | collective-permute-done | bytes 327712 | tf_op jit(solution)/shard_map/ppermute | solution.py:598
  39.7 1.6 %collective-permute-start.11 = (bf16[1,320,128]{2,1,0:T(8,128)(2,1)S(1)}, bf16[1,320,128]{2,1,0:T(8,128)(2,1)S(1)}, u32[]{:S(2)}, u32[]{:S(2)}) collective-permute-start(bf16[1,320,128]{2,1,0:T(8,128)(2,1)S(1)} %get-tuple-element.45), channel_id=1, source_target_pairs={{0,2},{1,3},{2,0},{3,1},{4,6},{5,7},{6,4},{7,5},{8,10},{9,11},{10,... | collective-permute-start | bytes 245768 | tf_op jit(solution)/shard_map/ppermute | solution.py:598
  42.6 1.5 %collective-permute-start.13 = (bf16[1,320,128]{2,1,0:T(8,128)(2,1)S(1)}, bf16[1,320,128]{2,1,0:T(8,128)(2,1)S(1)}, u32[]{:S(2)}, u32[]{:S(2)}) collective-permute-start(bf16[1,320,128]{2,1,0:T(8,128)(2,1)S(1)} %get-tuple-element.47), channel_id=1, source_target_pairs={{0,6},{1,7},{2,4},{3,5},{4,2},{5,3},{6,0},{7,1},{8,14},{9,15},{10,... | collective-permute-start | bytes 245768 | tf_op jit(solution)/shard_map/ppermute | solution.py:598
  44.2 6.5 %collective-permute-done.12.refs_1_ = bf16[1,320,128]{2,1,0:T(8,128)(2,1)S(1)} collective-permute-done((bf16[1,320,128]{2,1,0:T(8,128)(2,1)S(1)}, bf16[1,320,128]{2,1,0:T(8,128)(2,1)S(1)}, u32[]{:S(2)}, u32[]{:S(2)}) %collective-permute-start.12) | collective-permute-done | bytes 81952 | tf_op jit(solution)/shard_map/ppermute | solution.py:598
  51.0 1.6 %collective-permute-start.18 = (bf16[1,320,128]{2,1,0:T(8,128)(2,1)S(1)}, bf16[1,320,128]{2,1,0:T(8,128)(2,1)S(1)}, u32[]{:S(2)}, u32[]{:S(2)}) collective-permute-start(bf16[1,320,128]{2,1,0:T(8,128)(2,1)S(1)} %pair_add.1), channel_id=1, source_target_pairs={{0,2},{1,3},{2,0},{3,1},{4,6},{5,7},{6,4},{7,5},{8,10},{9,11},{10,... | collective-permute-start | bytes 245768 | tf_op jit(solution)/shard_map/ppermute | solution.py:598
  53.7 1.7 %collective-permute-start.15 = (bf16[1,320,128]{2,1,0:T(8,128)(2,1)S(1)}, bf16[1,320,128]{2,1,0:T(8,128)(2,1)S(1)}, u32[]{:S(2)}, u32[]{:S(2)}) collective-permute-start(bf16[1,320,128]{2,1,0:T(8,128)(2,1)S(1)} %pair_add.1), channel_id=1, source_target_pairs={{0,6},{1,7},{2,4},{3,5},{4,2},{5,3},{6,0},{7,1},{8,14},{9,15},{10,... | collective-permute-start | bytes 245768 | tf_op jit(solution)/shard_map/ppermute | solution.py:598
  58.5 1.4 %collective-permute-start.24 = (bf16[2,320,128]{2,1,0:T(8,128)(2,1)S(1)}, bf16[2,320,128]{2,1,0:T(8,128)(2,1)S(1)}, u32[]{:S(2)}, u32[]{:S(2)}) collective-permute-start(bf16[2,320,128]{2,1,0:T(8,128)(2,1)S(1)} %pad_maximum_fusion.refs_0_), channel_id=1, source_target_pairs={{0,24},{8,16},{16,8},{24,0},{1,25},{9,17},{17,9},{25,1},{2,26},{10... | collective-permute-start | bytes 491528 | tf_op jit(solution)/shard_map/ppermute | solution.py:605
  63.5 3.1 %collective-permute-start.16 = (bf16[2,320,128]{2,1,0:T(8,128)(2,1)S(1)}, bf16[2,320,128]{2,1,0:T(8,128)(2,1)S(1)}, u32[]{:S(2)}, u32[]{:S(2)}) collective-permute-start(bf16[2,320,128]{2,1,0:T(8,128)(2,1)S(1)} %constant_dynamic-update-slice_fusion.refs_0_), channel_id=1, source_target_pairs={{0,24},{8,16},{16,8},{24,0},{1,25},{9,17},{17,9},{25,1},{2,26},{10... | collective-permute-start | bytes 491528 | tf_op jit(solution)/shard_map/ppermute | solution.py:605
  67.1 1.4 %collective-permute-done.27.refs_2_ = bf16[2,320,128]{2,1,0:T(8,128)(2,1)S(1)} collective-permute-done((bf16[2,320,128]{2,1,0:T(8,128)(2,1)S(1)}, bf16[2,320,128]{2,1,0:T(8,128)(2,1)S(1)}, u32[]{:S(2)}, u32[]{:S(2)}) %collective-permute-start.27) | collective-permute-done | bytes 163872 | tf_op jit(solution)/shard_map/ppermute | solution.py:605
  68.5 2.4 %collective-permute-done.29.refs_4_ = bf16[2,320,128]{2,1,0:T(8,128)(2,1)S(1)} collective-permute-done((bf16[2,320,128]{2,1,0:T(8,128)(2,1)S(1)}, bf16[2,320,128]{2,1,0:T(8,128)(2,1)S(1)}, u32[]{:S(2)}, u32[]{:S(2)}) %collective-permute-start.29) | collective-permute-done | bytes 163872 | tf_op jit(solution)/shard_map/ppermute | solution.py:605
  70.9 1.6 %collective-permute-done.16.refs_0_ = bf16[2,320,128]{2,1,0:T(8,128)(2,1)S(1)} collective-permute-done((bf16[2,320,128]{2,1,0:T(8,128)(2,1)S(1)}, bf16[2,320,128]{2,1,0:T(8,128)(2,1)S(1)}, u32[]{:S(2)}, u32[]{:S(2)}) %collective-permute-start.16) | collective-permute-done | bytes 163872 | tf_op jit(solution)/shard_map/ppermute | solution.py:605
  75.6 2.0 %assemble.3 = (f32[25,73,641]{2,1,0:T(8,128)}, f32[5,64,128]{2,1,0:T(8,128)S(1)}) custom-call(bf16[2,320,128]{2,1,0:T(8,128)(2,1)S(1)} %pad_maximum_fusion.refs_0_, bf16[2,320,128]{2,1,0:T(8,128)(2,1)S(1)} %collective-permute-done.19.refs_1_, bf16[2,320,128]{2,1,0:T(8,128)(2,1)S(1)} %collective-permute-done.20.refs_2_, ...), custom_call_target="tpu_custom_call" | custom-call | bytes 5000000 | tf_op jit(solution)/shard_map/assemble/pallas_call | solution.py:761
  79.0 2.3 %assemble.5 = (f32[25,73,641]{2,1,0:T(8,128)}, f32[1,73]{1,0:T(1,128)}) custom-call(bf16[2,320,128]{2,1,0:T(8,128)(2,1)S(1)} %collective-permute-done.16.refs_0_, bf16[2,320,128]{2,1,0:T(8,128)(2,1)S(1)} %collective-permute-done.17.refs_1_, f32[5,64,128]{2,1,0:T(8,128)S(1)} %get-tuple-element.48.refs_6_.refs_2_, ...), custom_call_target="tpu_custom_call", output_to_operand_aliasing={{0}: (3, {})} | custom-call | bytes 5000000 | tf_op jit(solution)/shard_map/assemble/pallas_call | solution.py:761
  (69 shorter events, 22.2 us)
Async XLA Ops:
  3.8 11.0 %collective-permute-start.2 = (bf16[20,4,641]{2,1,0:T(4,128)(2,1)S(1)}, bf16[20,4,641]{2,1,0:T(4,128)(2,1)S(1)}, u32[]{:S(2)}, u32[]{:S(2)}) collective-permute-start(bf16[20,4,641]{2,1,0:T(4,128)(2,1)S(1)} %get-tuple-element.31), channel_id=1, source_target_pairs={{0,1},{1,0},{2,3},{3,2},{4,5},{5,4},{6,7},{7,6},{8,9},{9,8},{10,11... | collective-permute-start | bytes 307688 | tf_op jit(solution)/shard_map/ppermute | solution.py:598
  4.3 10.5 %collective-permute-start.3 = (bf16[20,4,641]{2,1,0:T(4,128)(2,1)S(1)}, bf16[20,4,641]{2,1,0:T(4,128)(2,1)S(1)}, u32[]{:S(2)}, u32[]{:S(2)}) collective-permute-start(bf16[20,4,641]{2,1,0:T(4,128)(2,1)S(1)} %get-tuple-element.32), channel_id=1, source_target_pairs={{0,7},{1,2},{2,1},{3,4},{4,3},{5,6},{6,5},{7,0},{8,15},{9,10},{10,... | collective-permute-start | bytes 307688 | tf_op jit(solution)/shard_map/ppermute | solution.py:602
  9.0 13.4 %collective-permute-start.4 = (bf16[26,45,128]{2,1,0:T(8,128)(2,1)S(1)}, bf16[26,45,128]{2,1,0:T(8,128)(2,1)S(1)}, u32[]{:S(2)}, u32[]{:S(2)}) collective-permute-start(bf16[26,45,128]{2,1,0:T(8,128)(2,1)S(1)} %get-tuple-element.34), channel_id=1, source_target_pairs={{0,8},{8,0},{16,24},{24,16},{1,9},{9,1},{17,25},{25,17},{2,10},{10... | collective-permute-start | bytes 898568 | tf_op jit(solution)/shard_map/ppermute | solution.py:605
  10.5 13.2 %collective-permute-start.5 = (bf16[26,45,128]{2,1,0:T(8,128)(2,1)S(1)}, bf16[26,45,128]{2,1,0:T(8,128)(2,1)S(1)}, u32[]{:S(2)}, u32[]{:S(2)}) collective-permute-start(bf16[26,45,128]{2,1,0:T(8,128)(2,1)S(1)} %get-tuple-element.35), channel_id=1, source_target_pairs={{0,16},{8,24},{16,0},{24,8},{1,17},{9,25},{17,1},{25,9},{2,18},{10... | collective-permute-start | bytes 898568 | tf_op jit(solution)/shard_map/ppermute | solution.py:605
  12.0 14.1 %collective-permute-start.6 = (bf16[26,45,128]{2,1,0:T(8,128)(2,1)S(1)}, bf16[26,45,128]{2,1,0:T(8,128)(2,1)S(1)}, u32[]{:S(2)}, u32[]{:S(2)}) collective-permute-start(bf16[26,45,128]{2,1,0:T(8,128)(2,1)S(1)} %get-tuple-element.36), channel_id=1, source_target_pairs={{0,24},{8,16},{16,8},{24,0},{1,25},{9,17},{17,9},{25,1},{2,26},{10... | collective-permute-start | bytes 898568 | tf_op jit(solution)/shard_map/ppermute | solution.py:605
  14.8 6.1 %collective-permute-start.1 = (f32[2,16,73]{2,1,0:T(8,128)S(1)}, f32[2,16,73]{2,1,0:T(8,128)S(1)}, u32[]{:S(2)}, u32[]{:S(2)}) collective-permute-start(f32[2,16,73]{2,1,0:T(8,128)S(1)} %get-tuple-element.30), channel_id=1, source_target_pairs={{0,7},{1,2},{2,1},{3,4},{4,3},{5,6},{6,5},{7,0},{8,15},{9,10},{10,... | collective-permute-start | bytes 28040 | tf_op jit(solution)/shard_map/ppermute | solution.py:602
  19.4 9.3 %collective-permute-start.7 = (bf16[80,1024]{1,0:T(8,128)(2,1)S(1)}, bf16[80,1024]{1,0:T(8,128)(2,1)S(1)}, u32[]{:S(2)}, u32[]{:S(2)}) collective-permute-start(bf16[80,1024]{1,0:T(8,128)(2,1)S(1)} %forward.1.own_ref), channel_id=1, source_target_pairs={{0,8},{8,0},{16,24},{24,16},{1,9},{9,1},{17,25},{25,17},{2,10},{10... | collective-permute-start | bytes 491528 | tf_op jit(solution)/shard_map/ppermute | solution.py:605
  20.9 10.7 %collective-permute-start.8 = (bf16[80,1024]{1,0:T(8,128)(2,1)S(1)}, bf16[80,1024]{1,0:T(8,128)(2,1)S(1)}, u32[]{:S(2)}, u32[]{:S(2)}) collective-permute-start(bf16[80,1024]{1,0:T(8,128)(2,1)S(1)} %forward.1.own_ref), channel_id=1, source_target_pairs={{0,16},{8,24},{16,0},{24,8},{1,17},{9,25},{17,1},{25,9},{2,18},{10... | collective-permute-start | bytes 491528 | tf_op jit(solution)/shard_map/ppermute | solution.py:605
  22.4 9.1 %collective-permute-start.9 = (bf16[80,1024]{1,0:T(8,128)(2,1)S(1)}, bf16[80,1024]{1,0:T(8,128)(2,1)S(1)}, u32[]{:S(2)}, u32[]{:S(2)}) collective-permute-start(bf16[80,1024]{1,0:T(8,128)(2,1)S(1)} %forward.1.own_ref), channel_id=1, source_target_pairs={{0,24},{8,16},{16,8},{24,0},{1,25},{9,17},{17,9},{25,1},{2,26},{10... | collective-permute-start | bytes 491528 | tf_op jit(solution)/shard_map/ppermute | solution.py:605
  41.3 9.5 %collective-permute-start.12 = (bf16[1,320,128]{2,1,0:T(8,128)(2,1)S(1)}, bf16[1,320,128]{2,1,0:T(8,128)(2,1)S(1)}, u32[]{:S(2)}, u32[]{:S(2)}) collective-permute-start(bf16[1,320,128]{2,1,0:T(8,128)(2,1)S(1)} %get-tuple-element.46), channel_id=1, source_target_pairs={{0,4},{1,5},{2,6},{3,7},{4,0},{5,1},{6,2},{7,3},{8,12},{9,13},{10,... | collective-permute-start | bytes 245768 | tf_op jit(solution)/shard_map/ppermute | solution.py:598
  42.6 8.1 %collective-permute-start.13 = (bf16[1,320,128]{2,1,0:T(8,128)(2,1)S(1)}, bf16[1,320,128]{2,1,0:T(8,128)(2,1)S(1)}, u32[]{:S(2)}, u32[]{:S(2)}) collective-permute-start(bf16[1,320,128]{2,1,0:T(8,128)(2,1)S(1)} %get-tuple-element.47), channel_id=1, source_target_pairs={{0,6},{1,7},{2,4},{3,5},{4,2},{5,3},{6,0},{7,1},{8,14},{9,15},{10,... | collective-permute-start | bytes 245768 | tf_op jit(solution)/shard_map/ppermute | solution.py:598
  51.0 5.4 %collective-permute-start.18 = (bf16[1,320,128]{2,1,0:T(8,128)(2,1)S(1)}, bf16[1,320,128]{2,1,0:T(8,128)(2,1)S(1)}, u32[]{:S(2)}, u32[]{:S(2)}) collective-permute-start(bf16[1,320,128]{2,1,0:T(8,128)(2,1)S(1)} %pair_add.1), channel_id=1, source_target_pairs={{0,2},{1,3},{2,0},{3,1},{4,6},{5,7},{6,4},{7,5},{8,10},{9,11},{10,... | collective-permute-start | bytes 245768 | tf_op jit(solution)/shard_map/ppermute | solution.py:598
  52.6 8.7 %collective-permute-start.14 = (bf16[1,320,128]{2,1,0:T(8,128)(2,1)S(1)}, bf16[1,320,128]{2,1,0:T(8,128)(2,1)S(1)}, u32[]{:S(2)}, u32[]{:S(2)}) collective-permute-start(bf16[1,320,128]{2,1,0:T(8,128)(2,1)S(1)} %pair_add.1), channel_id=1, source_target_pairs={{0,4},{1,5},{2,6},{3,7},{4,0},{5,1},{6,2},{7,3},{8,12},{9,13},{10,... | collective-permute-start | bytes 245768 | tf_op jit(solution)/shard_map/ppermute | solution.py:598
  53.7 7.6 %collective-permute-start.15 = (bf16[1,320,128]{2,1,0:T(8,128)(2,1)S(1)}, bf16[1,320,128]{2,1,0:T(8,128)(2,1)S(1)}, u32[]{:S(2)}, u32[]{:S(2)}) collective-permute-start(bf16[1,320,128]{2,1,0:T(8,128)(2,1)S(1)} %pair_add.1), channel_id=1, source_target_pairs={{0,6},{1,7},{2,4},{3,5},{4,2},{5,3},{6,0},{7,1},{8,14},{9,15},{10,... | collective-permute-start | bytes 245768 | tf_op jit(solution)/shard_map/ppermute | solution.py:598
  56.4 5.8 %collective-permute-start.20 = (bf16[2,320,128]{2,1,0:T(8,128)(2,1)S(1)}, bf16[2,320,128]{2,1,0:T(8,128)(2,1)S(1)}, u32[]{:S(2)}, u32[]{:S(2)}) collective-permute-start(bf16[2,320,128]{2,1,0:T(8,128)(2,1)S(1)} %pad_maximum_fusion.refs_0_), channel_id=1, source_target_pairs={{0,8},{8,0},{16,24},{24,16},{1,9},{9,1},{17,25},{25,17},{2,10},{10... | collective-permute-start | bytes 491528 | tf_op jit(solution)/shard_map/ppermute | solution.py:605
  57.3 6.2 %collective-permute-start.22 = (bf16[2,320,128]{2,1,0:T(8,128)(2,1)S(1)}, bf16[2,320,128]{2,1,0:T(8,128)(2,1)S(1)}, u32[]{:S(2)}, u32[]{:S(2)}) collective-permute-start(bf16[2,320,128]{2,1,0:T(8,128)(2,1)S(1)} %pad_maximum_fusion.refs_0_), channel_id=1, source_target_pairs={{0,16},{8,24},{16,0},{24,8},{1,17},{9,25},{17,1},{25,9},{2,18},{10... | collective-permute-start | bytes 491528 | tf_op jit(solution)/shard_map/ppermute | solution.py:605
  58.5 8.0 %collective-permute-start.24 = (bf16[2,320,128]{2,1,0:T(8,128)(2,1)S(1)}, bf16[2,320,128]{2,1,0:T(8,128)(2,1)S(1)}, u32[]{:S(2)}, u32[]{:S(2)}) collective-permute-start(bf16[2,320,128]{2,1,0:T(8,128)(2,1)S(1)} %pad_maximum_fusion.refs_0_), channel_id=1, source_target_pairs={{0,24},{8,16},{16,8},{24,0},{1,25},{9,17},{17,9},{25,1},{2,26},{10... | collective-permute-start | bytes 491528 | tf_op jit(solution)/shard_map/ppermute | solution.py:605
  61.4 7.1 %collective-permute-start.27 = (bf16[2,320,128]{2,1,0:T(8,128)(2,1)S(1)}, bf16[2,320,128]{2,1,0:T(8,128)(2,1)S(1)}, u32[]{:S(2)}, u32[]{:S(2)}) collective-permute-start(bf16[2,320,128]{2,1,0:T(8,128)(2,1)S(1)} %constant_dynamic-update-slice_fusion.refs_0_), channel_id=1, source_target_pairs={{0,8},{8,0},{16,24},{24,16},{1,9},{9,1},{17,25},{25,17},{2,10},{10... | collective-permute-start | bytes 491528 | tf_op jit(solution)/shard_map/ppermute | solution.py:605
  62.3 8.6 %collective-permute-start.29 = (bf16[2,320,128]{2,1,0:T(8,128)(2,1)S(1)}, bf16[2,320,128]{2,1,0:T(8,128)(2,1)S(1)}, u32[]{:S(2)}, u32[]{:S(2)}) collective-permute-start(bf16[2,320,128]{2,1,0:T(8,128)(2,1)S(1)} %constant_dynamic-update-slice_fusion.refs_0_), channel_id=1, source_target_pairs={{0,16},{8,24},{16,0},{24,8},{1,17},{9,25},{17,1},{25,9},{2,18},{10... | collective-permute-start | bytes 491528 | tf_op jit(solution)/shard_map/ppermute | solution.py:605
  63.5 9.0 %collective-permute-start.16 = (bf16[2,320,128]{2,1,0:T(8,128)(2,1)S(1)}, bf16[2,320,128]{2,1,0:T(8,128)(2,1)S(1)}, u32[]{:S(2)}, u32[]{:S(2)}) collective-permute-start(bf16[2,320,128]{2,1,0:T(8,128)(2,1)S(1)} %constant_dynamic-update-slice_fusion.refs_0_), channel_id=1, source_target_pairs={{0,24},{8,16},{16,8},{24,0},{1,25},{9,17},{17,9},{25,1},{2,26},{10... | collective-permute-start | bytes 491528 | tf_op jit(solution)/shard_map/ppermute | solution.py:605
  66.6 5.9 %collective-permute-start.21 = (bf16[2,320,128]{2,1,0:T(8,128)(2,1)S(1)}, bf16[2,320,128]{2,1,0:T(8,128)(2,1)S(1)}, u32[]{:S(2)}, u32[]{:S(2)}) collective-permute-start(bf16[2,320,128]{2,1,0:T(8,128)(2,1)S(1)} %collective-permute-done.20.refs_2_), channel_id=1, source_target_pairs={{0,1},{1,0},{2,3},{3,2},{4,5},{5,4},{6,7},{7,6},{8,9},{9,8},{10,11... | collective-permute-start | bytes 491528 | tf_op jit(solution)/shard_map/ppermute | solution.py:598
  66.6 6.4 %collective-permute-start.23 = (bf16[2,320,128]{2,1,0:T(8,128)(2,1)S(1)}, bf16[2,320,128]{2,1,0:T(8,128)(2,1)S(1)}, u32[]{:S(2)}, u32[]{:S(2)}) collective-permute-start(bf16[2,320,128]{2,1,0:T(8,128)(2,1)S(1)} %collective-permute-done.22.refs_4_), channel_id=1, source_target_pairs={{0,1},{1,0},{2,3},{3,2},{4,5},{5,4},{6,7},{7,6},{8,9},{9,8},{10,11... | collective-permute-start | bytes 491528 | tf_op jit(solution)/shard_map/ppermute | solution.py:598
  68.5 9.1 %collective-permute-start.26 = (bf16[2,320,128]{2,1,0:T(8,128)(2,1)S(1)}, bf16[2,320,128]{2,1,0:T(8,128)(2,1)S(1)}, u32[]{:S(2)}, u32[]{:S(2)}) collective-permute-start(bf16[2,320,128]{2,1,0:T(8,128)(2,1)S(1)} %constant_dynamic-update-slice_fusion.refs_0_), channel_id=1, source_target_pairs={{0,1},{1,0},{2,3},{3,2},{4,5},{5,4},{6,7},{7,6},{8,9},{9,8},{10,11... | collective-permute-start | bytes 491528 | tf_op jit(solution)/shard_map/ppermute | solution.py:598
  73.0 6.0 %collective-permute-start.17 = (bf16[2,320,128]{2,1,0:T(8,128)(2,1)S(1)}, bf16[2,320,128]{2,1,0:T(8,128)(2,1)S(1)}, u32[]{:S(2)}, u32[]{:S(2)}) collective-permute-start(bf16[2,320,128]{2,1,0:T(8,128)(2,1)S(1)} %collective-permute-done.16.refs_0_), channel_id=1, source_target_pairs={{0,1},{1,0},{2,3},{3,2},{4,5},{5,4},{6,7},{7,6},{8,9},{9,8},{10,11... | collective-permute-start | bytes 491528 | tf_op jit(solution)/shard_map/ppermute | solution.py:598
  (15 other events, 106.9 us)

commit v3 on v2

--- a/solution.py
+++ b/solution.py
@@ -53,7 +53,16 @@
     return jnp.transpose(jnp.broadcast_to(row, (LANES, LANES)))[:, :1]
 
 
-def pack_kernel(plan, f_ref, seen_ref, near_ref, far_ref, seen_near_ref, seen_far_ref, *out_refs):
+def strips_kernel(seen_ref, near_ref, far_ref):
+    even = here()[2] == 0
+    width = near_ref.shape[0]
+    start = seen_ref[:width]
+    end = seen_ref[seen_ref.shape[0] - width :]
+    far_ref[...] = jnp.where(even, start, end)
+    near_ref[...] = jnp.where(even, end, start)
+
+
+def pack_kernel(plan, f_ref, near_ref, far_ref, *out_refs):
     members, main, rest = plan.members, plan.main, plan.rest
     pack, valid, sub = plan.pack, plan.valid, plan.sub
     rows_in, lon_dev, in_chan = f_ref.shape
@@ -65,10 +74,6 @@
     end_edge = f_ref[:, final:, :].astype(jnp.float32)[:, lon_dev - halo - final :]
     far_ref[...] = jnp.where(even, start_edge, end_edge).astype(far_ref.dtype)
     near_ref[...] = jnp.where(even, end_edge, start_edge).astype(near_ref.dtype)
-    start_seen = seen_ref[: plan.half]
-    end_seen = seen_ref[lon_dev - plan.half :]
-    seen_far_ref[...] = jnp.where(even, start_seen, end_seen)
-    seen_near_ref[...] = jnp.where(even, end_seen, start_seen)
     group = rows_in // pack
     base = main * members
     lane = lax.broadcasted_iota(jnp.int32, (1, 1, LANES), 2)
@@ -610,22 +615,31 @@
     edge = jax.ShapeDtypeStruct((rows_in, halo, in_chan), jnp.bfloat16)
     seen = jnp.transpose(observed, (2, 1, 0))
     strip = jax.ShapeDtypeStruct((half, rows_out, out_chan), jnp.float32)
-    near, far, seen_near, seen_far, *packed = pl.pallas_call(
+    near, far, *packed = pl.pallas_call(
         functools.partial(pack_kernel, plan),
-        out_shape=[edge, edge, strip, strip]
+        out_shape=[edge, edge]
         + [jax.ShapeDtypeStruct((packed_rows, lon_dev, LANES), jnp.bfloat16)] * members,
-        in_specs=[vmem()] * 2,
-        out_specs=[vmem()] * (members + 4),
+        in_specs=[vmem()],
+        out_specs=[vmem()] * (members + 2),
         cost_estimate=cost(0, 4_000_000),
         compiler_params=limit(16),
         name="pack",
-    )(field, seen)
+    )(field)
     far = swap_far(far)
     near = swap_lon(near, 1)
     traded = [packed[0]]
     for d in range(1, members):
         traded.append(swap_member(packed[d], d))
 
+    seen_near, seen_far = pl.pallas_call(
+        strips_kernel,
+        out_shape=[strip, strip],
+        in_specs=[vmem()],
+        out_specs=[vmem()] * 2,
+        cost_estimate=cost(0, 400_000),
+        compiler_params=limit(4),
+        name="strips",
+    )(seen)
     seen_far = swap_far(seen_far)
     seen_near = swap_lon(seen_near, 1)
     weight_flat = weight.reshape(total_taps, out_chan, in_chan)

time: 81.7 us -> 80.6 us (0.987)
    unnamed x17 -> x15, local copies, waits for them, and re-layouts: 4.64 us -> 3.91 us
where the time goes in v3:
time: 80.6 us; the launch traced here: 80.4 us
  starting transfers between devices  32 us (40%)
  waiting for transfers between devices  23.1 us (29%)
  Pallas kernels  20.4 us (25%)
  local copies, waits for them, and re-layouts  3.93 us (5%)
  between operations  0.98 us (1%)
    ppermute x12, starting transfers between devices, swap_member(): return lax.ppermute(value, 'member', [(i, i ^ d) for i in range(members)])  16.1 us
    ppermute x12, waiting for transfers between devices, swap_member(): return lax.ppermute(value, 'member', [(i, i ^ d) for i in range(members)])  12.5 us
    ppermute x17, starting transfers between devices, swap_lon(): return lax.ppermute(value, 'lon', [(i, i ^ d) for i in range(lon_count)])  10.7 us
    ppermute x17, waiting for transfers between devices, swap_lon(): return lax.ppermute(value, 'lon', [(i, i ^ d) for i in range(lon_count)])  10.6 us
    pallas_call x1, Pallas kernels, body(): pl.pallas_call(functools.partial(gradient_kernel, plan), out_shape=(jax.S...  6.29 us
    pallas_call x3, Pallas kernels, assemble(): pl.pallas_call(kernel, out_shape=[grad_shape, jax.ShapeDtypeStruct(other_...  5.66 us
    ppermute x2, starting transfers between devices, swap_far(): return lax.ppermute(value, 'lon', step)  5.24 us
    unnamed x15, local copies, waits for them, and re-layouts  3.91 us
  transfers between devices with their start and end apart: 31, of which 12 were waited for; matrix products, arithmetic and copies ran while one was open for 0% of the time, Pallas kernels for 13%

profile of v3, /device:TPU:0, one launch (start us, length us, event | category | flops | bytes accessed | tf_op | source)
XLA Modules:
  0.0 80.4 jit_solution(14275772634007037475)
XLA Ops:
  3.3 4.7 %collective-permute-start.3 = (bf16[20,4,641]{2,1,0:T(4,128)(2,1)S(1)}, bf16[20,4,641]{2,1,0:T(4,128)(2,1)S(1)}, u32[]{:S(2)}, u32[]{:S(2)}) collective-permute-start(bf16[20,4,641]{2,1,0:T(4,128)(2,1)S(1)} %get-tuple-element.32), channel_id=1, source_target_pairs={{0,7},{1,2},{2,1},{3,4},{4,3},{5,6},{6,5},{7,0},{8,15},{9,10},{10,... | collective-permute-start | bytes 307688 | tf_op jit(solution)/shard_map/ppermute | solution.py:607
  8.0 1.5 %collective-permute-start.4 = (bf16[26,45,128]{2,1,0:T(8,128)(2,1)S(1)}, bf16[26,45,128]{2,1,0:T(8,128)(2,1)S(1)}, u32[]{:S(2)}, u32[]{:S(2)}) collective-permute-start(bf16[26,45,128]{2,1,0:T(8,128)(2,1)S(1)} %get-tuple-element.34), channel_id=1, source_target_pairs={{0,8},{8,0},{16,24},{24,16},{1,9},{9,1},{17,25},{25,17},{2,10},{10... | collective-permute-start | bytes 898568 | tf_op jit(solution)/shard_map/ppermute | solution.py:610
  9.5 1.5 %collective-permute-start.5 = (bf16[26,45,128]{2,1,0:T(8,128)(2,1)S(1)}, bf16[26,45,128]{2,1,0:T(8,128)(2,1)S(1)}, u32[]{:S(2)}, u32[]{:S(2)}) collective-permute-start(bf16[26,45,128]{2,1,0:T(8,128)(2,1)S(1)} %get-tuple-element.35), channel_id=1, source_target_pairs={{0,16},{8,24},{16,0},{24,8},{1,17},{9,25},{17,1},{25,9},{2,18},{10... | collective-permute-start | bytes 898568 | tf_op jit(solution)/shard_map/ppermute | solution.py:610
  11.5 1.9 %copy-done = bf16[5,5,73,641]{3,2,1,0:T(8,128)(2,1)S(1)} copy-done((bf16[5,5,73,641]{3,2,1,0:T(8,128)(2,1)S(1)}, bf16[5,5,73,641]{3,2,1,0:T(8,128)(2,1)}, u32[]{:S(2)}) %copy-start) | copy-done | bytes 2339674
  15.0 3.6 %forward.1.own_ref = bf16[80,1024]{1,0:T(8,128)(2,1)S(1)} custom-call(bf16[20,45,641]{2,1,0:T(8,128)(2,1)S(1)} %bitcast.17, bf16[20,4,641]{2,1,0:T(4,128)(2,1)S(1)} %collective-permute-done.2.near_ref, bf16[20,4,641]{2,1,0:T(4,128)(2,1)S(1)} %collective-permute-done.3.far_ref, bf16[25,80,768]{2,1,0:T(8,128)(2,1)S(1)} %stage.1.w_s, f32[1,73]{1,0:T(1,128)S(1)} %bitcast.18), custom_call_target="tpu_custom_call" | custom-call | flops 3145728000 | bytes 6000000 | tf_op jit(solution)/shard_map/forward/pallas_call | solution.py:655
  18.6 1.6 %collective-permute-start.7 = (bf16[80,1024]{1,0:T(8,128)(2,1)S(1)}, bf16[80,1024]{1,0:T(8,128)(2,1)S(1)}, u32[]{:S(2)}, u32[]{:S(2)}) collective-permute-start(bf16[80,1024]{1,0:T(8,128)(2,1)S(1)} %forward.1.own_ref), channel_id=1, source_target_pairs={{0,8},{8,0},{16,24},{24,16},{1,9},{9,1},{17,25},{25,17},{2,10},{10... | collective-permute-start | bytes 491528 | tf_op jit(solution)/shard_map/ppermute | solution.py:610
  20.2 1.5 %collective-permute-start.8 = (bf16[80,1024]{1,0:T(8,128)(2,1)S(1)}, bf16[80,1024]{1,0:T(8,128)(2,1)S(1)}, u32[]{:S(2)}, u32[]{:S(2)}) collective-permute-start(bf16[80,1024]{1,0:T(8,128)(2,1)S(1)} %forward.1.own_ref), channel_id=1, source_target_pairs={{0,16},{8,24},{16,0},{24,8},{1,17},{9,25},{17,1},{25,9},{2,18},{10... | collective-permute-start | bytes 491528 | tf_op jit(solution)/shard_map/ppermute | solution.py:610
  23.1 1.4 %collective-permute-done.6.refs_3_ = bf16[26,45,128]{2,1,0:T(8,128)(2,1)S(1)} collective-permute-done((bf16[26,45,128]{2,1,0:T(8,128)(2,1)S(1)}, bf16[26,45,128]{2,1,0:T(8,128)(2,1)S(1)}, u32[]{:S(2)}, u32[]{:S(2)}) %collective-permute-start.6) | collective-permute-done | bytes 299552 | tf_op jit(solution)/shard_map/ppermute | solution.py:610
  25.5 1.5 %collective-permute-done.7.refs_1_ = bf16[80,1024]{1,0:T(8,128)(2,1)S(1)} collective-permute-done((bf16[80,1024]{1,0:T(8,128)(2,1)S(1)}, bf16[80,1024]{1,0:T(8,128)(2,1)S(1)}, u32[]{:S(2)}, u32[]{:S(2)}) %collective-permute-start.7) | collective-permute-done | bytes 163872 | tf_op jit(solution)/shard_map/ppermute | solution.py:610
  27.1 3.5 %collective-permute-done.8.refs_2_ = bf16[80,1024]{1,0:T(8,128)(2,1)S(1)} collective-permute-done((bf16[80,1024]{1,0:T(8,128)(2,1)S(1)}, bf16[80,1024]{1,0:T(8,128)(2,1)S(1)}, u32[]{:S(2)}, u32[]{:S(2)}) %collective-permute-start.8) | collective-permute-done | bytes 163872 | tf_op jit(solution)/shard_map/ppermute | solution.py:610
  30.6 6.3 %gradient.1 = (bf16[80,1024]{1,0:T(8,128)(2,1)S(1)}, f32[1,1024]{1,0:T(1,128)S(1)}, bf16[4,320,128]{2,1,0:T(8,128)(2,1)S(1)}, f32[4,320,128]{2,1,0:T(8,128)S(1)}) custom-call(bf16[80,1024]{1,0:T(8,128)(2,1)S(1)} %get-tuple-element.37.refs_0_, bf16[80,1024]{1,0:T(8,128)(2,1)S(1)} %collective-permute-done.7.refs_1_, ...), custom_call_target="tpu_custom_call" | custom-call | flops 4194304000 | bytes 6000000 | tf_op jit(solution)/shard_map/gradient/pallas_call | solution.py:692
  37.0 1.6 %collective-permute-done.10.got_ref = bf16[4,320,128]{2,1,0:T(8,128)(2,1)S(1)} collective-permute-done((bf16[4,320,128]{2,1,0:T(8,128)(2,1)S(1)}, bf16[4,320,128]{2,1,0:T(8,128)(2,1)S(1)}, u32[]{:S(2)}, u32[]{:S(2)}) %collective-permute-start.10) | collective-permute-done | bytes 327712 | tf_op jit(solution)/shard_map/ppermute | solution.py:603
  38.7 1.6 %collective-permute-start.11 = (bf16[1,320,128]{2,1,0:T(8,128)(2,1)S(1)}, bf16[1,320,128]{2,1,0:T(8,128)(2,1)S(1)}, u32[]{:S(2)}, u32[]{:S(2)}) collective-permute-start(bf16[1,320,128]{2,1,0:T(8,128)(2,1)S(1)} %get-tuple-element.45), channel_id=1, source_target_pairs={{0,2},{1,3},{2,0},{3,1},{4,6},{5,7},{6,4},{7,5},{8,10},{9,11},{10,... | collective-permute-start | bytes 245768 | tf_op jit(solution)/shard_map/ppermute | solution.py:603
  41.6 1.5 %collective-permute-start.13 = (bf16[1,320,128]{2,1,0:T(8,128)(2,1)S(1)}, bf16[1,320,128]{2,1,0:T(8,128)(2,1)S(1)}, u32[]{:S(2)}, u32[]{:S(2)}) collective-permute-start(bf16[1,320,128]{2,1,0:T(8,128)(2,1)S(1)} %get-tuple-element.47), channel_id=1, source_target_pairs={{0,6},{1,7},{2,4},{3,5},{4,2},{5,3},{6,0},{7,1},{8,14},{9,15},{10,... | collective-permute-start | bytes 245768 | tf_op jit(solution)/shard_map/ppermute | solution.py:603
  43.2 6.5 %collective-permute-done.12.refs_1_ = bf16[1,320,128]{2,1,0:T(8,128)(2,1)S(1)} collective-permute-done((bf16[1,320,128]{2,1,0:T(8,128)(2,1)S(1)}, bf16[1,320,128]{2,1,0:T(8,128)(2,1)S(1)}, u32[]{:S(2)}, u32[]{:S(2)}) %collective-permute-start.12) | collective-permute-done | bytes 81952 | tf_op jit(solution)/shard_map/ppermute | solution.py:603
  50.0 1.6 %collective-permute-start.18 = (bf16[1,320,128]{2,1,0:T(8,128)(2,1)S(1)}, bf16[1,320,128]{2,1,0:T(8,128)(2,1)S(1)}, u32[]{:S(2)}, u32[]{:S(2)}) collective-permute-start(bf16[1,320,128]{2,1,0:T(8,128)(2,1)S(1)} %pair_add.1), channel_id=1, source_target_pairs={{0,2},{1,3},{2,0},{3,1},{4,6},{5,7},{6,4},{7,5},{8,10},{9,11},{10,... | collective-permute-start | bytes 245768 | tf_op jit(solution)/shard_map/ppermute | solution.py:603
  52.7 1.7 %collective-permute-start.15 = (bf16[1,320,128]{2,1,0:T(8,128)(2,1)S(1)}, bf16[1,320,128]{2,1,0:T(8,128)(2,1)S(1)}, u32[]{:S(2)}, u32[]{:S(2)}) collective-permute-start(bf16[1,320,128]{2,1,0:T(8,128)(2,1)S(1)} %pair_add.1), channel_id=1, source_target_pairs={{0,6},{1,7},{2,4},{3,5},{4,2},{5,3},{6,0},{7,1},{8,14},{9,15},{10,... | collective-permute-start | bytes 245768 | tf_op jit(solution)/shard_map/ppermute | solution.py:603
  57.6 1.4 %collective-permute-start.24 = (bf16[2,320,128]{2,1,0:T(8,128)(2,1)S(1)}, bf16[2,320,128]{2,1,0:T(8,128)(2,1)S(1)}, u32[]{:S(2)}, u32[]{:S(2)}) collective-permute-start(bf16[2,320,128]{2,1,0:T(8,128)(2,1)S(1)} %pad_maximum_fusion.refs_0_), channel_id=1, source_target_pairs={{0,24},{8,16},{16,8},{24,0},{1,25},{9,17},{17,9},{25,1},{2,26},{10... | collective-permute-start | bytes 491528 | tf_op jit(solution)/shard_map/ppermute | solution.py:610
  62.5 3.1 %collective-permute-start.16 = (bf16[2,320,128]{2,1,0:T(8,128)(2,1)S(1)}, bf16[2,320,128]{2,1,0:T(8,128)(2,1)S(1)}, u32[]{:S(2)}, u32[]{:S(2)}) collective-permute-start(bf16[2,320,128]{2,1,0:T(8,128)(2,1)S(1)} %constant_dynamic-update-slice_fusion.refs_0_), channel_id=1, source_target_pairs={{0,24},{8,16},{16,8},{24,0},{1,25},{9,17},{17,9},{25,1},{2,26},{10... | collective-permute-start | bytes 491528 | tf_op jit(solution)/shard_map/ppermute | solution.py:610
  66.1 1.4 %collective-permute-done.27.refs_2_ = bf16[2,320,128]{2,1,0:T(8,128)(2,1)S(1)} collective-permute-done((bf16[2,320,128]{2,1,0:T(8,128)(2,1)S(1)}, bf16[2,320,128]{2,1,0:T(8,128)(2,1)S(1)}, u32[]{:S(2)}, u32[]{:S(2)}) %collective-permute-start.27) | collective-permute-done | bytes 163872 | tf_op jit(solution)/shard_map/ppermute | solution.py:610
  67.5 2.4 %collective-permute-done.29.refs_4_ = bf16[2,320,128]{2,1,0:T(8,128)(2,1)S(1)} collective-permute-done((bf16[2,320,128]{2,1,0:T(8,128)(2,1)S(1)}, bf16[2,320,128]{2,1,0:T(8,128)(2,1)S(1)}, u32[]{:S(2)}, u32[]{:S(2)}) %collective-permute-start.29) | collective-permute-done | bytes 163872 | tf_op jit(solution)/shard_map/ppermute | solution.py:610
  69.9 1.6 %collective-permute-done.16.refs_0_ = bf16[2,320,128]{2,1,0:T(8,128)(2,1)S(1)} collective-permute-done((bf16[2,320,128]{2,1,0:T(8,128)(2,1)S(1)}, bf16[2,320,128]{2,1,0:T(8,128)(2,1)S(1)}, u32[]{:S(2)}, u32[]{:S(2)}) %collective-permute-start.16) | collective-permute-done | bytes 163872 | tf_op jit(solution)/shard_map/ppermute | solution.py:610
  74.6 2.0 %assemble.3 = (f32[25,73,641]{2,1,0:T(8,128)}, f32[5,64,128]{2,1,0:T(8,128)S(1)}) custom-call(bf16[2,320,128]{2,1,0:T(8,128)(2,1)S(1)} %pad_maximum_fusion.refs_0_, bf16[2,320,128]{2,1,0:T(8,128)(2,1)S(1)} %collective-permute-done.19.refs_1_, bf16[2,320,128]{2,1,0:T(8,128)(2,1)S(1)} %collective-permute-done.20.refs_2_, ...), custom_call_target="tpu_custom_call" | custom-call | bytes 5000000 | tf_op jit(solution)/shard_map/assemble/pallas_call | solution.py:775
  78.0 2.3 %assemble.5 = (f32[25,73,641]{2,1,0:T(8,128)}, f32[1,73]{1,0:T(1,128)}) custom-call(bf16[2,320,128]{2,1,0:T(8,128)(2,1)S(1)} %collective-permute-done.16.refs_0_, bf16[2,320,128]{2,1,0:T(8,128)(2,1)S(1)} %collective-permute-done.17.refs_1_, f32[5,64,128]{2,1,0:T(8,128)S(1)} %get-tuple-element.48.refs_6_.refs_2_, ...), custom_call_target="tpu_custom_call", output_to_operand_aliasing={{0}: (3, {})} | custom-call | bytes 5000000 | tf_op jit(solution)/shard_map/assemble/pallas_call | solution.py:775
  (68 shorter events, 21.5 us)
Async XLA Ops:
  2.8 11.6 %collective-permute-start.2 = (bf16[20,4,641]{2,1,0:T(4,128)(2,1)S(1)}, bf16[20,4,641]{2,1,0:T(4,128)(2,1)S(1)}, u32[]{:S(2)}, u32[]{:S(2)}) collective-permute-start(bf16[20,4,641]{2,1,0:T(4,128)(2,1)S(1)} %get-tuple-element.31), channel_id=1, source_target_pairs={{0,1},{1,0},{2,3},{3,2},{4,5},{5,4},{6,7},{7,6},{8,9},{9,8},{10,11... | collective-permute-start | bytes 307688 | tf_op jit(solution)/shard_map/ppermute | solution.py:603
  3.3 11.1 %collective-permute-start.3 = (bf16[20,4,641]{2,1,0:T(4,128)(2,1)S(1)}, bf16[20,4,641]{2,1,0:T(4,128)(2,1)S(1)}, u32[]{:S(2)}, u32[]{:S(2)}) collective-permute-start(bf16[20,4,641]{2,1,0:T(4,128)(2,1)S(1)} %get-tuple-element.32), channel_id=1, source_target_pairs={{0,7},{1,2},{2,1},{3,4},{4,3},{5,6},{6,5},{7,0},{8,15},{9,10},{10,... | collective-permute-start | bytes 307688 | tf_op jit(solution)/shard_map/ppermute | solution.py:607
  8.0 13.7 %collective-permute-start.4 = (bf16[26,45,128]{2,1,0:T(8,128)(2,1)S(1)}, bf16[26,45,128]{2,1,0:T(8,128)(2,1)S(1)}, u32[]{:S(2)}, u32[]{:S(2)}) collective-permute-start(bf16[26,45,128]{2,1,0:T(8,128)(2,1)S(1)} %get-tuple-element.34), channel_id=1, source_target_pairs={{0,8},{8,0},{16,24},{24,16},{1,9},{9,1},{17,25},{25,17},{2,10},{10... | collective-permute-start | bytes 898568 | tf_op jit(solution)/shard_map/ppermute | solution.py:610
  9.5 13.5 %collective-permute-start.5 = (bf16[26,45,128]{2,1,0:T(8,128)(2,1)S(1)}, bf16[26,45,128]{2,1,0:T(8,128)(2,1)S(1)}, u32[]{:S(2)}, u32[]{:S(2)}) collective-permute-start(bf16[26,45,128]{2,1,0:T(8,128)(2,1)S(1)} %get-tuple-element.35), channel_id=1, source_target_pairs={{0,16},{8,24},{16,0},{24,8},{1,17},{9,25},{17,1},{25,9},{2,18},{10... | collective-permute-start | bytes 898568 | tf_op jit(solution)/shard_map/ppermute | solution.py:610
  11.0 13.5 %collective-permute-start.6 = (bf16[26,45,128]{2,1,0:T(8,128)(2,1)S(1)}, bf16[26,45,128]{2,1,0:T(8,128)(2,1)S(1)}, u32[]{:S(2)}, u32[]{:S(2)}) collective-permute-start(bf16[26,45,128]{2,1,0:T(8,128)(2,1)S(1)} %get-tuple-element.36), channel_id=1, source_target_pairs={{0,24},{8,16},{16,8},{24,0},{1,25},{9,17},{17,9},{25,1},{2,26},{10... | collective-permute-start | bytes 898568 | tf_op jit(solution)/shard_map/ppermute | solution.py:610
  14.5 5.7 %collective-permute-start.1 = (f32[2,16,73]{2,1,0:T(8,128)S(1)}, f32[2,16,73]{2,1,0:T(8,128)S(1)}, u32[]{:S(2)}, u32[]{:S(2)}) collective-permute-start(f32[2,16,73]{2,1,0:T(8,128)S(1)} %get-tuple-element.30), channel_id=1, source_target_pairs={{0,7},{1,2},{2,1},{3,4},{4,3},{5,6},{6,5},{7,0},{8,15},{9,10},{10,... | collective-permute-start | bytes 28040 | tf_op jit(solution)/shard_map/ppermute | solution.py:607
  18.6 8.4 %collective-permute-start.7 = (bf16[80,1024]{1,0:T(8,128)(2,1)S(1)}, bf16[80,1024]{1,0:T(8,128)(2,1)S(1)}, u32[]{:S(2)}, u32[]{:S(2)}) collective-permute-start(bf16[80,1024]{1,0:T(8,128)(2,1)S(1)} %forward.1.own_ref), channel_id=1, source_target_pairs={{0,8},{8,0},{16,24},{24,16},{1,9},{9,1},{17,25},{25,17},{2,10},{10... | collective-permute-start | bytes 491528 | tf_op jit(solution)/shard_map/ppermute | solution.py:610
  20.2 10.4 %collective-permute-start.8 = (bf16[80,1024]{1,0:T(8,128)(2,1)S(1)}, bf16[80,1024]{1,0:T(8,128)(2,1)S(1)}, u32[]{:S(2)}, u32[]{:S(2)}) collective-permute-start(bf16[80,1024]{1,0:T(8,128)(2,1)S(1)} %forward.1.own_ref), channel_id=1, source_target_pairs={{0,16},{8,24},{16,0},{24,8},{1,17},{9,25},{17,1},{25,9},{2,18},{10... | collective-permute-start | bytes 491528 | tf_op jit(solution)/shard_map/ppermute | solution.py:610
  21.7 8.9 %collective-permute-start.9 = (bf16[80,1024]{1,0:T(8,128)(2,1)S(1)}, bf16[80,1024]{1,0:T(8,128)(2,1)S(1)}, u32[]{:S(2)}, u32[]{:S(2)}) collective-permute-start(bf16[80,1024]{1,0:T(8,128)(2,1)S(1)} %forward.1.own_ref), channel_id=1, source_target_pairs={{0,24},{8,16},{16,8},{24,0},{1,25},{9,17},{17,9},{25,1},{2,26},{10... | collective-permute-start | bytes 491528 | tf_op jit(solution)/shard_map/ppermute | solution.py:610
  40.3 9.5 %collective-permute-start.12 = (bf16[1,320,128]{2,1,0:T(8,128)(2,1)S(1)}, bf16[1,320,128]{2,1,0:T(8,128)(2,1)S(1)}, u32[]{:S(2)}, u32[]{:S(2)}) collective-permute-start(bf16[1,320,128]{2,1,0:T(8,128)(2,1)S(1)} %get-tuple-element.46), channel_id=1, source_target_pairs={{0,4},{1,5},{2,6},{3,7},{4,0},{5,1},{6,2},{7,3},{8,12},{9,13},{10,... | collective-permute-start | bytes 245768 | tf_op jit(solution)/shard_map/ppermute | solution.py:603
  41.6 8.2 %collective-permute-start.13 = (bf16[1,320,128]{2,1,0:T(8,128)(2,1)S(1)}, bf16[1,320,128]{2,1,0:T(8,128)(2,1)S(1)}, u32[]{:S(2)}, u32[]{:S(2)}) collective-permute-start(bf16[1,320,128]{2,1,0:T(8,128)(2,1)S(1)} %get-tuple-element.47), channel_id=1, source_target_pairs={{0,6},{1,7},{2,4},{3,5},{4,2},{5,3},{6,0},{7,1},{8,14},{9,15},{10,... | collective-permute-start | bytes 245768 | tf_op jit(solution)/shard_map/ppermute | solution.py:603
  50.0 5.4 %collective-permute-start.18 = (bf16[1,320,128]{2,1,0:T(8,128)(2,1)S(1)}, bf16[1,320,128]{2,1,0:T(8,128)(2,1)S(1)}, u32[]{:S(2)}, u32[]{:S(2)}) collective-permute-start(bf16[1,320,128]{2,1,0:T(8,128)(2,1)S(1)} %pair_add.1), channel_id=1, source_target_pairs={{0,2},{1,3},{2,0},{3,1},{4,6},{5,7},{6,4},{7,5},{8,10},{9,11},{10,... | collective-permute-start | bytes 245768 | tf_op jit(solution)/shard_map/ppermute | solution.py:603
  51.6 8.7 %collective-permute-start.14 = (bf16[1,320,128]{2,1,0:T(8,128)(2,1)S(1)}, bf16[1,320,128]{2,1,0:T(8,128)(2,1)S(1)}, u32[]{:S(2)}, u32[]{:S(2)}) collective-permute-start(bf16[1,320,128]{2,1,0:T(8,128)(2,1)S(1)} %pair_add.1), channel_id=1, source_target_pairs={{0,4},{1,5},{2,6},{3,7},{4,0},{5,1},{6,2},{7,3},{8,12},{9,13},{10,... | collective-permute-start | bytes 245768 | tf_op jit(solution)/shard_map/ppermute | solution.py:603
  52.7 7.6 %collective-permute-start.15 = (bf16[1,320,128]{2,1,0:T(8,128)(2,1)S(1)}, bf16[1,320,128]{2,1,0:T(8,128)(2,1)S(1)}, u32[]{:S(2)}, u32[]{:S(2)}) collective-permute-start(bf16[1,320,128]{2,1,0:T(8,128)(2,1)S(1)} %pair_add.1), channel_id=1, source_target_pairs={{0,6},{1,7},{2,4},{3,5},{4,2},{5,3},{6,0},{7,1},{8,14},{9,15},{10,... | collective-permute-start | bytes 245768 | tf_op jit(solution)/shard_map/ppermute | solution.py:603
  55.4 5.9 %collective-permute-start.20 = (bf16[2,320,128]{2,1,0:T(8,128)(2,1)S(1)}, bf16[2,320,128]{2,1,0:T(8,128)(2,1)S(1)}, u32[]{:S(2)}, u32[]{:S(2)}) collective-permute-start(bf16[2,320,128]{2,1,0:T(8,128)(2,1)S(1)} %pad_maximum_fusion.refs_0_), channel_id=1, source_target_pairs={{0,8},{8,0},{16,24},{24,16},{1,9},{9,1},{17,25},{25,17},{2,10},{10... | collective-permute-start | bytes 491528 | tf_op jit(solution)/shard_map/ppermute | solution.py:610
  56.4 6.1 %collective-permute-start.22 = (bf16[2,320,128]{2,1,0:T(8,128)(2,1)S(1)}, bf16[2,320,128]{2,1,0:T(8,128)(2,1)S(1)}, u32[]{:S(2)}, u32[]{:S(2)}) collective-permute-start(bf16[2,320,128]{2,1,0:T(8,128)(2,1)S(1)} %pad_maximum_fusion.refs_0_), channel_id=1, source_target_pairs={{0,16},{8,24},{16,0},{24,8},{1,17},{9,25},{17,1},{25,9},{2,18},{10... | collective-permute-start | bytes 491528 | tf_op jit(solution)/shard_map/ppermute | solution.py:610
  57.6 8.0 %collective-permute-start.24 = (bf16[2,320,128]{2,1,0:T(8,128)(2,1)S(1)}, bf16[2,320,128]{2,1,0:T(8,128)(2,1)S(1)}, u32[]{:S(2)}, u32[]{:S(2)}) collective-permute-start(bf16[2,320,128]{2,1,0:T(8,128)(2,1)S(1)} %pad_maximum_fusion.refs_0_), channel_id=1, source_target_pairs={{0,24},{8,16},{16,8},{24,0},{1,25},{9,17},{17,9},{25,1},{2,26},{10... | collective-permute-start | bytes 491528 | tf_op jit(solution)/shard_map/ppermute | solution.py:610
  60.4 7.1 %collective-permute-start.27 = (bf16[2,320,128]{2,1,0:T(8,128)(2,1)S(1)}, bf16[2,320,128]{2,1,0:T(8,128)(2,1)S(1)}, u32[]{:S(2)}, u32[]{:S(2)}) collective-permute-start(bf16[2,320,128]{2,1,0:T(8,128)(2,1)S(1)} %constant_dynamic-update-slice_fusion.refs_0_), channel_id=1, source_target_pairs={{0,8},{8,0},{16,24},{24,16},{1,9},{9,1},{17,25},{25,17},{2,10},{10... | collective-permute-start | bytes 491528 | tf_op jit(solution)/shard_map/ppermute | solution.py:610
  61.4 8.5 %collective-permute-start.29 = (bf16[2,320,128]{2,1,0:T(8,128)(2,1)S(1)}, bf16[2,320,128]{2,1,0:T(8,128)(2,1)S(1)}, u32[]{:S(2)}, u32[]{:S(2)}) collective-permute-start(bf16[2,320,128]{2,1,0:T(8,128)(2,1)S(1)} %constant_dynamic-update-slice_fusion.refs_0_), channel_id=1, source_target_pairs={{0,16},{8,24},{16,0},{24,8},{1,17},{9,25},{17,1},{25,9},{2,18},{10... | collective-permute-start | bytes 491528 | tf_op jit(solution)/shard_map/ppermute | solution.py:610
  62.5 9.0 %collective-permute-start.16 = (bf16[2,320,128]{2,1,0:T(8,128)(2,1)S(1)}, bf16[2,320,128]{2,1,0:T(8,128)(2,1)S(1)}, u32[]{:S(2)}, u32[]{:S(2)}) collective-permute-start(bf16[2,320,128]{2,1,0:T(8,128)(2,1)S(1)} %constant_dynamic-update-slice_fusion.refs_0_), channel_id=1, source_target_pairs={{0,24},{8,16},{16,8},{24,0},{1,25},{9,17},{17,9},{25,1},{2,26},{10... | collective-permute-start | bytes 491528 | tf_op jit(solution)/shard_map/ppermute | solution.py:610
  65.6 5.9 %collective-permute-start.21 = (bf16[2,320,128]{2,1,0:T(8,128)(2,1)S(1)}, bf16[2,320,128]{2,1,0:T(8,128)(2,1)S(1)}, u32[]{:S(2)}, u32[]{:S(2)}) collective-permute-start(bf16[2,320,128]{2,1,0:T(8,128)(2,1)S(1)} %collective-permute-done.20.refs_2_), channel_id=1, source_target_pairs={{0,1},{1,0},{2,3},{3,2},{4,5},{5,4},{6,7},{7,6},{8,9},{9,8},{10,11... | collective-permute-start | bytes 491528 | tf_op jit(solution)/shard_map/ppermute | solution.py:603
  65.6 6.4 %collective-permute-start.23 = (bf16[2,320,128]{2,1,0:T(8,128)(2,1)S(1)}, bf16[2,320,128]{2,1,0:T(8,128)(2,1)S(1)}, u32[]{:S(2)}, u32[]{:S(2)}) collective-permute-start(bf16[2,320,128]{2,1,0:T(8,128)(2,1)S(1)} %collective-permute-done.22.refs_4_), channel_id=1, source_target_pairs={{0,1},{1,0},{2,3},{3,2},{4,5},{5,4},{6,7},{7,6},{8,9},{9,8},{10,11... | collective-permute-start | bytes 491528 | tf_op jit(solution)/shard_map/ppermute | solution.py:603
  67.5 9.1 %collective-permute-start.26 = (bf16[2,320,128]{2,1,0:T(8,128)(2,1)S(1)}, bf16[2,320,128]{2,1,0:T(8,128)(2,1)S(1)}, u32[]{:S(2)}, u32[]{:S(2)}) collective-permute-start(bf16[2,320,128]{2,1,0:T(8,128)(2,1)S(1)} %constant_dynamic-update-slice_fusion.refs_0_), channel_id=1, source_target_pairs={{0,1},{1,0},{2,3},{3,2},{4,5},{5,4},{6,7},{7,6},{8,9},{9,8},{10,11... | collective-permute-start | bytes 491528 | tf_op jit(solution)/shard_map/ppermute | solution.py:603
  72.0 6.0 %collective-permute-start.17 = (bf16[2,320,128]{2,1,0:T(8,128)(2,1)S(1)}, bf16[2,320,128]{2,1,0:T(8,128)(2,1)S(1)}, u32[]{:S(2)}, u32[]{:S(2)}) collective-permute-start(bf16[2,320,128]{2,1,0:T(8,128)(2,1)S(1)} %collective-permute-done.16.refs_0_), channel_id=1, source_target_pairs={{0,1},{1,0},{2,3},{3,2},{4,5},{5,4},{6,7},{7,6},{8,9},{9,8},{10,11... | collective-permute-start | bytes 491528 | tf_op jit(solution)/shard_map/ppermute | solution.py:603
  (14 other events, 96.3 us)

commit v4 on v3

--- a/solution.py
+++ b/solution.py
@@ -174,8 +174,8 @@
 
 
 def prep_kernel(plan, obs_ref, near_ref, far_ref, own_ref, *refs):
-    truth_ref, own_out_ref, row_s = refs[-3:]
-    refs = refs[:-3]
+    even_out, odd_out, truth_ref, own_out_ref, row_s = refs[-5:]
+    refs = refs[:-5]
     own_out_ref[...] = own_ref[...]
     half, offset, padded_out = plan.half, plan.offset, plan.padded_out
     even = here()[2] == 0
@@ -195,21 +195,27 @@
         truth_ref[:, j * LANES : (j + 1) * LANES] = jnp.transpose(tile)[:padded_out]
     members, main = plan.members, plan.main
     pack, valid, extras = plan.pack, plan.valid, plan.extras
-    out_ref = refs[-1]
-    _, rows_in, slots, _ = out_ref.shape
-    lon_dev = plan.lon_dev
+    rows_in, slots, lon_dev = plan.rows_in, plan.slots, plan.lon_dev
     bulk = lon_dev // ROWS * ROWS
     group = rows_in // pack
     lane = lax.broadcasted_iota(jnp.int32, (1, LANES), 1)
-    out_ref[:, :, bulk:, :] = jnp.zeros(
-        (members, rows_in, slots - bulk, out_ref.shape[3]), out_ref.dtype
-    )
+    for out in (even_out, odd_out):
+        for first in range(0, LANES, slots):
+            out[:, :, first + bulk : first + slots, :] = jnp.zeros(
+                out.shape[:2] + (slots - bulk, out.shape[3]), out.dtype
+            )
+
+    def put(d, r, lanes, value):
+        even_out[r // per, d, r % per * slots : r % per * slots + lon_dev, lanes] = value
+        if 0 < r <= per * odd_out.shape[0]:
+            at = (r - 1) % per * slots
+            odd_out[(r - 1) // per, d, at : at + lon_dev, lanes] = value
+
     for d in range(members):
         ref = refs[d]
         for k in range(main):
-            out_ref[d, :, :lon_dev, k * LANES : (k + 1) * LANES] = ref[
-                k * rows_in : (k + 1) * rows_in
-            ]
+            for r in range(rows_in):
+                put(d, r, slice(k * LANES, (k + 1) * LANES), ref[k * rows_in + r])
         slab = ref[main * rows_in + group].astype(jnp.float32)
         for g in range(pack):
             for i in range(group):
@@ -222,7 +228,9 @@
                     moved = pltpu.roll(slab, shift, 1) if shift else slab
                     value = jnp.where(lane == valid + e, moved, value)
                 value = jnp.where(lane == valid + extras, 1.0, value)
-                out_ref[d, r, :lon_dev, main * LANES :] = value.astype(out_ref.dtype)
+                put(
+                    d, r, slice(main * LANES, (main + 1) * LANES), value.astype(even_out.dtype)
+                )
 
 
 def split_bias(tile, row_high):
@@ -249,9 +257,9 @@
     per_half, special = plan.per_half, plan.special
     place_ref = here()
     y_refs = refs[:members]
-    x_ref, obs_ref, wid_ref = refs[members : 3 + members]
-    g_ref, score_ref, send_ref, keep_ref = refs[3 + members : 7 + members]
-    g_s, gs_s, wide_s, packed_s = refs[7 + members :]
+    even_ref, odd_ref, obs_ref, wid_ref = refs[members : 4 + members]
+    g_ref, score_ref, send_ref, keep_ref = refs[4 + members : 8 + members]
+    g_s, gs_s, wide_s, packed_s = refs[8 + members :]
     step = 2 * LANES
     width_all = column_of(wid_ref, 1.0)
     for left in range(0, points, step):
@@ -262,26 +270,27 @@
             shape = (2 * ROWS, step)
             width = width_all[rows]
             inverse = 1.0 / (width * width)
+            scale = (-0.5 * math.log2(math.e)) * inverse
             values = [y[rows, cols].astype(jnp.float32) for y in y_refs]
             target = obs_ref[rows, cols]
-            pair_sum = jnp.full(shape, float(members), jnp.float32)
+            pair_sum = jnp.full(shape, 0.5 * members, jnp.float32)
             pull = [jnp.zeros(shape, jnp.float32) for _ in values]
             for x in range(members):
                 for y in range(x + 1, members):
                     spread = values[x] - values[y]
-                    kernel_pair = jnp.exp(-0.5 * spread * spread * inverse)
-                    pair_sum = pair_sum + 2.0 * kernel_pair
+                    kernel_pair = jnp.exp2(spread * spread * scale)
+                    pair_sum = pair_sum + kernel_pair
                     weighted = kernel_pair * spread
                     pull[x] = pull[x] + weighted
                     pull[y] = pull[y] - weighted
             obs_sum = jnp.zeros(shape, jnp.float32)
             for x in range(members):
                 misfit = values[x] - target
-                kernel_obs = jnp.exp(-0.5 * misfit * misfit * inverse)
+                kernel_obs = jnp.exp2(misfit * misfit * scale)
                 obs_sum = obs_sum + kernel_obs
-                grad = inverse * (misfit * kernel_obs - pull[x] / members)
+                grad = inverse * (misfit * kernel_obs - pull[x] * (1.0 / members))
                 g_s[x, rows, cols] = grad.astype(jnp.bfloat16)
-            terms = pair_sum / (2.0 * members * members) - obs_sum / members
+            terms = pair_sum * (1.0 / (members * members)) - obs_sum * (1.0 / members)
             row = lo + lax.broadcasted_iota(jnp.int32, (2 * ROWS, 1), 0)
             terms = jnp.where(row < out_chan, terms, 0.0)
             tally = tally + terms[:ROWS] + terms[ROWS:]
@@ -294,7 +303,10 @@
                 shift = (b - half - plan.offset) % points
                 moved = pltpu.roll(grad, shift, 1) if shift else grad
                 start = b * padded_out + lo
-                gs_s[x, start : start + 2 * ROWS, :] = moved.astype(jnp.bfloat16)
+                moved = moved.astype(jnp.bfloat16)
+                for t in range(points // LANES):
+                    lanes = slice((t * members + x) * LANES, (t * members + x + 1) * LANES)
+                    gs_s[start : start + 2 * ROWS, lanes] = moved[:, t * LANES : (t + 1) * LANES]
     tiles = main + 1
     split = size - special - SPECIAL
     for h in range(2):
@@ -302,15 +314,13 @@
             (tiles, size - special, LANES), jnp.float32
         )
     for a in range(taps):
-        total = None
-        for x in range(members):
-            part = lax.dot_general(
-                gs_s[x],
-                x_ref[x, a : a + rows_out].reshape(points, tiles * LANES),
-                NN,
-                preferred_element_type=jnp.float32,
-            )
-            total = part if total is None else total + part
+        x_ref = odd_ref if a % 2 else even_ref
+        total = lax.dot_general(
+            gs_s[...],
+            x_ref[a // 2 : (a + rows_out) // 2].reshape(points * members, tiles * LANES),
+            NN,
+            preferred_element_type=jnp.float32,
+        )
         for b in range(taps):
             tap = a * taps + b
             block = total[b * padded_out : (b + 1) * padded_out]
@@ -589,12 +599,13 @@
     )
     bias_row = (per_half + 1) * extras
     assert rest and total_taps % 2 and bias_row + 2 <= SPECIAL
+    assert 2 * slots == LANES and rows_in % 2 == 0
     wide = round_up(in_chan, LANES)
     plan = types.SimpleNamespace(
         members=members, taps=taps, half=half, offset=offset, lon_dev=lon_dev, out_chan=out_chan,
         padded_out=padded_out, rows_out=rows_out, points=points, main=main, rest=rest, pairs=pairs,
         pack=pack, valid=valid, sub=sub, extras=extras, half_rows=half_rows, per_half=per_half,
-        special=special, bias_row=bias_row,
+        special=special, bias_row=bias_row, rows_in=rows_in, slots=slots,
         special_row=special - (pairs - 1) * (half_rows // pairs),
     )
     factor = 1.0 / math.sqrt(members * rows_out * lon_dev * lon_count)
@@ -670,15 +681,16 @@
         outputs.append(swap_member(own_outputs, d))
 
     tiles = main + 1
-    x_all, truth, own_copy = pl.pallas_call(
+    x_even, x_odd, truth, own_copy = pl.pallas_call(
         functools.partial(prep_kernel, plan),
         out_shape=(
-            jax.ShapeDtypeStruct((members, rows_in, slots, tiles * LANES), jnp.bfloat16),
+            jax.ShapeDtypeStruct((rows_in // 2, members, LANES, tiles * LANES), jnp.bfloat16),
+            jax.ShapeDtypeStruct(((rows_in - 2) // 2, members, LANES, tiles * LANES), jnp.bfloat16),
             jax.ShapeDtypeStruct((padded_out, points), jnp.float32),
             jax.ShapeDtypeStruct((padded_out, points), jnp.bfloat16),
         ),
         in_specs=[vmem()] * (members + 4),
-        out_specs=[vmem()] * 3,
+        out_specs=[vmem()] * 4,
         scratch_shapes=[pltpu.VMEM((rows_out, slots, LANES), jnp.float32)],
         cost_estimate=cost(0, 4_000_000),
         compiler_params=limit(20),
@@ -697,11 +709,11 @@
             jax.ShapeDtypeStruct((pairs, piece_rows, LANES), jnp.bfloat16),
             jax.ShapeDtypeStruct((pairs, piece_rows, LANES), jnp.float32),
         ),
-        in_specs=[vmem()] * (members + 3),
+        in_specs=[vmem()] * (members + 4),
         out_specs=[vmem()] * 4,
         scratch_shapes=[
             pltpu.VMEM((members, padded_out, points), jnp.bfloat16),
-            pltpu.VMEM((members, stack, points), jnp.bfloat16),
+            pltpu.VMEM((stack, members * points), jnp.bfloat16),
             pltpu.VMEM((tiles, 2 * half_rows, LANES), jnp.float32),
             pltpu.VMEM((2 * half_rows // pack, LANES), jnp.float32),
         ],
@@ -710,7 +722,7 @@
         ),
         compiler_params=limit(32),
         name="gradient",
-    )(*outputs, x_all, truth, widths[None, :])
+    )(*outputs, x_even, x_odd, truth, widths[None, :])
 
     mine, *out_pieces = pl.pallas_call(
         functools.partial(core_add_kernel, plan),

time: 80.6 us -> 80.8 us (level)
  transfers between devices with their start and end apart: 31 -> 31, of which waited for: 12 -> 12; matrix products, arithmetic and copies ran while one was open for 0% -> 0% of each run, Pallas kernels for 13% -> 14%
where the time goes in v4:
time: 80.8 us; the launch traced here: 80.6 us
  starting transfers between devices  32 us (40%)
  waiting for transfers between devices  23 us (28%)
  Pallas kernels  20.8 us (26%)
  local copies, waits for them, and re-layouts  3.93 us (5%)
  between operations  0.98 us (1%)
    ppermute x12, starting transfers between devices, swap_member(): return lax.ppermute(value, 'member', [(i, i ^ d) for i in range(members)])  16.1 us
    ppermute x12, waiting for transfers between devices, swap_member(): return lax.ppermute(value, 'member', [(i, i ^ d) for i in range(members)])  12.4 us
    ppermute x17, starting transfers between devices, swap_lon(): return lax.ppermute(value, 'lon', [(i, i ^ d) for i in range(lon_count)])  10.7 us
    ppermute x17, waiting for transfers between devices, swap_lon(): return lax.ppermute(value, 'lon', [(i, i ^ d) for i in range(lon_count)])  10.6 us
    pallas_call x1, Pallas kernels, body(): pl.pallas_call(functools.partial(gradient_kernel, plan), out_shape=(jax.S...  6.48 us
    pallas_call x3, Pallas kernels, assemble(): pl.pallas_call(kernel, out_shape=[grad_shape, jax.ShapeDtypeStruct(other_...  5.66 us
    ppermute x2, starting transfers between devices, swap_far(): return lax.ppermute(value, 'lon', step)  5.24 us
    unnamed x15, local copies, waits for them, and re-layouts  3.91 us
  transfers between devices with their start and end apart: 31, of which 12 were waited for; matrix products, arithmetic and copies ran while one was open for 0% of the time, Pallas kernels for 14%

profile of v4, /device:TPU:0, one launch (start us, length us, event | category | flops | bytes accessed | tf_op | source)
XLA Modules:
  0.0 80.6 jit_solution(1148784489212057594)
XLA Ops:
  3.3 4.7 %collective-permute-start.3 = (bf16[20,4,641]{2,1,0:T(4,128)(2,1)S(1)}, bf16[20,4,641]{2,1,0:T(4,128)(2,1)S(1)}, u32[]{:S(2)}, u32[]{:S(2)}) collective-permute-start(bf16[20,4,641]{2,1,0:T(4,128)(2,1)S(1)} %get-tuple-element.33), channel_id=1, source_target_pairs={{0,7},{1,2},{2,1},{3,4},{4,3},{5,6},{6,5},{7,0},{8,15},{9,10},{10,... | collective-permute-start | bytes 307688 | tf_op jit(solution)/shard_map/ppermute | solution.py:618
  8.0 1.5 %collective-permute-start.4 = (bf16[26,45,128]{2,1,0:T(8,128)(2,1)S(1)}, bf16[26,45,128]{2,1,0:T(8,128)(2,1)S(1)}, u32[]{:S(2)}, u32[]{:S(2)}) collective-permute-start(bf16[26,45,128]{2,1,0:T(8,128)(2,1)S(1)} %get-tuple-element.35), channel_id=1, source_target_pairs={{0,8},{8,0},{16,24},{24,16},{1,9},{9,1},{17,25},{25,17},{2,10},{10... | collective-permute-start | bytes 898568 | tf_op jit(solution)/shard_map/ppermute | solution.py:621
  9.5 1.5 %collective-permute-start.5 = (bf16[26,45,128]{2,1,0:T(8,128)(2,1)S(1)}, bf16[26,45,128]{2,1,0:T(8,128)(2,1)S(1)}, u32[]{:S(2)}, u32[]{:S(2)}) collective-permute-start(bf16[26,45,128]{2,1,0:T(8,128)(2,1)S(1)} %get-tuple-element.36), channel_id=1, source_target_pairs={{0,16},{8,24},{16,0},{24,8},{1,17},{9,25},{17,1},{25,9},{2,18},{10... | collective-permute-start | bytes 898568 | tf_op jit(solution)/shard_map/ppermute | solution.py:621
  11.5 1.9 %copy-done = bf16[5,5,73,641]{3,2,1,0:T(8,128)(2,1)S(1)} copy-done((bf16[5,5,73,641]{3,2,1,0:T(8,128)(2,1)S(1)}, bf16[5,5,73,641]{3,2,1,0:T(8,128)(2,1)}, u32[]{:S(2)}) %copy-start) | copy-done | bytes 2339674
  15.0 3.6 %forward.1.own_ref = bf16[80,1024]{1,0:T(8,128)(2,1)S(1)} custom-call(bf16[20,45,641]{2,1,0:T(8,128)(2,1)S(1)} %bitcast.17, bf16[20,4,641]{2,1,0:T(4,128)(2,1)S(1)} %collective-permute-done.2.near_ref, bf16[20,4,641]{2,1,0:T(4,128)(2,1)S(1)} %collective-permute-done.3.far_ref, bf16[25,80,768]{2,1,0:T(8,128)(2,1)S(1)} %stage.1.w_s, f32[1,73]{1,0:T(1,128)S(1)} %bitcast.18), custom_call_target="tpu_custom_call" | custom-call | flops 3145728000 | bytes 6000000 | tf_op jit(solution)/shard_map/forward/pallas_call | solution.py:666
  18.6 1.6 %collective-permute-start.7 = (bf16[80,1024]{1,0:T(8,128)(2,1)S(1)}, bf16[80,1024]{1,0:T(8,128)(2,1)S(1)}, u32[]{:S(2)}, u32[]{:S(2)}) collective-permute-start(bf16[80,1024]{1,0:T(8,128)(2,1)S(1)} %forward.1.own_ref), channel_id=1, source_target_pairs={{0,8},{8,0},{16,24},{24,16},{1,9},{9,1},{17,25},{25,17},{2,10},{10... | collective-permute-start | bytes 491528 | tf_op jit(solution)/shard_map/ppermute | solution.py:621
  20.2 1.5 %collective-permute-start.8 = (bf16[80,1024]{1,0:T(8,128)(2,1)S(1)}, bf16[80,1024]{1,0:T(8,128)(2,1)S(1)}, u32[]{:S(2)}, u32[]{:S(2)}) collective-permute-start(bf16[80,1024]{1,0:T(8,128)(2,1)S(1)} %forward.1.own_ref), channel_id=1, source_target_pairs={{0,16},{8,24},{16,0},{24,8},{1,17},{9,25},{17,1},{25,9},{2,18},{10... | collective-permute-start | bytes 491528 | tf_op jit(solution)/shard_map/ppermute | solution.py:621
  23.1 1.5 %collective-permute-done.6.refs_3_ = bf16[26,45,128]{2,1,0:T(8,128)(2,1)S(1)} collective-permute-done((bf16[26,45,128]{2,1,0:T(8,128)(2,1)S(1)}, bf16[26,45,128]{2,1,0:T(8,128)(2,1)S(1)}, u32[]{:S(2)}, u32[]{:S(2)}) %collective-permute-start.6) | collective-permute-done | bytes 299552 | tf_op jit(solution)/shard_map/ppermute | solution.py:621
  25.7 1.4 %collective-permute-done.7.refs_1_ = bf16[80,1024]{1,0:T(8,128)(2,1)S(1)} collective-permute-done((bf16[80,1024]{1,0:T(8,128)(2,1)S(1)}, bf16[80,1024]{1,0:T(8,128)(2,1)S(1)}, u32[]{:S(2)}, u32[]{:S(2)}) %collective-permute-start.7) | collective-permute-done | bytes 163872 | tf_op jit(solution)/shard_map/ppermute | solution.py:621
  27.1 3.5 %collective-permute-done.8.refs_2_ = bf16[80,1024]{1,0:T(8,128)(2,1)S(1)} collective-permute-done((bf16[80,1024]{1,0:T(8,128)(2,1)S(1)}, bf16[80,1024]{1,0:T(8,128)(2,1)S(1)}, u32[]{:S(2)}, u32[]{:S(2)}) %collective-permute-start.8) | collective-permute-done | bytes 163872 | tf_op jit(solution)/shard_map/ppermute | solution.py:621
  30.6 6.5 %gradient.1 = (bf16[80,1024]{1,0:T(8,128)(2,1)S(1)}, f32[1,1024]{1,0:T(1,128)S(1)}, bf16[4,320,128]{2,1,0:T(8,128)(2,1)S(1)}, f32[4,320,128]{2,1,0:T(8,128)S(1)}) custom-call(bf16[80,1024]{1,0:T(8,128)(2,1)S(1)} %get-tuple-element.38.refs_0_, bf16[80,1024]{1,0:T(8,128)(2,1)S(1)} %collective-permute-done.7.refs_1_, ...), custom_call_target="tpu_custom_call" | custom-call | flops 4194304000 | bytes 6000000 | tf_op jit(solution)/shard_map/gradient/pallas_call | solution.py:704
  37.2 1.6 %collective-permute-done.10.got_ref = bf16[4,320,128]{2,1,0:T(8,128)(2,1)S(1)} collective-permute-done((bf16[4,320,128]{2,1,0:T(8,128)(2,1)S(1)}, bf16[4,320,128]{2,1,0:T(8,128)(2,1)S(1)}, u32[]{:S(2)}, u32[]{:S(2)}) %collective-permute-start.10) | collective-permute-done | bytes 327712 | tf_op jit(solution)/shard_map/ppermute | solution.py:614
  38.9 1.6 %collective-permute-start.11 = (bf16[1,320,128]{2,1,0:T(8,128)(2,1)S(1)}, bf16[1,320,128]{2,1,0:T(8,128)(2,1)S(1)}, u32[]{:S(2)}, u32[]{:S(2)}) collective-permute-start(bf16[1,320,128]{2,1,0:T(8,128)(2,1)S(1)} %get-tuple-element.47), channel_id=1, source_target_pairs={{0,2},{1,3},{2,0},{3,1},{4,6},{5,7},{6,4},{7,5},{8,10},{9,11},{10,... | collective-permute-start | bytes 245768 | tf_op jit(solution)/shard_map/ppermute | solution.py:614
  41.8 1.5 %collective-permute-start.13 = (bf16[1,320,128]{2,1,0:T(8,128)(2,1)S(1)}, bf16[1,320,128]{2,1,0:T(8,128)(2,1)S(1)}, u32[]{:S(2)}, u32[]{:S(2)}) collective-permute-start(bf16[1,320,128]{2,1,0:T(8,128)(2,1)S(1)} %get-tuple-element.49), channel_id=1, source_target_pairs={{0,6},{1,7},{2,4},{3,5},{4,2},{5,3},{6,0},{7,1},{8,14},{9,15},{10,... | collective-permute-start | bytes 245768 | tf_op jit(solution)/shard_map/ppermute | solution.py:614
  43.4 6.5 %collective-permute-done.12.refs_1_ = bf16[1,320,128]{2,1,0:T(8,128)(2,1)S(1)} collective-permute-done((bf16[1,320,128]{2,1,0:T(8,128)(2,1)S(1)}, bf16[1,320,128]{2,1,0:T(8,128)(2,1)S(1)}, u32[]{:S(2)}, u32[]{:S(2)}) %collective-permute-start.12) | collective-permute-done | bytes 81952 | tf_op jit(solution)/shard_map/ppermute | solution.py:614
  50.2 1.6 %collective-permute-start.18 = (bf16[1,320,128]{2,1,0:T(8,128)(2,1)S(1)}, bf16[1,320,128]{2,1,0:T(8,128)(2,1)S(1)}, u32[]{:S(2)}, u32[]{:S(2)}) collective-permute-start(bf16[1,320,128]{2,1,0:T(8,128)(2,1)S(1)} %pair_add.1), channel_id=1, source_target_pairs={{0,2},{1,3},{2,0},{3,1},{4,6},{5,7},{6,4},{7,5},{8,10},{9,11},{10,... | collective-permute-start | bytes 245768 | tf_op jit(solution)/shard_map/ppermute | solution.py:614
  52.9 1.7 %collective-permute-start.15 = (bf16[1,320,128]{2,1,0:T(8,128)(2,1)S(1)}, bf16[1,320,128]{2,1,0:T(8,128)(2,1)S(1)}, u32[]{:S(2)}, u32[]{:S(2)}) collective-permute-start(bf16[1,320,128]{2,1,0:T(8,128)(2,1)S(1)} %pair_add.1), channel_id=1, source_target_pairs={{0,6},{1,7},{2,4},{3,5},{4,2},{5,3},{6,0},{7,1},{8,14},{9,15},{10,... | collective-permute-start | bytes 245768 | tf_op jit(solution)/shard_map/ppermute | solution.py:614
  57.7 1.4 %collective-permute-start.24 = (bf16[2,320,128]{2,1,0:T(8,128)(2,1)S(1)}, bf16[2,320,128]{2,1,0:T(8,128)(2,1)S(1)}, u32[]{:S(2)}, u32[]{:S(2)}) collective-permute-start(bf16[2,320,128]{2,1,0:T(8,128)(2,1)S(1)} %pad_maximum_fusion.refs_0_), channel_id=1, source_target_pairs={{0,24},{8,16},{16,8},{24,0},{1,25},{9,17},{17,9},{25,1},{2,26},{10... | collective-permute-start | bytes 491528 | tf_op jit(solution)/shard_map/ppermute | solution.py:621
  62.7 3.1 %collective-permute-start.16 = (bf16[2,320,128]{2,1,0:T(8,128)(2,1)S(1)}, bf16[2,320,128]{2,1,0:T(8,128)(2,1)S(1)}, u32[]{:S(2)}, u32[]{:S(2)}) collective-permute-start(bf16[2,320,128]{2,1,0:T(8,128)(2,1)S(1)} %constant_dynamic-update-slice_fusion.refs_0_), channel_id=1, source_target_pairs={{0,24},{8,16},{16,8},{24,0},{1,25},{9,17},{17,9},{25,1},{2,26},{10... | collective-permute-start | bytes 491528 | tf_op jit(solution)/shard_map/ppermute | solution.py:621
  66.3 1.4 %collective-permute-done.27.refs_2_ = bf16[2,320,128]{2,1,0:T(8,128)(2,1)S(1)} collective-permute-done((bf16[2,320,128]{2,1,0:T(8,128)(2,1)S(1)}, bf16[2,320,128]{2,1,0:T(8,128)(2,1)S(1)}, u32[]{:S(2)}, u32[]{:S(2)}) %collective-permute-start.27) | collective-permute-done | bytes 163872 | tf_op jit(solution)/shard_map/ppermute | solution.py:621
  67.7 2.4 %collective-permute-done.29.refs_4_ = bf16[2,320,128]{2,1,0:T(8,128)(2,1)S(1)} collective-permute-done((bf16[2,320,128]{2,1,0:T(8,128)(2,1)S(1)}, bf16[2,320,128]{2,1,0:T(8,128)(2,1)S(1)}, u32[]{:S(2)}, u32[]{:S(2)}) %collective-permute-start.29) | collective-permute-done | bytes 163872 | tf_op jit(solution)/shard_map/ppermute | solution.py:621
  70.1 1.6 %collective-permute-done.16.refs_0_ = bf16[2,320,128]{2,1,0:T(8,128)(2,1)S(1)} collective-permute-done((bf16[2,320,128]{2,1,0:T(8,128)(2,1)S(1)}, bf16[2,320,128]{2,1,0:T(8,128)(2,1)S(1)}, u32[]{:S(2)}, u32[]{:S(2)}) %collective-permute-start.16) | collective-permute-done | bytes 163872 | tf_op jit(solution)/shard_map/ppermute | solution.py:621
  74.8 2.0 %assemble.3 = (f32[25,73,641]{2,1,0:T(8,128)}, f32[5,64,128]{2,1,0:T(8,128)S(1)}) custom-call(bf16[2,320,128]{2,1,0:T(8,128)(2,1)S(1)} %pad_maximum_fusion.refs_0_, bf16[2,320,128]{2,1,0:T(8,128)(2,1)S(1)} %collective-permute-done.19.refs_1_, bf16[2,320,128]{2,1,0:T(8,128)(2,1)S(1)} %collective-permute-done.20.refs_2_, ...), custom_call_target="tpu_custom_call" | custom-call | bytes 5000000 | tf_op jit(solution)/shard_map/assemble/pallas_call | solution.py:787
  78.2 2.3 %assemble.5 = (f32[25,73,641]{2,1,0:T(8,128)}, f32[1,73]{1,0:T(1,128)}) custom-call(bf16[2,320,128]{2,1,0:T(8,128)(2,1)S(1)} %collective-permute-done.16.refs_0_, bf16[2,320,128]{2,1,0:T(8,128)(2,1)S(1)} %collective-permute-done.17.refs_1_, f32[5,64,128]{2,1,0:T(8,128)S(1)} %get-tuple-element.50.refs_6_.refs_2_, ...), custom_call_target="tpu_custom_call", output_to_operand_aliasing={{0}: (3, {})} | custom-call | bytes 5000000 | tf_op jit(solution)/shard_map/assemble/pallas_call | solution.py:787
  (68 shorter events, 21.7 us)
Async XLA Ops:
  2.8 11.6 %collective-permute-start.2 = (bf16[20,4,641]{2,1,0:T(4,128)(2,1)S(1)}, bf16[20,4,641]{2,1,0:T(4,128)(2,1)S(1)}, u32[]{:S(2)}, u32[]{:S(2)}) collective-permute-start(bf16[20,4,641]{2,1,0:T(4,128)(2,1)S(1)} %get-tuple-element.32), channel_id=1, source_target_pairs={{0,1},{1,0},{2,3},{3,2},{4,5},{5,4},{6,7},{7,6},{8,9},{9,8},{10,11... | collective-permute-start | bytes 307688 | tf_op jit(solution)/shard_map/ppermute | solution.py:614
  3.3 11.1 %collective-permute-start.3 = (bf16[20,4,641]{2,1,0:T(4,128)(2,1)S(1)}, bf16[20,4,641]{2,1,0:T(4,128)(2,1)S(1)}, u32[]{:S(2)}, u32[]{:S(2)}) collective-permute-start(bf16[20,4,641]{2,1,0:T(4,128)(2,1)S(1)} %get-tuple-element.33), channel_id=1, source_target_pairs={{0,7},{1,2},{2,1},{3,4},{4,3},{5,6},{6,5},{7,0},{8,15},{9,10},{10,... | collective-permute-start | bytes 307688 | tf_op jit(solution)/shard_map/ppermute | solution.py:618
  8.0 13.7 %collective-permute-start.4 = (bf16[26,45,128]{2,1,0:T(8,128)(2,1)S(1)}, bf16[26,45,128]{2,1,0:T(8,128)(2,1)S(1)}, u32[]{:S(2)}, u32[]{:S(2)}) collective-permute-start(bf16[26,45,128]{2,1,0:T(8,128)(2,1)S(1)} %get-tuple-element.35), channel_id=1, source_target_pairs={{0,8},{8,0},{16,24},{24,16},{1,9},{9,1},{17,25},{25,17},{2,10},{10... | collective-permute-start | bytes 898568 | tf_op jit(solution)/shard_map/ppermute | solution.py:621
  9.5 13.5 %collective-permute-start.5 = (bf16[26,45,128]{2,1,0:T(8,128)(2,1)S(1)}, bf16[26,45,128]{2,1,0:T(8,128)(2,1)S(1)}, u32[]{:S(2)}, u32[]{:S(2)}) collective-permute-start(bf16[26,45,128]{2,1,0:T(8,128)(2,1)S(1)} %get-tuple-element.36), channel_id=1, source_target_pairs={{0,16},{8,24},{16,0},{24,8},{1,17},{9,25},{17,1},{25,9},{2,18},{10... | collective-permute-start | bytes 898568 | tf_op jit(solution)/shard_map/ppermute | solution.py:621
  11.0 13.5 %collective-permute-start.6 = (bf16[26,45,128]{2,1,0:T(8,128)(2,1)S(1)}, bf16[26,45,128]{2,1,0:T(8,128)(2,1)S(1)}, u32[]{:S(2)}, u32[]{:S(2)}) collective-permute-start(bf16[26,45,128]{2,1,0:T(8,128)(2,1)S(1)} %get-tuple-element.37), channel_id=1, source_target_pairs={{0,24},{8,16},{16,8},{24,0},{1,25},{9,17},{17,9},{25,1},{2,26},{10... | collective-permute-start | bytes 898568 | tf_op jit(solution)/shard_map/ppermute | solution.py:621
  14.5 5.7 %collective-permute-start.1 = (f32[2,16,73]{2,1,0:T(8,128)S(1)}, f32[2,16,73]{2,1,0:T(8,128)S(1)}, u32[]{:S(2)}, u32[]{:S(2)}) collective-permute-start(f32[2,16,73]{2,1,0:T(8,128)S(1)} %get-tuple-element.31), channel_id=1, source_target_pairs={{0,7},{1,2},{2,1},{3,4},{4,3},{5,6},{6,5},{7,0},{8,15},{9,10},{10,... | collective-permute-start | bytes 28040 | tf_op jit(solution)/shard_map/ppermute | solution.py:618
  18.6 8.4 %collective-permute-start.7 = (bf16[80,1024]{1,0:T(8,128)(2,1)S(1)}, bf16[80,1024]{1,0:T(8,128)(2,1)S(1)}, u32[]{:S(2)}, u32[]{:S(2)}) collective-permute-start(bf16[80,1024]{1,0:T(8,128)(2,1)S(1)} %forward.1.own_ref), channel_id=1, source_target_pairs={{0,8},{8,0},{16,24},{24,16},{1,9},{9,1},{17,25},{25,17},{2,10},{10... | collective-permute-start | bytes 491528 | tf_op jit(solution)/shard_map/ppermute | solution.py:621
  20.2 10.4 %collective-permute-start.8 = (bf16[80,1024]{1,0:T(8,128)(2,1)S(1)}, bf16[80,1024]{1,0:T(8,128)(2,1)S(1)}, u32[]{:S(2)}, u32[]{:S(2)}) collective-permute-start(bf16[80,1024]{1,0:T(8,128)(2,1)S(1)} %forward.1.own_ref), channel_id=1, source_target_pairs={{0,16},{8,24},{16,0},{24,8},{1,17},{9,25},{17,1},{25,9},{2,18},{10... | collective-permute-start | bytes 491528 | tf_op jit(solution)/shard_map/ppermute | solution.py:621
  21.7 8.9 %collective-permute-start.9 = (bf16[80,1024]{1,0:T(8,128)(2,1)S(1)}, bf16[80,1024]{1,0:T(8,128)(2,1)S(1)}, u32[]{:S(2)}, u32[]{:S(2)}) collective-permute-start(bf16[80,1024]{1,0:T(8,128)(2,1)S(1)} %forward.1.own_ref), channel_id=1, source_target_pairs={{0,24},{8,16},{16,8},{24,0},{1,25},{9,17},{17,9},{25,1},{2,26},{10... | collective-permute-start | bytes 491528 | tf_op jit(solution)/shard_map/ppermute | solution.py:621
  40.5 9.5 %collective-permute-start.12 = (bf16[1,320,128]{2,1,0:T(8,128)(2,1)S(1)}, bf16[1,320,128]{2,1,0:T(8,128)(2,1)S(1)}, u32[]{:S(2)}, u32[]{:S(2)}) collective-permute-start(bf16[1,320,128]{2,1,0:T(8,128)(2,1)S(1)} %get-tuple-element.48), channel_id=1, source_target_pairs={{0,4},{1,5},{2,6},{3,7},{4,0},{5,1},{6,2},{7,3},{8,12},{9,13},{10,... | collective-permute-start | bytes 245768 | tf_op jit(solution)/shard_map/ppermute | solution.py:614
  41.8 8.2 %collective-permute-start.13 = (bf16[1,320,128]{2,1,0:T(8,128)(2,1)S(1)}, bf16[1,320,128]{2,1,0:T(8,128)(2,1)S(1)}, u32[]{:S(2)}, u32[]{:S(2)}) collective-permute-start(bf16[1,320,128]{2,1,0:T(8,128)(2,1)S(1)} %get-tuple-element.49), channel_id=1, source_target_pairs={{0,6},{1,7},{2,4},{3,5},{4,2},{5,3},{6,0},{7,1},{8,14},{9,15},{10,... | collective-permute-start | bytes 245768 | tf_op jit(solution)/shard_map/ppermute | solution.py:614
  50.2 5.4 %collective-permute-start.18 = (bf16[1,320,128]{2,1,0:T(8,128)(2,1)S(1)}, bf16[1,320,128]{2,1,0:T(8,128)(2,1)S(1)}, u32[]{:S(2)}, u32[]{:S(2)}) collective-permute-start(bf16[1,320,128]{2,1,0:T(8,128)(2,1)S(1)} %pair_add.1), channel_id=1, source_target_pairs={{0,2},{1,3},{2,0},{3,1},{4,6},{5,7},{6,4},{7,5},{8,10},{9,11},{10,... | collective-permute-start | bytes 245768 | tf_op jit(solution)/shard_map/ppermute | solution.py:614
  51.8 8.7 %collective-permute-start.14 = (bf16[1,320,128]{2,1,0:T(8,128)(2,1)S(1)}, bf16[1,320,128]{2,1,0:T(8,128)(2,1)S(1)}, u32[]{:S(2)}, u32[]{:S(2)}) collective-permute-start(bf16[1,320,128]{2,1,0:T(8,128)(2,1)S(1)} %pair_add.1), channel_id=1, source_target_pairs={{0,4},{1,5},{2,6},{3,7},{4,0},{5,1},{6,2},{7,3},{8,12},{9,13},{10,... | collective-permute-start | bytes 245768 | tf_op jit(solution)/shard_map/ppermute | solution.py:614
  52.9 7.6 %collective-permute-start.15 = (bf16[1,320,128]{2,1,0:T(8,128)(2,1)S(1)}, bf16[1,320,128]{2,1,0:T(8,128)(2,1)S(1)}, u32[]{:S(2)}, u32[]{:S(2)}) collective-permute-start(bf16[1,320,128]{2,1,0:T(8,128)(2,1)S(1)} %pair_add.1), channel_id=1, source_target_pairs={{0,6},{1,7},{2,4},{3,5},{4,2},{5,3},{6,0},{7,1},{8,14},{9,15},{10,... | collective-permute-start | bytes 245768 | tf_op jit(solution)/shard_map/ppermute | solution.py:614
  55.6 5.9 %collective-permute-start.20 = (bf16[2,320,128]{2,1,0:T(8,128)(2,1)S(1)}, bf16[2,320,128]{2,1,0:T(8,128)(2,1)S(1)}, u32[]{:S(2)}, u32[]{:S(2)}) collective-permute-start(bf16[2,320,128]{2,1,0:T(8,128)(2,1)S(1)} %pad_maximum_fusion.refs_0_), channel_id=1, source_target_pairs={{0,8},{8,0},{16,24},{24,16},{1,9},{9,1},{17,25},{25,17},{2,10},{10... | collective-permute-start | bytes 491528 | tf_op jit(solution)/shard_map/ppermute | solution.py:621
  56.6 6.1 %collective-permute-start.22 = (bf16[2,320,128]{2,1,0:T(8,128)(2,1)S(1)}, bf16[2,320,128]{2,1,0:T(8,128)(2,1)S(1)}, u32[]{:S(2)}, u32[]{:S(2)}) collective-permute-start(bf16[2,320,128]{2,1,0:T(8,128)(2,1)S(1)} %pad_maximum_fusion.refs_0_), channel_id=1, source_target_pairs={{0,16},{8,24},{16,0},{24,8},{1,17},{9,25},{17,1},{25,9},{2,18},{10... | collective-permute-start | bytes 491528 | tf_op jit(solution)/shard_map/ppermute | solution.py:621
  57.7 8.0 %collective-permute-start.24 = (bf16[2,320,128]{2,1,0:T(8,128)(2,1)S(1)}, bf16[2,320,128]{2,1,0:T(8,128)(2,1)S(1)}, u32[]{:S(2)}, u32[]{:S(2)}) collective-permute-start(bf16[2,320,128]{2,1,0:T(8,128)(2,1)S(1)} %pad_maximum_fusion.refs_0_), channel_id=1, source_target_pairs={{0,24},{8,16},{16,8},{24,0},{1,25},{9,17},{17,9},{25,1},{2,26},{10... | collective-permute-start | bytes 491528 | tf_op jit(solution)/shard_map/ppermute | solution.py:621
  60.6 7.1 %collective-permute-start.27 = (bf16[2,320,128]{2,1,0:T(8,128)(2,1)S(1)}, bf16[2,320,128]{2,1,0:T(8,128)(2,1)S(1)}, u32[]{:S(2)}, u32[]{:S(2)}) collective-permute-start(bf16[2,320,128]{2,1,0:T(8,128)(2,1)S(1)} %constant_dynamic-update-slice_fusion.refs_0_), channel_id=1, source_target_pairs={{0,8},{8,0},{16,24},{24,16},{1,9},{9,1},{17,25},{25,17},{2,10},{10... | collective-permute-start | bytes 491528 | tf_op jit(solution)/shard_map/ppermute | solution.py:621
  61.6 8.5 %collective-permute-start.29 = (bf16[2,320,128]{2,1,0:T(8,128)(2,1)S(1)}, bf16[2,320,128]{2,1,0:T(8,128)(2,1)S(1)}, u32[]{:S(2)}, u32[]{:S(2)}) collective-permute-start(bf16[2,320,128]{2,1,0:T(8,128)(2,1)S(1)} %constant_dynamic-update-slice_fusion.refs_0_), channel_id=1, source_target_pairs={{0,16},{8,24},{16,0},{24,8},{1,17},{9,25},{17,1},{25,9},{2,18},{10... | collective-permute-start | bytes 491528 | tf_op jit(solution)/shard_map/ppermute | solution.py:621
  62.7 9.0 %collective-permute-start.16 = (bf16[2,320,128]{2,1,0:T(8,128)(2,1)S(1)}, bf16[2,320,128]{2,1,0:T(8,128)(2,1)S(1)}, u32[]{:S(2)}, u32[]{:S(2)}) collective-permute-start(bf16[2,320,128]{2,1,0:T(8,128)(2,1)S(1)} %constant_dynamic-update-slice_fusion.refs_0_), channel_id=1, source_target_pairs={{0,24},{8,16},{16,8},{24,0},{1,25},{9,17},{17,9},{25,1},{2,26},{10... | collective-permute-start | bytes 491528 | tf_op jit(solution)/shard_map/ppermute | solution.py:621
  65.8 5.9 %collective-permute-start.21 = (bf16[2,320,128]{2,1,0:T(8,128)(2,1)S(1)}, bf16[2,320,128]{2,1,0:T(8,128)(2,1)S(1)}, u32[]{:S(2)}, u32[]{:S(2)}) collective-permute-start(bf16[2,320,128]{2,1,0:T(8,128)(2,1)S(1)} %collective-permute-done.20.refs_2_), channel_id=1, source_target_pairs={{0,1},{1,0},{2,3},{3,2},{4,5},{5,4},{6,7},{7,6},{8,9},{9,8},{10,11... | collective-permute-start | bytes 491528 | tf_op jit(solution)/shard_map/ppermute | solution.py:614
  65.8 6.4 %collective-permute-start.23 = (bf16[2,320,128]{2,1,0:T(8,128)(2,1)S(1)}, bf16[2,320,128]{2,1,0:T(8,128)(2,1)S(1)}, u32[]{:S(2)}, u32[]{:S(2)}) collective-permute-start(bf16[2,320,128]{2,1,0:T(8,128)(2,1)S(1)} %collective-permute-done.22.refs_4_), channel_id=1, source_target_pairs={{0,1},{1,0},{2,3},{3,2},{4,5},{5,4},{6,7},{7,6},{8,9},{9,8},{10,11... | collective-permute-start | bytes 491528 | tf_op jit(solution)/shard_map/ppermute | solution.py:614
  67.7 9.1 %collective-permute-start.26 = (bf16[2,320,128]{2,1,0:T(8,128)(2,1)S(1)}, bf16[2,320,128]{2,1,0:T(8,128)(2,1)S(1)}, u32[]{:S(2)}, u32[]{:S(2)}) collective-permute-start(bf16[2,320,128]{2,1,0:T(8,128)(2,1)S(1)} %constant_dynamic-update-slice_fusion.refs_0_), channel_id=1, source_target_pairs={{0,1},{1,0},{2,3},{3,2},{4,5},{5,4},{6,7},{7,6},{8,9},{9,8},{10,11... | collective-permute-start | bytes 491528 | tf_op jit(solution)/shard_map/ppermute | solution.py:614
  72.2 6.0 %collective-permute-start.17 = (bf16[2,320,128]{2,1,0:T(8,128)(2,1)S(1)}, bf16[2,320,128]{2,1,0:T(8,128)(2,1)S(1)}, u32[]{:S(2)}, u32[]{:S(2)}) collective-permute-start(bf16[2,320,128]{2,1,0:T(8,128)(2,1)S(1)} %collective-permute-done.16.refs_0_), channel_id=1, source_target_pairs={{0,1},{1,0},{2,3},{3,2},{4,5},{5,4},{6,7},{7,6},{8,9},{9,8},{10,11... | collective-permute-start | bytes 491528 | tf_op jit(solution)/shard_map/ppermute | solution.py:614
  (14 other events, 96.5 us)

commit v5 on v3

--- a/solution.py
+++ b/solution.py
@@ -744,29 +744,38 @@
     for second in range(2):
         group = range(second * pairs // 2, (second + 1) * pairs // 2)
         column = jnp.concatenate([gathered[s] for s in group])
+        middle = len(group) // 2
         held = []
         for d in range(members):
-            value = column
-            if d:
-                value = swap_member(column, d)
-            held.append((d, (value, swap_lon(value, 1))))
+            parts = [(column, tuple(group))]
+            if members == 4 and d == 3 and second == 0 and middle:
+                parts = []
+                for way, span in ((1, slice(0, middle)), (2, slice(middle, len(group)))):
+                    value = swap_member(held[way][1][0][0][0][span], 3 - way)
+                    parts.append((value, tuple(group)[span]))
+            elif d:
+                parts = [(swap_member(column, d), tuple(group))]
+            held.append(
+                (d, [((value, swap_lon(value, 1)), shifts) for value, shifts in parts])
+            )
         halves.append((group, held))
     rest_lanes = rest * LANES + extras
     short = half_rows // pack
 
     def assemble(second, final, held, extra_inputs, other_shape):
-        group = halves[second][0]
-        arrays, layout = [], []
-        for d, both in held:
-            for other, value in enumerate(both):
-                arrays.append(value)
-                layout += [(d, s, bool(other)) for s in group]
-        count, each = len(arrays), len(group)
+        arrays, layout, spots = [], [], []
+        for d, parts in held:
+            for both, shifts in parts:
+                for other, value in enumerate(both):
+                    spots += [(len(arrays), at) for at in range(len(shifts))]
+                    arrays.append(value)
+                    layout += [(d, s, bool(other)) for s in shifts]
+        count = len(arrays)
         stages = max(len(held) * main, 1)
         taps_held = per_half + second
 
         def kernel(*refs):
-            pieces = [ref.at[pl.ds(at, 1)] for ref in refs[:count] for at in range(each)]
+            pieces = [refs[which].at[pl.ds(at, 1)] for which, at in spots]
             assemble_kernel(plan, second, tuple(layout), final, *pieces, *refs[count:])
 
         specs = [vmem()] * count

time: 80.6 us -> 83.1 us (1.031)
  waiting for transfers between devices: 23.1 us -> 25.9 us
    ppermute x12 -> x13, starting transfers between devices: 16.1 us -> 14.6 us  [swap_member(): return lax.ppermute(value, 'member', [(i, i ^ d) for i in range(members)])]
    ppermute x17 -> x18, waiting for transfers between devices: 10.6 us -> 12 us  [swap_lon(): return lax.ppermute(value, 'lon', [(i, i ^ d) for i in range(lon_count)])]
    ppermute x12 -> x13, waiting for transfers between devices: 12.5 us -> 13.9 us  [swap_member(): return lax.ppermute(value, 'member', [(i, i ^ d) for i in range(members)])]
    ppermute x17 -> x18, starting transfers between devices: 10.7 us -> 11.6 us  [swap_lon(): return lax.ppermute(value, 'lon', [(i, i ^ d) for i in range(lon_count)])]
  transfers between devices with their start and end apart: 31 -> 33, of which waited for: 12 -> 13; matrix products, arithmetic and copies ran while one was open for 0% -> 0% of each run, Pallas kernels for 13% -> 13%
where the time goes in v5:
time: 83.1 us; the launch traced here: 82.7 us
  starting transfers between devices  31.5 us (38%)
  waiting for transfers between devices  25.9 us (31%)
  Pallas kernels  20.4 us (25%)
  local copies, waits for them, and re-layouts  3.94 us (5%)
  between operations  0.97 us (1%)
    ppermute x13, starting transfers between devices, swap_member(): return lax.ppermute(value, 'member', [(i, i ^ d) for i in range(members)])  14.6 us
    ppermute x13, waiting for transfers between devices, swap_member(): return lax.ppermute(value, 'member', [(i, i ^ d) for i in range(members)])  13.9 us
    ppermute x18, waiting for transfers between devices, swap_lon(): return lax.ppermute(value, 'lon', [(i, i ^ d) for i in range(lon_count)])  12 us
    ppermute x18, starting transfers between devices, swap_lon(): return lax.ppermute(value, 'lon', [(i, i ^ d) for i in range(lon_count)])  11.6 us
    pallas_call x1, Pallas kernels, body(): pl.pallas_call(functools.partial(gradient_kernel, plan), out_shape=(jax.S...  6.29 us
    pallas_call x3, Pallas kernels, assemble(): pl.pallas_call(kernel, out_shape=[grad_shape, jax.ShapeDtypeStruct(other_...  5.66 us
    ppermute x2, starting transfers between devices, swap_far(): return lax.ppermute(value, 'lon', step)  5.24 us
    unnamed x15, local copies, waits for them, and re-layouts  3.91 us
  transfers between devices with their start and end apart: 33, of which 13 were waited for; matrix products, arithmetic and copies ran while one was open for 0% of the time, Pallas kernels for 13%

profile of v5, /device:TPU:0, one launch (start us, length us, event | category | flops | bytes accessed | tf_op | source)
XLA Modules:
  0.0 82.7 jit_solution(689109341296422330)
XLA Ops:
  3.3 4.7 %collective-permute-start.3 = (bf16[20,4,641]{2,1,0:T(4,128)(2,1)S(1)}, bf16[20,4,641]{2,1,0:T(4,128)(2,1)S(1)}, u32[]{:S(2)}, u32[]{:S(2)}) collective-permute-start(bf16[20,4,641]{2,1,0:T(4,128)(2,1)S(1)} %get-tuple-element.32), channel_id=1, source_target_pairs={{0,7},{1,2},{2,1},{3,4},{4,3},{5,6},{6,5},{7,0},{8,15},{9,10},{10,... | collective-permute-start | bytes 307688 | tf_op jit(solution)/shard_map/ppermute | solution.py:607
  8.0 1.5 %collective-permute-start.4 = (bf16[26,45,128]{2,1,0:T(8,128)(2,1)S(1)}, bf16[26,45,128]{2,1,0:T(8,128)(2,1)S(1)}, u32[]{:S(2)}, u32[]{:S(2)}) collective-permute-start(bf16[26,45,128]{2,1,0:T(8,128)(2,1)S(1)} %get-tuple-element.34), channel_id=1, source_target_pairs={{0,8},{8,0},{16,24},{24,16},{1,9},{9,1},{17,25},{25,17},{2,10},{10... | collective-permute-start | bytes 898568 | tf_op jit(solution)/shard_map/ppermute | solution.py:610
  9.5 1.5 %collective-permute-start.5 = (bf16[26,45,128]{2,1,0:T(8,128)(2,1)S(1)}, bf16[26,45,128]{2,1,0:T(8,128)(2,1)S(1)}, u32[]{:S(2)}, u32[]{:S(2)}) collective-permute-start(bf16[26,45,128]{2,1,0:T(8,128)(2,1)S(1)} %get-tuple-element.35), channel_id=1, source_target_pairs={{0,16},{8,24},{16,0},{24,8},{1,17},{9,25},{17,1},{25,9},{2,18},{10... | collective-permute-start | bytes 898568 | tf_op jit(solution)/shard_map/ppermute | solution.py:610
  11.5 1.9 %copy-done = bf16[5,5,73,641]{3,2,1,0:T(8,128)(2,1)S(1)} copy-done((bf16[5,5,73,641]{3,2,1,0:T(8,128)(2,1)S(1)}, bf16[5,5,73,641]{3,2,1,0:T(8,128)(2,1)}, u32[]{:S(2)}) %copy-start) | copy-done | bytes 2339674
  15.0 3.6 %forward.1.own_ref = bf16[80,1024]{1,0:T(8,128)(2,1)S(1)} custom-call(bf16[20,45,641]{2,1,0:T(8,128)(2,1)S(1)} %bitcast.17, bf16[20,4,641]{2,1,0:T(4,128)(2,1)S(1)} %collective-permute-done.2.near_ref, bf16[20,4,641]{2,1,0:T(4,128)(2,1)S(1)} %collective-permute-done.3.far_ref, bf16[25,80,768]{2,1,0:T(8,128)(2,1)S(1)} %stage.1.w_s, f32[1,73]{1,0:T(1,128)S(1)} %bitcast.18), custom_call_target="tpu_custom_call" | custom-call | flops 3145728000 | bytes 6000000 | tf_op jit(solution)/shard_map/forward/pallas_call | solution.py:655
  18.6 1.6 %collective-permute-start.7 = (bf16[80,1024]{1,0:T(8,128)(2,1)S(1)}, bf16[80,1024]{1,0:T(8,128)(2,1)S(1)}, u32[]{:S(2)}, u32[]{:S(2)}) collective-permute-start(bf16[80,1024]{1,0:T(8,128)(2,1)S(1)} %forward.1.own_ref), channel_id=1, source_target_pairs={{0,8},{8,0},{16,24},{24,16},{1,9},{9,1},{17,25},{25,17},{2,10},{10... | collective-permute-start | bytes 491528 | tf_op jit(solution)/shard_map/ppermute | solution.py:610
  20.2 1.5 %collective-permute-start.8 = (bf16[80,1024]{1,0:T(8,128)(2,1)S(1)}, bf16[80,1024]{1,0:T(8,128)(2,1)S(1)}, u32[]{:S(2)}, u32[]{:S(2)}) collective-permute-start(bf16[80,1024]{1,0:T(8,128)(2,1)S(1)} %forward.1.own_ref), channel_id=1, source_target_pairs={{0,16},{8,24},{16,0},{24,8},{1,17},{9,25},{17,1},{25,9},{2,18},{10... | collective-permute-start | bytes 491528 | tf_op jit(solution)/shard_map/ppermute | solution.py:610
  23.1 1.4 %collective-permute-done.6.refs_3_ = bf16[26,45,128]{2,1,0:T(8,128)(2,1)S(1)} collective-permute-done((bf16[26,45,128]{2,1,0:T(8,128)(2,1)S(1)}, bf16[26,45,128]{2,1,0:T(8,128)(2,1)S(1)}, u32[]{:S(2)}, u32[]{:S(2)}) %collective-permute-start.6) | collective-permute-done | bytes 299552 | tf_op jit(solution)/shard_map/ppermute | solution.py:610
  25.5 1.5 %collective-permute-done.7.refs_1_ = bf16[80,1024]{1,0:T(8,128)(2,1)S(1)} collective-permute-done((bf16[80,1024]{1,0:T(8,128)(2,1)S(1)}, bf16[80,1024]{1,0:T(8,128)(2,1)S(1)}, u32[]{:S(2)}, u32[]{:S(2)}) %collective-permute-start.7) | collective-permute-done | bytes 163872 | tf_op jit(solution)/shard_map/ppermute | solution.py:610
  27.1 3.5 %collective-permute-done.8.refs_2_ = bf16[80,1024]{1,0:T(8,128)(2,1)S(1)} collective-permute-done((bf16[80,1024]{1,0:T(8,128)(2,1)S(1)}, bf16[80,1024]{1,0:T(8,128)(2,1)S(1)}, u32[]{:S(2)}, u32[]{:S(2)}) %collective-permute-start.8) | collective-permute-done | bytes 163872 | tf_op jit(solution)/shard_map/ppermute | solution.py:610
  30.6 6.3 %gradient.1 = (bf16[80,1024]{1,0:T(8,128)(2,1)S(1)}, f32[1,1024]{1,0:T(1,128)S(1)}, bf16[4,320,128]{2,1,0:T(8,128)(2,1)S(1)}, f32[4,320,128]{2,1,0:T(8,128)S(1)}) custom-call(bf16[80,1024]{1,0:T(8,128)(2,1)S(1)} %get-tuple-element.37.refs_0_, bf16[80,1024]{1,0:T(8,128)(2,1)S(1)} %collective-permute-done.7.refs_1_, ...), custom_call_target="tpu_custom_call" | custom-call | flops 4194304000 | bytes 6000000 | tf_op jit(solution)/shard_map/gradient/pallas_call | solution.py:692
  37.0 1.6 %collective-permute-done.10.got_ref = bf16[4,320,128]{2,1,0:T(8,128)(2,1)S(1)} collective-permute-done((bf16[4,320,128]{2,1,0:T(8,128)(2,1)S(1)}, bf16[4,320,128]{2,1,0:T(8,128)(2,1)S(1)}, u32[]{:S(2)}, u32[]{:S(2)}) %collective-permute-start.10) | collective-permute-done | bytes 327712 | tf_op jit(solution)/shard_map/ppermute | solution.py:603
  38.7 1.6 %collective-permute-start.11 = (bf16[1,320,128]{2,1,0:T(8,128)(2,1)S(1)}, bf16[1,320,128]{2,1,0:T(8,128)(2,1)S(1)}, u32[]{:S(2)}, u32[]{:S(2)}) collective-permute-start(bf16[1,320,128]{2,1,0:T(8,128)(2,1)S(1)} %get-tuple-element.45), channel_id=1, source_target_pairs={{0,2},{1,3},{2,0},{3,1},{4,6},{5,7},{6,4},{7,5},{8,10},{9,11},{10,... | collective-permute-start | bytes 245768 | tf_op jit(solution)/shard_map/ppermute | solution.py:603
  41.6 1.5 %collective-permute-start.13 = (bf16[1,320,128]{2,1,0:T(8,128)(2,1)S(1)}, bf16[1,320,128]{2,1,0:T(8,128)(2,1)S(1)}, u32[]{:S(2)}, u32[]{:S(2)}) collective-permute-start(bf16[1,320,128]{2,1,0:T(8,128)(2,1)S(1)} %get-tuple-element.47), channel_id=1, source_target_pairs={{0,6},{1,7},{2,4},{3,5},{4,2},{5,3},{6,0},{7,1},{8,14},{9,15},{10,... | collective-permute-start | bytes 245768 | tf_op jit(solution)/shard_map/ppermute | solution.py:603
  43.2 6.5 %collective-permute-done.12.refs_1_ = bf16[1,320,128]{2,1,0:T(8,128)(2,1)S(1)} collective-permute-done((bf16[1,320,128]{2,1,0:T(8,128)(2,1)S(1)}, bf16[1,320,128]{2,1,0:T(8,128)(2,1)S(1)}, u32[]{:S(2)}, u32[]{:S(2)}) %collective-permute-start.12) | collective-permute-done | bytes 81952 | tf_op jit(solution)/shard_map/ppermute | solution.py:603
  50.0 1.6 %collective-permute-start.18 = (bf16[1,320,128]{2,1,0:T(8,128)(2,1)S(1)}, bf16[1,320,128]{2,1,0:T(8,128)(2,1)S(1)}, u32[]{:S(2)}, u32[]{:S(2)}) collective-permute-start(bf16[1,320,128]{2,1,0:T(8,128)(2,1)S(1)} %pair_add.1), channel_id=1, source_target_pairs={{0,2},{1,3},{2,0},{3,1},{4,6},{5,7},{6,4},{7,5},{8,10},{9,11},{10,... | collective-permute-start | bytes 245768 | tf_op jit(solution)/shard_map/ppermute | solution.py:603
  52.7 1.7 %collective-permute-start.15 = (bf16[1,320,128]{2,1,0:T(8,128)(2,1)S(1)}, bf16[1,320,128]{2,1,0:T(8,128)(2,1)S(1)}, u32[]{:S(2)}, u32[]{:S(2)}) collective-permute-start(bf16[1,320,128]{2,1,0:T(8,128)(2,1)S(1)} %pair_add.1), channel_id=1, source_target_pairs={{0,6},{1,7},{2,4},{3,5},{4,2},{5,3},{6,0},{7,1},{8,14},{9,15},{10,... | collective-permute-start | bytes 245768 | tf_op jit(solution)/shard_map/ppermute | solution.py:603
  57.6 2.8 %collective-permute-done.14 = bf16[1,320,128]{2,1,0:T(8,128)(2,1)S(1)} collective-permute-done((bf16[1,320,128]{2,1,0:T(8,128)(2,1)S(1)}, bf16[1,320,128]{2,1,0:T(8,128)(2,1)S(1)}, u32[]{:S(2)}, u32[]{:S(2)}) %collective-permute-start.14) | collective-permute-done | bytes 81952 | tf_op jit(solution)/shard_map/ppermute | solution.py:603
  62.5 1.4 %collective-permute-start.16 = (bf16[2,320,128]{2,1,0:T(8,128)(2,1)S(1)}, bf16[2,320,128]{2,1,0:T(8,128)(2,1)S(1)}, u32[]{:S(2)}, u32[]{:S(2)}) collective-permute-start(bf16[2,320,128]{2,1,0:T(8,128)(2,1)S(1)} %constant_dynamic-update-slice_fusion.refs_0_), channel_id=1, source_target_pairs={{0,24},{8,16},{16,8},{24,0},{1,25},{9,17},{17,9},{25,1},{2,26},{10... | collective-permute-start | bytes 491528 | tf_op jit(solution)/shard_map/ppermute | solution.py:610
  64.4 2.2 %collective-permute-done.29.refs_2_ = bf16[2,320,128]{2,1,0:T(8,128)(2,1)S(1)} collective-permute-done((bf16[2,320,128]{2,1,0:T(8,128)(2,1)S(1)}, bf16[2,320,128]{2,1,0:T(8,128)(2,1)S(1)}, u32[]{:S(2)}, u32[]{:S(2)}) %collective-permute-start.29) | collective-permute-done | bytes 163872 | tf_op jit(solution)/shard_map/ppermute | solution.py:610
  69.5 1.7 %collective-permute-done.24.refs_6_ = bf16[1,320,128]{2,1,0:T(8,128)(2,1)S(1)} collective-permute-done((bf16[1,320,128]{2,1,0:T(8,128)(2,1)S(1)}, bf16[1,320,128]{2,1,0:T(8,128)(2,1)S(1)}, u32[]{:S(2)}, u32[]{:S(2)}) %collective-permute-start.24) | collective-permute-done | bytes 81952 | tf_op jit(solution)/shard_map/ppermute | solution.py:610
  71.6 1.6 %collective-permute-done.26.refs_8_ = bf16[1,320,128]{2,1,0:T(8,128)(2,1)S(1)} collective-permute-done((bf16[1,320,128]{2,1,0:T(8,128)(2,1)S(1)}, bf16[1,320,128]{2,1,0:T(8,128)(2,1)S(1)}, u32[]{:S(2)}, u32[]{:S(2)}) %collective-permute-start.26) | collective-permute-done | bytes 81952 | tf_op jit(solution)/shard_map/ppermute | solution.py:610
  76.8 2.0 %assemble.3 = (f32[25,73,641]{2,1,0:T(8,128)}, f32[5,64,128]{2,1,0:T(8,128)S(1)}) custom-call(bf16[2,320,128]{2,1,0:T(8,128)(2,1)S(1)} %pad_maximum_fusion.refs_0_, bf16[2,320,128]{2,1,0:T(8,128)(2,1)S(1)} %collective-permute-done.19.refs_1_, bf16[2,320,128]{2,1,0:T(8,128)(2,1)S(1)} %collective-permute-done.20.refs_2_, ...), custom_call_target="tpu_custom_call" | custom-call | bytes 5000000 | tf_op jit(solution)/shard_map/assemble/pallas_call | solution.py:784
  80.2 2.3 %assemble.5 = (f32[25,73,641]{2,1,0:T(8,128)}, f32[1,73]{1,0:T(1,128)}) custom-call(bf16[2,320,128]{2,1,0:T(8,128)(2,1)S(1)} %collective-permute-done.16.refs_0_, bf16[2,320,128]{2,1,0:T(8,128)(2,1)S(1)} %collective-permute-done.17.refs_1_, f32[5,64,128]{2,1,0:T(8,128)S(1)} %get-tuple-element.48.refs_6_.refs_2_, ...), custom_call_target="tpu_custom_call", output_to_operand_aliasing={{0}: (3, {})} | custom-call | bytes 5000000 | tf_op jit(solution)/shard_map/assemble/pallas_call | solution.py:784
  (74 shorter events, 23.9 us)
Async XLA Ops:
  2.8 11.6 %collective-permute-start.2 = (bf16[20,4,641]{2,1,0:T(4,128)(2,1)S(1)}, bf16[20,4,641]{2,1,0:T(4,128)(2,1)S(1)}, u32[]{:S(2)}, u32[]{:S(2)}) collective-permute-start(bf16[20,4,641]{2,1,0:T(4,128)(2,1)S(1)} %get-tuple-element.31), channel_id=1, source_target_pairs={{0,1},{1,0},{2,3},{3,2},{4,5},{5,4},{6,7},{7,6},{8,9},{9,8},{10,11... | collective-permute-start | bytes 307688 | tf_op jit(solution)/shard_map/ppermute | solution.py:603
  3.3 11.1 %collective-permute-start.3 = (bf16[20,4,641]{2,1,0:T(4,128)(2,1)S(1)}, bf16[20,4,641]{2,1,0:T(4,128)(2,1)S(1)}, u32[]{:S(2)}, u32[]{:S(2)}) collective-permute-start(bf16[20,4,641]{2,1,0:T(4,128)(2,1)S(1)} %get-tuple-element.32), channel_id=1, source_target_pairs={{0,7},{1,2},{2,1},{3,4},{4,3},{5,6},{6,5},{7,0},{8,15},{9,10},{10,... | collective-permute-start | bytes 307688 | tf_op jit(solution)/shard_map/ppermute | solution.py:607
  8.0 13.7 %collective-permute-start.4 = (bf16[26,45,128]{2,1,0:T(8,128)(2,1)S(1)}, bf16[26,45,128]{2,1,0:T(8,128)(2,1)S(1)}, u32[]{:S(2)}, u32[]{:S(2)}) collective-permute-start(bf16[26,45,128]{2,1,0:T(8,128)(2,1)S(1)} %get-tuple-element.34), channel_id=1, source_target_pairs={{0,8},{8,0},{16,24},{24,16},{1,9},{9,1},{17,25},{25,17},{2,10},{10... | collective-permute-start | bytes 898568 | tf_op jit(solution)/shard_map/ppermute | solution.py:610
  9.5 13.5 %collective-permute-start.5 = (bf16[26,45,128]{2,1,0:T(8,128)(2,1)S(1)}, bf16[26,45,128]{2,1,0:T(8,128)(2,1)S(1)}, u32[]{:S(2)}, u32[]{:S(2)}) collective-permute-start(bf16[26,45,128]{2,1,0:T(8,128)(2,1)S(1)} %get-tuple-element.35), channel_id=1, source_target_pairs={{0,16},{8,24},{16,0},{24,8},{1,17},{9,25},{17,1},{25,9},{2,18},{10... | collective-permute-start | bytes 898568 | tf_op jit(solution)/shard_map/ppermute | solution.py:610
  11.0 13.5 %collective-permute-start.6 = (bf16[26,45,128]{2,1,0:T(8,128)(2,1)S(1)}, bf16[26,45,128]{2,1,0:T(8,128)(2,1)S(1)}, u32[]{:S(2)}, u32[]{:S(2)}) collective-permute-start(bf16[26,45,128]{2,1,0:T(8,128)(2,1)S(1)} %get-tuple-element.36), channel_id=1, source_target_pairs={{0,24},{8,16},{16,8},{24,0},{1,25},{9,17},{17,9},{25,1},{2,26},{10... | collective-permute-start | bytes 898568 | tf_op jit(solution)/shard_map/ppermute | solution.py:610
  14.5 5.7 %collective-permute-start.1 = (f32[2,16,73]{2,1,0:T(8,128)S(1)}, f32[2,16,73]{2,1,0:T(8,128)S(1)}, u32[]{:S(2)}, u32[]{:S(2)}) collective-permute-start(f32[2,16,73]{2,1,0:T(8,128)S(1)} %get-tuple-element.30), channel_id=1, source_target_pairs={{0,7},{1,2},{2,1},{3,4},{4,3},{5,6},{6,5},{7,0},{8,15},{9,10},{10,... | collective-permute-start | bytes 28040 | tf_op jit(solution)/shard_map/ppermute | solution.py:607
  18.6 8.4 %collective-permute-start.7 = (bf16[80,1024]{1,0:T(8,128)(2,1)S(1)}, bf16[80,1024]{1,0:T(8,128)(2,1)S(1)}, u32[]{:S(2)}, u32[]{:S(2)}) collective-permute-start(bf16[80,1024]{1,0:T(8,128)(2,1)S(1)} %forward.1.own_ref), channel_id=1, source_target_pairs={{0,8},{8,0},{16,24},{24,16},{1,9},{9,1},{17,25},{25,17},{2,10},{10... | collective-permute-start | bytes 491528 | tf_op jit(solution)/shard_map/ppermute | solution.py:610
  20.2 10.4 %collective-permute-start.8 = (bf16[80,1024]{1,0:T(8,128)(2,1)S(1)}, bf16[80,1024]{1,0:T(8,128)(2,1)S(1)}, u32[]{:S(2)}, u32[]{:S(2)}) collective-permute-start(bf16[80,1024]{1,0:T(8,128)(2,1)S(1)} %forward.1.own_ref), channel_id=1, source_target_pairs={{0,16},{8,24},{16,0},{24,8},{1,17},{9,25},{17,1},{25,9},{2,18},{10... | collective-permute-start | bytes 491528 | tf_op jit(solution)/shard_map/ppermute | solution.py:610
  21.7 8.9 %collective-permute-start.9 = (bf16[80,1024]{1,0:T(8,128)(2,1)S(1)}, bf16[80,1024]{1,0:T(8,128)(2,1)S(1)}, u32[]{:S(2)}, u32[]{:S(2)}) collective-permute-start(bf16[80,1024]{1,0:T(8,128)(2,1)S(1)} %forward.1.own_ref), channel_id=1, source_target_pairs={{0,24},{8,16},{16,8},{24,0},{1,25},{9,17},{17,9},{25,1},{2,26},{10... | collective-permute-start | bytes 491528 | tf_op jit(solution)/shard_map/ppermute | solution.py:610
  40.3 9.5 %collective-permute-start.12 = (bf16[1,320,128]{2,1,0:T(8,128)(2,1)S(1)}, bf16[1,320,128]{2,1,0:T(8,128)(2,1)S(1)}, u32[]{:S(2)}, u32[]{:S(2)}) collective-permute-start(bf16[1,320,128]{2,1,0:T(8,128)(2,1)S(1)} %get-tuple-element.46), channel_id=1, source_target_pairs={{0,4},{1,5},{2,6},{3,7},{4,0},{5,1},{6,2},{7,3},{8,12},{9,13},{10,... | collective-permute-start | bytes 245768 | tf_op jit(solution)/shard_map/ppermute | solution.py:603
  41.6 8.2 %collective-permute-start.13 = (bf16[1,320,128]{2,1,0:T(8,128)(2,1)S(1)}, bf16[1,320,128]{2,1,0:T(8,128)(2,1)S(1)}, u32[]{:S(2)}, u32[]{:S(2)}) collective-permute-start(bf16[1,320,128]{2,1,0:T(8,128)(2,1)S(1)} %get-tuple-element.47), channel_id=1, source_target_pairs={{0,6},{1,7},{2,4},{3,5},{4,2},{5,3},{6,0},{7,1},{8,14},{9,15},{10,... | collective-permute-start | bytes 245768 | tf_op jit(solution)/shard_map/ppermute | solution.py:603
  51.6 8.7 %collective-permute-start.14 = (bf16[1,320,128]{2,1,0:T(8,128)(2,1)S(1)}, bf16[1,320,128]{2,1,0:T(8,128)(2,1)S(1)}, u32[]{:S(2)}, u32[]{:S(2)}) collective-permute-start(bf16[1,320,128]{2,1,0:T(8,128)(2,1)S(1)} %pair_add.1), channel_id=1, source_target_pairs={{0,4},{1,5},{2,6},{3,7},{4,0},{5,1},{6,2},{7,3},{8,12},{9,13},{10,... | collective-permute-start | bytes 245768 | tf_op jit(solution)/shard_map/ppermute | solution.py:603
  52.7 7.6 %collective-permute-start.15 = (bf16[1,320,128]{2,1,0:T(8,128)(2,1)S(1)}, bf16[1,320,128]{2,1,0:T(8,128)(2,1)S(1)}, u32[]{:S(2)}, u32[]{:S(2)}) collective-permute-start(bf16[1,320,128]{2,1,0:T(8,128)(2,1)S(1)} %pair_add.1), channel_id=1, source_target_pairs={{0,6},{1,7},{2,4},{3,5},{4,2},{5,3},{6,0},{7,1},{8,14},{9,15},{10,... | collective-permute-start | bytes 245768 | tf_op jit(solution)/shard_map/ppermute | solution.py:603
  55.4 7.0 %collective-permute-start.20 = (bf16[2,320,128]{2,1,0:T(8,128)(2,1)S(1)}, bf16[2,320,128]{2,1,0:T(8,128)(2,1)S(1)}, u32[]{:S(2)}, u32[]{:S(2)}) collective-permute-start(bf16[2,320,128]{2,1,0:T(8,128)(2,1)S(1)} %pad_maximum_fusion.refs_0_), channel_id=1, source_target_pairs={{0,8},{8,0},{16,24},{24,16},{1,9},{9,1},{17,25},{25,17},{2,10},{10... | collective-permute-start | bytes 491528 | tf_op jit(solution)/shard_map/ppermute | solution.py:610
  56.4 7.5 %collective-permute-start.22 = (bf16[2,320,128]{2,1,0:T(8,128)(2,1)S(1)}, bf16[2,320,128]{2,1,0:T(8,128)(2,1)S(1)}, u32[]{:S(2)}, u32[]{:S(2)}) collective-permute-start(bf16[2,320,128]{2,1,0:T(8,128)(2,1)S(1)} %pad_maximum_fusion.refs_0_), channel_id=1, source_target_pairs={{0,16},{8,24},{16,0},{24,8},{1,17},{9,25},{17,1},{25,9},{2,18},{10... | collective-permute-start | bytes 491528 | tf_op jit(solution)/shard_map/ppermute | solution.py:610
  57.6 6.4 %collective-permute-start.19 = (bf16[2,320,128]{2,1,0:T(8,128)(2,1)S(1)}, bf16[2,320,128]{2,1,0:T(8,128)(2,1)S(1)}, u32[]{:S(2)}, u32[]{:S(2)}) collective-permute-start(bf16[2,320,128]{2,1,0:T(8,128)(2,1)S(1)} %pad_maximum_fusion.refs_0_), channel_id=1, source_target_pairs={{0,1},{1,0},{2,3},{3,2},{4,5},{5,4},{6,7},{7,6},{8,9},{9,8},{10,11... | collective-permute-start | bytes 491528 | tf_op jit(solution)/shard_map/ppermute | solution.py:603
  60.4 6.3 %collective-permute-start.29 = (bf16[2,320,128]{2,1,0:T(8,128)(2,1)S(1)}, bf16[2,320,128]{2,1,0:T(8,128)(2,1)S(1)}, u32[]{:S(2)}, u32[]{:S(2)}) collective-permute-start(bf16[2,320,128]{2,1,0:T(8,128)(2,1)S(1)} %constant_dynamic-update-slice_fusion.refs_0_), channel_id=1, source_target_pairs={{0,8},{8,0},{16,24},{24,16},{1,9},{9,1},{17,25},{25,17},{2,10},{10... | collective-permute-start | bytes 491528 | tf_op jit(solution)/shard_map/ppermute | solution.py:610
  61.4 7.5 %collective-permute-start.31 = (bf16[2,320,128]{2,1,0:T(8,128)(2,1)S(1)}, bf16[2,320,128]{2,1,0:T(8,128)(2,1)S(1)}, u32[]{:S(2)}, u32[]{:S(2)}) collective-permute-start(bf16[2,320,128]{2,1,0:T(8,128)(2,1)S(1)} %constant_dynamic-update-slice_fusion.refs_0_), channel_id=1, source_target_pairs={{0,16},{8,24},{16,0},{24,8},{1,17},{9,25},{17,1},{25,9},{2,18},{10... | collective-permute-start | bytes 491528 | tf_op jit(solution)/shard_map/ppermute | solution.py:610
  62.5 8.7 %collective-permute-start.16 = (bf16[2,320,128]{2,1,0:T(8,128)(2,1)S(1)}, bf16[2,320,128]{2,1,0:T(8,128)(2,1)S(1)}, u32[]{:S(2)}, u32[]{:S(2)}) collective-permute-start(bf16[2,320,128]{2,1,0:T(8,128)(2,1)S(1)} %constant_dynamic-update-slice_fusion.refs_0_), channel_id=1, source_target_pairs={{0,24},{8,16},{16,8},{24,0},{1,25},{9,17},{17,9},{25,1},{2,26},{10... | collective-permute-start | bytes 491528 | tf_op jit(solution)/shard_map/ppermute | solution.py:610
  63.9 9.4 %collective-permute-start.21 = (bf16[2,320,128]{2,1,0:T(8,128)(2,1)S(1)}, bf16[2,320,128]{2,1,0:T(8,128)(2,1)S(1)}, u32[]{:S(2)}, u32[]{:S(2)}) collective-permute-start(bf16[2,320,128]{2,1,0:T(8,128)(2,1)S(1)} %collective-permute-done.20.refs_2_), channel_id=1, source_target_pairs={{0,1},{1,0},{2,3},{3,2},{4,5},{5,4},{6,7},{7,6},{8,9},{9,8},{10,11... | collective-permute-start | bytes 491528 | tf_op jit(solution)/shard_map/ppermute | solution.py:603
  63.9 9.9 %collective-permute-start.23 = (bf16[2,320,128]{2,1,0:T(8,128)(2,1)S(1)}, bf16[2,320,128]{2,1,0:T(8,128)(2,1)S(1)}, u32[]{:S(2)}, u32[]{:S(2)}) collective-permute-start(bf16[2,320,128]{2,1,0:T(8,128)(2,1)S(1)} %collective-permute-done.22.refs_4_), channel_id=1, source_target_pairs={{0,1},{1,0},{2,3},{3,2},{4,5},{5,4},{6,7},{7,6},{8,9},{9,8},{10,11... | collective-permute-start | bytes 491528 | tf_op jit(solution)/shard_map/ppermute | solution.py:603
  71.1 7.7 %collective-permute-start.28 = (bf16[2,320,128]{2,1,0:T(8,128)(2,1)S(1)}, bf16[2,320,128]{2,1,0:T(8,128)(2,1)S(1)}, u32[]{:S(2)}, u32[]{:S(2)}) collective-permute-start(bf16[2,320,128]{2,1,0:T(8,128)(2,1)S(1)} %constant_dynamic-update-slice_fusion.refs_0_), channel_id=1, source_target_pairs={{0,1},{1,0},{2,3},{3,2},{4,5},{5,4},{6,7},{7,6},{8,9},{9,8},{10,11... | collective-permute-start | bytes 491528 | tf_op jit(solution)/shard_map/ppermute | solution.py:603
  73.3 5.5 %collective-permute-start.32 = (bf16[2,320,128]{2,1,0:T(8,128)(2,1)S(1)}, bf16[2,320,128]{2,1,0:T(8,128)(2,1)S(1)}, u32[]{:S(2)}, u32[]{:S(2)}) collective-permute-start(bf16[2,320,128]{2,1,0:T(8,128)(2,1)S(1)} %collective-permute-done.31.refs_4_), channel_id=1, source_target_pairs={{0,1},{1,0},{2,3},{3,2},{4,5},{5,4},{6,7},{7,6},{8,9},{9,8},{10,11... | collective-permute-start | bytes 491528 | tf_op jit(solution)/shard_map/ppermute | solution.py:603
  73.8 6.4 %collective-permute-start.17 = (bf16[2,320,128]{2,1,0:T(8,128)(2,1)S(1)}, bf16[2,320,128]{2,1,0:T(8,128)(2,1)S(1)}, u32[]{:S(2)}, u32[]{:S(2)}) collective-permute-start(bf16[2,320,128]{2,1,0:T(8,128)(2,1)S(1)} %collective-permute-done.16.refs_0_), channel_id=1, source_target_pairs={{0,1},{1,0},{2,3},{3,2},{4,5},{5,4},{6,7},{7,6},{8,9},{9,8},{10,11... | collective-permute-start | bytes 491528 | tf_op jit(solution)/shard_map/ppermute | solution.py:603
  (16 other events, 103.9 us)
